TPU v7x, 128 devices: a whole 4x4x4 slice. The times are simulated.
128 devices in a mesh: ray: 16 (over x, z), tile: 8 (over y, core).
Axes of the slice: x: 4, y: 4, z: 4, core: 2. Of those that a mesh axis runs over, the one named last changes fastest.
Arguments:
- data: float32 [64, 262144], P(None, ('ray', 'tile')), may hold values from -6 to 6
- sensitivity: bfloat16 [4096, 256, 512], P(('ray', 'tile')), may hold values from -0.25 to 0.25
- block_tiles: int32 [128, 8, 4], P(('ray', 'tile')), may hold values from 0 to 47
- block_bundles: int32 [128, 8, 4], P(('ray', 'tile')), may hold values from 0 to 7
Outputs:
- solution: float32 [64, 196608], P(None, 'tile')
- residual: float32 [64, 262144], P(None, ('ray', 'tile'))
Inputs may be any that keep to these rules, and one draw needn't show every extreme that they name: `block_tiles`: position of the block's tile among the 48 tiles of the owner given by the second index. `block_bundles`: the block's ray bundle among the device's 8 bundles.
All inputs are finite; a program needn't handle non-finite values.
Results may differ from a plain program's by a relative error of at most 0.004.
The roundings to bfloat16 on the way count: a program that leaves them out, or rounds other values in their place, can miss the bound.
Values may be sent and summed in bfloat16 or wider, within the bound.
A program may use at most 128 MiB of HBM per device.

v0:
```python
import jax
import jax.numpy as jnp
from jax import lax
from jax.sharding import PartitionSpec as P

RB = 256
CB = 512
ITERS = 2
BUND_DEV = 8
TILE_DEV = 48


eps_norm = 1e-06


def per_device(data, sensitivity, block_tiles, block_bundles):
    columns = data.shape[0]
    bundles = block_bundles.reshape(-1)
    requests = lax.all_to_all(block_tiles, "tile", split_axis=1, concat_axis=1, tiled=True).reshape(
        -1
    )
    bundle_onehot = (bundles[:, None] == jnp.arange(BUND_DEV, dtype=jnp.int32)[None, :]).astype(
        jnp.float32
    )
    owner_onehot = (requests[:, None] == jnp.arange(TILE_DEV, dtype=jnp.int32)[None, :]).astype(
        jnp.bfloat16
    )

    def fetch(field_bf):
        owned = field_bf.reshape(columns, TILE_DEV, CB)
        outgoing = jnp.take(owned, requests, axis=1)
        tiles = lax.all_to_all(outgoing, "tile", split_axis=1, concat_axis=1, tiled=True)
        return tiles

    def forward(field_bf):
        tiles = fetch(field_bf)
        partial_value = jnp.einsum(
            "cnk,nrk->ncr", tiles, sensitivity, preferred_element_type=jnp.float32
        )
        summed = jnp.einsum(
            "ncr,nb->cbr", partial_value, bundle_onehot, precision=lax.Precision.HIGHEST
        )
        return summed.reshape(columns, BUND_DEV * RB)

    def adjoint(rays_bf):
        picked = jnp.take(rays_bf.reshape(columns, BUND_DEV, RB), bundles, axis=1)
        terms = jnp.einsum(
            "cnr,nrk->cnk", picked, sensitivity, preferred_element_type=jnp.float32
        ).astype(jnp.bfloat16)
        arrived = lax.all_to_all(terms, "tile", split_axis=1, concat_axis=1, tiled=True)
        owned = jnp.einsum(
            "cnk,nt->ctk", arrived, owner_onehot, preferred_element_type=jnp.float32
        ).reshape(columns, TILE_DEV * CB)
        total = lax.psum(owned, "ray")
        return total

    def cell_norm(field):
        local = jnp.sum(field * field, axis=1)
        total = lax.psum(local, "tile")
        return jnp.sqrt(total + eps_norm)

    def ray_norm(rays):
        total = lax.psum(jnp.sum(rays * rays, axis=1), ("ray", "tile"))
        return jnp.sqrt(total + eps_norm)

    beta_now = ray_norm(data)
    rays_dir = data / beta_now[:, None]
    model_dir = adjoint(rays_dir.astype(jnp.bfloat16))
    alpha_now = cell_norm(model_dir)
    model_dir = model_dir / alpha_now[:, None]
    search = model_dir
    solution = jnp.zeros_like(model_dir)
    phi_bar = beta_now
    rho_bar = alpha_now
    for step in range(ITERS):
        rounded = model_dir.astype(jnp.bfloat16)
        rays_dir = forward(rounded) - alpha_now[:, None] * rays_dir
        beta_now = ray_norm(rays_dir)
        rays_dir = rays_dir / beta_now[:, None]
        rho_now = jnp.sqrt(rho_bar * rho_bar + beta_now * beta_now)
        cosine = rho_bar / rho_now
        sine_part = beta_now / rho_now
        phi_now = cosine * phi_bar
        phi_bar = sine_part * phi_bar
        solution = solution + (phi_now / rho_now)[:, None] * search
        if step + 1 < ITERS:
            model_dir = adjoint(rays_dir.astype(jnp.bfloat16)) - beta_now[:, None] * model_dir
            alpha_now = cell_norm(model_dir)
            model_dir = model_dir / alpha_now[:, None]
            theta_now = sine_part * alpha_now
            rho_bar = -cosine * alpha_now
            search = model_dir - (theta_now / rho_now)[:, None] * search
    residual = data - forward(solution.astype(jnp.bfloat16))
    return (solution, residual)


def solution(mesh):
    return jax.shard_map(
        per_device,
        mesh=mesh,
        in_specs=(
            P(None, ("ray", "tile")),
            P(("ray", "tile"), None, None),
            P(("ray", "tile"), None, None),
            P(("ray", "tile"), None, None),
        ),
        out_specs=(P(None, "tile"), P(None, ("ray", "tile"))),
        check_vma=False,
    )
```

profile of v0, /device:TPU:1, one launch (start us, length us, event | category | flops | bytes accessed | tf_op | source)
XLA Modules:
  0.0 731.6 jit_solution(17410393598439722855)
XLA Ops:
  7.2 1.3 copy.22
  8.5 6.0 all-to-all-start
  14.5 0.8 copy.23
  15.3 1.2 multiply_reduce_fusion.4
  16.5 67.7 %psum.49 = f32[64]{0:T(128)S(1)} all-reduce(f32[64]{0:T(128)S(1)} %multiply_reduce_fusion.4), channel_id=1, replica_groups=mesh['ray'=16,'tile'=8] {'ray','tile'}, use_global_device_ids=true, to_apply=%region_1.0 | all-reduce | flops 64 | bytes 512 | tf_op jit(solution)/shard_map/psum | solution.py:63
  84.3 1.1 fusion.19
  85.5 0.6 gather_fusion
  86.1 6.3 convert_bitcast_fusion.1
  92.4 4.4 all-to-all-start.1
  96.8 0.5 broadcast.102
  97.3 0.7 reduce.3
  98.1 25.1 %all-to-all-done.1 = bf16[64,32,512]{2,0,1:T(8,128)(2,1)S(1)} async-done(((bf16[64,32,512]{2,0,1:T(8,128)(2,1)}), bf16[64,32,512]{2,0,1:T(8,128)(2,1)S(1)}, u32[]{:S(2)}, u32[]{:S(2)}) %all-to-all-start.1) | async-done | bytes 2097184 | tf_op jit(solution)/shard_map/all_to_all | solution.py:50
  123.1 1.7 fusion.8
  124.9 6.3 copy.39
  131.3 119.1 %all-reduce.3.cloned.1.call-done = f32[64,24576]{1,0:T(8,128)} async-done(((f32[64,24576]{1,0:T(8,128)}), f32[64,24576]{1,0:T(8,128)}) %all-reduce.3.cloned.1.call-update) | async-done | bytes 6291472 | tf_op jit(solution)/shard_map/psum | solution.py:54
  250.4 3.3 multiply_reduce_fusion.1
  253.7 12.4 %psum.51 = f32[64]{0:T(128)S(1)} all-reduce(f32[64]{0:T(128)S(1)} %multiply_reduce_fusion.1), channel_id=1, replica_groups=mesh['ray'=16,'tile'=8] {'tile'}, use_global_device_ids=true, to_apply=%region_4.6 | all-reduce | flops 64 | bytes 512 | tf_op jit(solution)/shard_map/psum | solution.py:59
  266.1 3.2 fusion.37
  269.4 0.4 copy.61
  269.8 2.0 gather_fusion.1
  271.8 1.8 select_bitcast_fusion.2
  273.7 31.7 %all_to_all.30 = bf16[64,32,512]{2,0,1:T(8,128)(2,1)S(1)} all-to-all(bf16[64,32,512]{2,0,1:T(8,128)(2,1)S(1)} %select_bitcast_fusion.2), channel_id=1, replica_groups=mesh['ray'=16,'tile'=8] {'tile'}, dimensions={1} | all-to-all | bytes 4194304 | tf_op jit(solution)/shard_map/all_to_all | solution.py:32
  305.4 6.0 fusion.41
  311.5 2.0 fusion.6
  313.9 64.5 %psum.52 = f32[64]{0:T(128)S(1)} all-reduce(f32[64]{0:T(128)S(1)} %get-tuple-element.11), channel_id=1, replica_groups=mesh['ray'=16,'tile'=8] {'ray','tile'}, use_global_device_ids=true, to_apply=%region_6.0 | all-reduce | flops 64 | bytes 512 | tf_op jit(solution)/shard_map/psum | solution.py:63
  378.6 0.6 gather_fusion.2
  379.2 5.0 convert_bitcast_fusion
  384.2 30.1 %all_to_all.31 = bf16[64,32,512]{2,0,1:T(8,128)(2,1)S(1)} all-to-all(bf16[64,32,512]{2,0,1:T(8,128)(2,1)S(1)} %convert_bitcast_fusion), channel_id=1, replica_groups=mesh['ray'=16,'tile'=8] {'tile'}, dimensions={1} | all-to-all | bytes 4194304 | tf_op jit(solution)/shard_map/all_to_all | solution.py:50
  414.3 1.7 fusion.4
  416.0 6.3 copy.41
  422.3 118.9 %all-reduce.5.cloned.1.call-done = f32[64,24576]{1,0:T(8,128)} async-done(((f32[64,24576]{1,0:T(8,128)}), f32[64,24576]{1,0:T(8,128)}) %all-reduce.5.cloned.1.call-update) | async-done | bytes 6291472 | tf_op jit(solution)/shard_map/psum | solution.py:54
  541.2 5.8 multiply_reduce_fusion
  547.0 12.4 %psum.54 = f32[64]{0:T(128)S(1)} all-reduce(f32[64]{0:T(128)S(1)} %multiply_reduce_fusion), channel_id=1, replica_groups=mesh['ray'=16,'tile'=8] {'tile'}, use_global_device_ids=true, to_apply=%region_9.12 | all-reduce | flops 64 | bytes 512 | tf_op jit(solution)/shard_map/psum | solution.py:59
  559.4 5.2 fusion.10
  564.6 0.4 copy.60
  565.1 2.0 gather_fusion.3
  567.1 1.8 select_bitcast_fusion.1
  568.9 31.7 %all_to_all.32 = bf16[64,32,512]{2,0,1:T(8,128)(2,1)S(1)} all-to-all(bf16[64,32,512]{2,0,1:T(8,128)(2,1)S(1)} %select_bitcast_fusion.1), channel_id=1, replica_groups=mesh['ray'=16,'tile'=8] {'tile'}, dimensions={1} | all-to-all | bytes 4194304 | tf_op jit(solution)/shard_map/all_to_all | solution.py:32
  600.7 6.0 fusion.42
  606.7 2.0 fusion.2
  609.1 64.8 %psum.55 = f32[64]{0:T(128)S(1)} all-reduce(f32[64]{0:T(128)S(1)} %multiply_reduce_fusion.2), channel_id=1, replica_groups=mesh['ray'=16,'tile'=8] {'ray','tile'}, use_global_device_ids=true, to_apply=%region_11.14 | all-reduce | flops 64 | bytes 512 | tf_op jit(solution)/shard_map/psum | solution.py:63
  673.9 7.4 %fusion.38 = (bf16[64,24576]{1,0:T(8,128)(2,1)S(1)}, f32[64,24576]{1,0:T(8,128)}) fusion(f32[64]{0:T(128)S(1)} %multiply_divide_fusion, f32[64]{0:T(128)S(1)} %add_sqrt_fusion, f32[64,24576]{1,0:T(8,128)} %all-reduce.5.cloned.1.call-done, f32[64]{0:T(128)S(1)} %get-tuple-element.13, f32[64]{0:T(128)S(1)} %get-tuple-element.9, ...), kind=kLoop, calls=%fused_computation.76 | loop fusion | flops 15728640 | bytes 22021632 | tf_op jit(solution)/shard_map/convert_element_type | solution.py:93
  681.7 2.0 gather_fusion.4
  683.7 1.8 select_bitcast_fusion
  685.6 30.1 %all_to_all.33 = bf16[64,32,512]{2,0,1:T(8,128)(2,1)S(1)} all-to-all(bf16[64,32,512]{2,0,1:T(8,128)(2,1)S(1)} %select_bitcast_fusion), channel_id=1, replica_groups=mesh['ray'=16,'tile'=8] {'tile'}, dimensions={1} | all-to-all | bytes 4194304 | tf_op jit(solution)/shard_map/all_to_all | solution.py:32
  715.7 6.0 fusion.43
  721.8 2.0 fusion
  723.9 0.9 sub.19
  (36 shorter events, 1.9 us)
Async XLA Ops:
  8.5 83.9 %all-to-all-start = ((s32[1,8,4]{2,0,1:T(1,128)}), s32[1,8,4]{2,0,1:T(1,128)S(1)}, u32[]{:S(2)}, u32[]{:S(2)}) async-start(s32[1,8,4]{2,0,1:T(1,128)} %copy.22), calls=%async_computation | async-start | bytes 8192 | tf_op jit(solution)/shard_map/all_to_all | solution.py:19
  92.4 30.8 %all-to-all-start.1 = ((bf16[64,32,512]{2,0,1:T(8,128)(2,1)}), bf16[64,32,512]{2,0,1:T(8,128)(2,1)S(1)}, u32[]{:S(2)}, u32[]{:S(2)}) async-start(bf16[64,32,512]{2,0,1:T(8,128)(2,1)} %convert_bitcast_fusion.1), calls=%async_computation.1 | async-start | bytes 4194304 | tf_op jit(solution)/shard_map/all_to_all | solution.py:50
  96.8 153.6 %all-reduce.3.cloned.1.call-start = ((), (), s32[]{:S(2)}) async-start(), calls=%async_computation.6 | async-start | bytes 12582912 | tf_op jit(solution)/shard_map/psum | solution.py:54
  131.2 410.0 %all-reduce.5.cloned.1.call-start = ((), (), s32[]{:S(2)}) async-start(), calls=%async_computation.7 | async-start | bytes 12582912 | tf_op jit(solution)/shard_map/psum | solution.py:54
  311.4 2.1 copy-start
  313.9 64.7 %copy-start.2 = (f32[64,2048]{1,0:T(8,128)}, f32[64,2048]{1,0:T(8,128)S(1)}, u32[]{:S(2)}) copy-start(f32[64,2048]{1,0:T(8,128)S(1)} %get-tuple-element.12) | copy-start | bytes 1572868
  606.7 2.1 copy-start.3
  721.7 2.1 copy-start.1
Sparse Core Ops, SparseCore 0:
  131.3 119.0 all-reduce.2
  422.4 118.6 all-reduce.4
where the time goes:
time: 733 us; the launch traced here: 732 us
  blocking collectives  346 us (47%)
  waiting for transfers between devices  263 us (36%)
  matrix products  38.8 us (5%)
  other arithmetic  35 us (5%)
  local copies, waits for them, and re-layouts  24.4 us (3%)
  between operations  14.3 us (2%)
  starting transfers between devices  10.4 us (1%)
    psum x2, waiting for transfers between devices, adjoint(): total = lax.psum(owned, 'ray')  238 us
    psum x3, blocking collectives, ray_norm(): total = lax.psum(jnp.sum(rays * rays, axis=1), ('ray', 'tile'))  197 us
    all_to_all x3, blocking collectives, fetch(): lax.all_to_all(outgoing, 'tile', split_axis=1, concat_axis=1, tiled=True)  93.6 us
    all_to_all x1, blocking collectives, adjoint(): lax.all_to_all(terms, 'tile', split_axis=1, concat_axis=1, tiled=True)  30.1 us
    all_to_all x1, waiting for transfers between devices, adjoint(): lax.all_to_all(terms, 'tile', split_axis=1, concat_axis=1, tiled=True)  25.1 us
    psum x2, blocking collectives, cell_norm(): total = lax.psum(local, 'tile')  24.9 us
    dot_general x3, matrix products, forward(): jnp.einsum('cnk,nrk->ncr', tiles, sensitivity, preferred_element_type=jnp...  18.1 us
    unnamed x15, local copies, waits for them, and re-layouts  15.1 us
  transfers between devices with their start and end apart: 4, of which 3 were waited for; matrix products, arithmetic and copies ran while one was open for 2% of the time, Pallas kernels for 0%

commit v1 on v0

--- a/solution.py
+++ b/solution.py
@@ -10,10 +10,99 @@
 TILE_DEV = 48
 
 
+import functools
+from jax.experimental import pallas as pl
+from jax.experimental.pallas import tpu as pltpu
+
+MESH = pl.DeviceIdType.MESH
+
+
+def stage_plan(mesh, axes):
+    plan = []
+    if "tile" in axes:
+        tiles = mesh.shape["tile"]
+        plan += [("tile", 2, 1), ("tile", tiles // 2, 2)]
+    if "ray" in axes:
+        rays = mesh.shape["ray"]
+        inner = 4 if rays % 4 == 0 else 1
+        plan += [("ray", inner, 1), ("ray", rays // inner, inner)]
+    return tuple(stage for stage in plan if stage[1] > 1)
+
+
+def reduce_kernel(plan, x_ref, o_ref, vals, send_sems, recv_sems):
+    here = {"ray": lax.axis_index("ray"), "tile": lax.axis_index("tile")}
+
+    def peer(axis, size, stride, k):
+        idx = here[axis]
+        pos = (idx // stride) % size
+        other = idx + (((pos + k) % size) - pos) * stride
+        coords = dict(here)
+        coords[axis] = other
+        return (coords["ray"], coords["tile"])
+
+    barrier = pltpu.get_barrier_semaphore()
+    count = 0
+    for axis, size, stride in plan:
+        for k in range(1, size):
+            pl.semaphore_signal(barrier, inc=1, device_id=peer(axis, size, stride, k), device_id_type=MESH)
+            count += 1
+    pl.semaphore_wait(barrier, count)
+
+    vals[0, 0] = x_ref[...]
+    copies = []
+    for s, (axis, size, stride) in enumerate(plan):
+        src = x_ref if s == 0 else vals.at[s, 0]
+        stage_copies = []
+        for k in range(1, size):
+            copy = pltpu.make_async_remote_copy(
+                src_ref=src,
+                dst_ref=vals.at[s, k],
+                send_sem=send_sems.at[s, k],
+                recv_sem=recv_sems.at[s, k],
+                device_id=peer(axis, size, stride, (size - k) % size),
+                device_id_type=MESH,
+            )
+            copy.start()
+            stage_copies.append(copy)
+        for copy in stage_copies:
+            copy.wait_recv()
+        copies += stage_copies
+        pos = (here[axis] // stride) % size
+        total = vals[s, (size - pos) % size]
+        for q in range(1, size):
+            total = total + vals[s, (q - pos + size) % size]
+        if s + 1 < len(plan):
+            vals[s + 1, 0] = total
+        else:
+            o_ref[...] = total
+    for copy in copies:
+        copy.wait_send()
+
+
+def group_sum(mesh, axes, collective_id, partial):
+    plan = stage_plan(mesh, axes)
+    width = partial.shape[0]
+    block = jnp.zeros((8, 128), jnp.float32).at[0, :width].set(partial)
+    depth = max(size for _, size, _ in plan)
+    out = pl.pallas_call(
+        functools.partial(reduce_kernel, plan),
+        out_shape=jax.ShapeDtypeStruct((8, 128), jnp.float32),
+        in_specs=[pl.BlockSpec(memory_space=pltpu.VMEM)],
+        out_specs=pl.BlockSpec(memory_space=pltpu.VMEM),
+        scratch_shapes=[
+            pltpu.VMEM((len(plan), depth, 8, 128), jnp.float32),
+            pltpu.SemaphoreType.DMA((len(plan), depth)),
+            pltpu.SemaphoreType.DMA((len(plan), depth)),
+        ],
+        compiler_params=pltpu.CompilerParams(collective_id=collective_id, has_side_effects=True),
+    )(block)
+    return out[0, :width]
+
+
 eps_norm = 1e-06
 
 
-def per_device(data, sensitivity, block_tiles, block_bundles):
+def per_device(mesh, data, sensitivity, block_tiles, block_bundles):
     columns = data.shape[0]
     bundles = block_bundles.reshape(-1)
     requests = lax.all_to_all(block_tiles, "tile", split_axis=1, concat_axis=1, tiled=True).reshape(
@@ -56,11 +145,11 @@
 
     def cell_norm(field):
         local = jnp.sum(field * field, axis=1)
-        total = lax.psum(local, "tile")
+        total = group_sum(mesh, ("tile",), 1, local)
         return jnp.sqrt(total + eps_norm)
 
     def ray_norm(rays):
-        total = lax.psum(jnp.sum(rays * rays, axis=1), ("ray", "tile"))
+        total = group_sum(mesh, ("ray", "tile"), 0, jnp.sum(rays * rays, axis=1))
         return jnp.sqrt(total + eps_norm)
 
     beta_now = ray_norm(data)
@@ -96,7 +185,7 @@
 
 def solution(mesh):
     return jax.shard_map(
-        per_device,
+        functools.partial(per_device, mesh),
         mesh=mesh,
         in_specs=(
             P(None, ("ray", "tile")),

time: 733 us -> 581 us (0.79)
  blocking collectives: 346 us -> 93.2 us
  Pallas kernels: 0 us -> 58.7 us
  waiting for transfers between devices: 263 us -> 290 us
    psum x5 -> x0, blocking collectives: 222 us -> none  [the longest x3 197 us: ray_norm(): total = lax.psum(jnp.sum(rays * rays, axis=1), ('ray', 'tile'))]
    pallas_call x0 -> x5, Pallas kernels: none -> 58.7 us  [group_sum(): pl.pallas_call(functools.partial(reduce_kernel, plan), out_shape=jax.Shap...]
    all_to_all x3 -> x2, blocking collectives: 93.6 us -> 61.8 us  [fetch(): lax.all_to_all(outgoing, 'tile', split_axis=1, concat_axis=1, tiled=True)]
    all_to_all x0 -> x1, waiting for transfers between devices: none -> 25.6 us  [fetch(): lax.all_to_all(outgoing, 'tile', split_axis=1, concat_axis=1, tiled=True)]
  transfers between devices with their start and end apart: 4 -> 5, of which waited for: 3 -> 4; matrix products, arithmetic and copies ran while one was open for 2% -> 2% of each run, Pallas kernels for 0% -> 3%
where the time goes in v1:
time: 581 us; the launch traced here: 580 us
  waiting for transfers between devices  290 us (50%)
  blocking collectives  93.2 us (16%)
  Pallas kernels  58.7 us (10%)
  other arithmetic  41.2 us (7%)
  matrix products  38.7 us (7%)
  local copies, waits for them, and re-layouts  27.4 us (5%)
  starting transfers between devices  16 us (3%)
  between operations  14.4 us (2%)
    psum x2, waiting for transfers between devices, adjoint(): total = lax.psum(owned, 'ray')  239 us
    all_to_all x2, blocking collectives, fetch(): lax.all_to_all(outgoing, 'tile', split_axis=1, concat_axis=1, tiled=True)  61.8 us
    pallas_call x5, Pallas kernels, group_sum(): pl.pallas_call(functools.partial(reduce_kernel, plan), out_shape=jax.Shap...  58.7 us
    all_to_all x1, blocking collectives, adjoint(): lax.all_to_all(terms, 'tile', split_axis=1, concat_axis=1, tiled=True)  31.5 us
    all_to_all x1, waiting for transfers between devices, fetch(): lax.all_to_all(outgoing, 'tile', split_axis=1, concat_axis=1, tiled=True)  25.6 us
    all_to_all x1, waiting for transfers between devices, adjoint(): lax.all_to_all(terms, 'tile', split_axis=1, concat_axis=1, tiled=True)  25.1 us
    dot_general x3, matrix products, forward(): jnp.einsum('cnk,nrk->ncr', tiles, sensitivity, preferred_element_type=jnp...  18.1 us
    unnamed x15, local copies, waits for them, and re-layouts  15.1 us
  transfers between devices with their start and end apart: 5, of which 4 were waited for; matrix products, arithmetic and copies ran while one was open for 2% of the time, Pallas kernels for 3%

profile of v1, /device:TPU:1, one launch (start us, length us, event | category | flops | bytes accessed | tf_op | source)
XLA Modules:
  0.0 579.5 jit_solution(17672580953668457361)
XLA Ops:
  7.2 1.3 copy.22
  8.5 6.0 %all-to-all-start = ((s32[1,8,4]{2,0,1:T(1,128)}), s32[1,8,4]{2,0,1:T(1,128)S(1)}, u32[]{:S(2)}, u32[]{:S(2)}) async-start(s32[1,8,4]{2,0,1:T(1,128)} %copy.22), calls=%async_computation | async-start | bytes 8192 | tf_op jit(solution)/shard_map/all_to_all | solution.py:108
  14.5 0.8 copy.23
  15.3 1.2 multiply_reduce_fusion.4
  17.1 16.5 %shard_map.59 = f32[8,128]{1,0:T(8,128)} custom-call(f32[8,128]{1,0:T(8,128)} %scatter.16.x_ref), custom_call_target="tpu_custom_call" | custom-call | tf_op jit(solution)/shard_map/pallas_call | solution.py:87
  34.3 1.1 fusion.19
  36.1 6.3 %convert_bitcast_fusion.1 = bf16[64,32,512]{2,0,1:T(8,128)(2,1)} fusion(bf16[32,256,512]{2,1,0:T(8,128)(2,1)} %param.19, bf16[32,64,256]{2,1,0:T(8,128)(2,1)S(1)} %gather_fusion, pred[32]{0:T(512)(128)(4,1)S(1)} %compare_and_fusion.1), kind=kOutput, calls=%fused_computation.28 | convolution fusion | flops 538443776 | bytes 11534368 | tf_op jit(solution)/shard_map/cnr,nrk->cnk/dot_general | solution.py:136
  42.4 6.0 %all-to-all-start.1 = ((bf16[64,32,512]{2,0,1:T(8,128)(2,1)}), bf16[64,32,512]{2,0,1:T(8,128)(2,1)S(1)}, u32[]{:S(2)}, u32[]{:S(2)}) async-start(bf16[64,32,512]{2,0,1:T(8,128)(2,1)} %convert_bitcast_fusion.1), calls=%async_computation.1 | async-start | bytes 4194304 | tf_op jit(solution)/shard_map/all_to_all | solution.py:139
  49.7 25.1 %all-to-all-done.1 = bf16[64,32,512]{2,0,1:T(8,128)(2,1)S(1)} async-done(((bf16[64,32,512]{2,0,1:T(8,128)(2,1)}), bf16[64,32,512]{2,0,1:T(8,128)(2,1)S(1)}, u32[]{:S(2)}, u32[]{:S(2)}) %all-to-all-start.1) | async-done | bytes 2097184 | tf_op jit(solution)/shard_map/all_to_all | solution.py:139
  74.8 1.7 fusion.8
  76.5 6.3 %copy.39 = f32[8,8,48,512]{3,1,2,0:T(8,128)} copy(f32[8,8,48,512]{3,2,1,0:T(8,128)S(1)} %bitcast.111) | data formatting | bytes 12582912
  82.9 119.5 %all-reduce.8.cloned.1.call-done = f32[64,24576]{1,0:T(8,128)} async-done(((f32[64,24576]{1,0:T(8,128)}), f32[64,24576]{1,0:T(8,128)}) %all-reduce.8.cloned.1.call-update) | async-done | bytes 6291472 | tf_op jit(solution)/shard_map/psum | solution.py:143
  202.4 3.3 multiply_reduce_fusion.1
  206.3 7.7 %shard_map.60 = f32[8,128]{1,0:T(8,128)} custom-call(f32[8,128]{1,0:T(8,128)} %scatter.19.x_ref), custom_call_target="tpu_custom_call" | custom-call | tf_op jit(solution)/shard_map/pallas_call | solution.py:87
  214.7 3.2 fusion.38
  218.3 2.0 gather_fusion.1
  220.3 1.8 select_bitcast_fusion.2
  222.2 30.3 %all_to_all.30 = bf16[64,32,512]{2,0,1:T(8,128)(2,1)S(1)} all-to-all(bf16[64,32,512]{2,0,1:T(8,128)(2,1)S(1)} %select_bitcast_fusion.2), channel_id=1, replica_groups=mesh['ray'=16,'tile'=8] {'tile'}, dimensions={1} | all-to-all | bytes 4194304 | tf_op jit(solution)/shard_map/all_to_all | solution.py:121
  252.5 6.0 %fusion.42 = f32[32,64,256]{2,1,0:T(8,128)S(1)} fusion(bf16[64,32,512]{2,0,1:T(8,128)(2,1)S(1)} %all_to_all.30, bf16[32,256,512]{2,1,0:T(8,128)(2,1)} %param.19), kind=kOutput, calls=%fused_computation.79 | convolution fusion | flops 536870912 | bytes 12582912 | tf_op jit(solution)/shard_map/cnk,nrk->ncr/dot_general | solution.py:126
  258.5 2.0 fusion.6
  261.6 13.5 %shard_map.61 = f32[8,128]{1,0:T(8,128)} custom-call(f32[8,128]{1,0:T(8,128)} %scatter.20.x_ref), custom_call_target="tpu_custom_call" | custom-call | tf_op jit(solution)/shard_map/pallas_call | solution.py:87
  275.1 0.7 sqrt_bitcast_fusion.1
  276.5 5.0 convert_bitcast_fusion
  281.5 31.5 %all_to_all.31 = bf16[64,32,512]{2,0,1:T(8,128)(2,1)S(1)} all-to-all(bf16[64,32,512]{2,0,1:T(8,128)(2,1)S(1)} %convert_bitcast_fusion), channel_id=1, replica_groups=mesh['ray'=16,'tile'=8] {'tile'}, dimensions={1} | all-to-all | bytes 4194304 | tf_op jit(solution)/shard_map/all_to_all | solution.py:139
  313.0 1.7 fusion.4
  314.8 6.3 %copy.41 = f32[8,8,48,512]{3,1,2,0:T(8,128)} copy(f32[8,8,48,512]{3,2,1,0:T(8,128)S(1)} %bitcast.110) | data formatting | bytes 12582912
  321.1 119.6 %all-reduce.10.cloned.1.call-done = f32[64,24576]{1,0:T(8,128)} async-done(((f32[64,24576]{1,0:T(8,128)}), f32[64,24576]{1,0:T(8,128)}) %all-reduce.10.cloned.1.call-update) | async-done | bytes 6291472 | tf_op jit(solution)/shard_map/psum | solution.py:143
  440.7 5.8 multiply_reduce_fusion
  447.1 7.7 %shard_map.62 = f32[8,128]{1,0:T(8,128)} custom-call(f32[8,128]{1,0:T(8,128)} %scatter.21.x_ref), custom_call_target="tpu_custom_call" | custom-call | tf_op jit(solution)/shard_map/pallas_call | solution.py:87
  454.8 0.7 sqrt_bitcast_fusion
  455.5 5.2 fusion.10
  461.2 2.0 gather_fusion.3
  463.2 3.2 select_bitcast_fusion.1
  466.3 4.0 all-to-all-start.4
  470.3 0.7 multiply_divide_fusion.2
  471.1 25.6 %all-to-all-done.4 = bf16[64,32,512]{2,0,1:T(8,128)(2,1)S(1)} async-done(((bf16[64,32,512]{2,0,1:T(8,128)(2,1)}), bf16[64,32,512]{2,0,1:T(8,128)(2,1)S(1)}, u32[]{:S(2)}, u32[]{:S(2)}) %all-to-all-start.4) | async-done | bytes 2097184 | tf_op jit(solution)/shard_map/all_to_all | solution.py:121
  496.7 6.0 %fusion.43 = f32[32,64,256]{2,1,0:T(8,128)S(1)} fusion(bf16[64,32,512]{2,0,1:T(8,128)(2,1)S(1)} %all-to-all-done.4, bf16[32,256,512]{2,1,0:T(8,128)(2,1)} %param.19), kind=kOutput, calls=%fused_computation.80 | convolution fusion | flops 536870912 | bytes 12582912 | tf_op jit(solution)/shard_map/cnk,nrk->ncr/dot_general | solution.py:126
  502.7 2.0 fusion.2
  505.7 13.3 %shard_map.63 = f32[8,128]{1,0:T(8,128)} custom-call(f32[8,128]{1,0:T(8,128)} %scatter.24.x_ref), custom_call_target="tpu_custom_call" | custom-call | tf_op jit(solution)/shard_map/pallas_call | solution.py:87
  519.0 0.7 multiply_divide_fusion.1
  519.8 0.7 multiply_divide_fusion
  520.5 7.4 %fusion.39 = (bf16[64,24576]{1,0:T(8,128)(2,1)S(1)}, f32[64,24576]{1,0:T(8,128)}) fusion(f32[64]{0:T(128)S(1)} %multiply_divide_fusion, f32[64]{0:T(128)S(1)} %sqrt_bitcast_fusion, f32[64,24576]{1,0:T(8,128)} %all-reduce.10.cloned.1.call-done, f32[64]{0:T(128)S(1)} %sqrt_bitcast_fusion.1, f32[64]{0:T(128)S(1)} %get-tuple-element.69, ...), kind=kLoop, calls=%fused_computation.78 | loop fusion | flops 15728640 | bytes 22021632 | tf_op jit(solution)/shard_map/convert_element_type | solution.py:182
  528.2 2.0 gather_fusion.4
  530.3 1.8 select_bitcast_fusion
  532.1 31.5 %all_to_all.32 = bf16[64,32,512]{2,0,1:T(8,128)(2,1)S(1)} all-to-all(bf16[64,32,512]{2,0,1:T(8,128)(2,1)S(1)} %select_bitcast_fusion), channel_id=1, replica_groups=mesh['ray'=16,'tile'=8] {'tile'}, dimensions={1} | all-to-all | bytes 4194304 | tf_op jit(solution)/shard_map/all_to_all | solution.py:121
  563.6 6.0 %fusion.44 = f32[32,64,256]{2,1,0:T(8,128)S(1)} fusion(bf16[64,32,512]{2,0,1:T(8,128)(2,1)S(1)} %all_to_all.32, bf16[32,256,512]{2,1,0:T(8,128)(2,1)} %param.19), kind=kOutput, calls=%fused_computation.81 | convolution fusion | flops 536870912 | bytes 12582912 | tf_op jit(solution)/shard_map/cnk,nrk->ncr/dot_general | solution.py:126
  569.7 2.0 fusion
  571.8 0.9 sub.19
  (43 shorter events, 9.5 us)
Async XLA Ops:
  8.5 33.9 %all-to-all-start = ((s32[1,8,4]{2,0,1:T(1,128)}), s32[1,8,4]{2,0,1:T(1,128)S(1)}, u32[]{:S(2)}, u32[]{:S(2)}) async-start(s32[1,8,4]{2,0,1:T(1,128)} %copy.22), calls=%async_computation | async-start | bytes 8192 | tf_op jit(solution)/shard_map/all_to_all | solution.py:108
  42.4 32.3 %all-to-all-start.1 = ((bf16[64,32,512]{2,0,1:T(8,128)(2,1)}), bf16[64,32,512]{2,0,1:T(8,128)(2,1)S(1)}, u32[]{:S(2)}, u32[]{:S(2)}) async-start(bf16[64,32,512]{2,0,1:T(8,128)(2,1)} %convert_bitcast_fusion.1), calls=%async_computation.1 | async-start | bytes 4194304 | tf_op jit(solution)/shard_map/all_to_all | solution.py:139
  48.4 154.0 %all-reduce.8.cloned.1.call-start = ((), (), s32[]{:S(2)}) async-start(), calls=%async_computation.6 | async-start | bytes 12582912 | tf_op jit(solution)/shard_map/psum | solution.py:143
  82.8 357.9 %all-reduce.10.cloned.1.call-start = ((), (), s32[]{:S(2)}) async-start(), calls=%async_computation.7 | async-start | bytes 12582912 | tf_op jit(solution)/shard_map/psum | solution.py:143
  258.5 2.1 copy-start
  260.9 15.0 %copy-start.2 = (f32[64,2048]{1,0:T(8,128)}, f32[64,2048]{1,0:T(8,128)S(1)}, u32[]{:S(2)}) copy-start(f32[64,2048]{1,0:T(8,128)S(1)} %get-tuple-element.72) | copy-start | bytes 1572868
  466.3 30.3 %all-to-all-start.4 = ((bf16[64,32,512]{2,0,1:T(8,128)(2,1)}), bf16[64,32,512]{2,0,1:T(8,128)(2,1)S(1)}, u32[]{:S(2)}, u32[]{:S(2)}) async-start(bf16[64,32,512]{2,0,1:T(8,128)(2,1)} %select_bitcast_fusion.1), calls=%async_computation.4 | async-start | bytes 4194304 | tf_op jit(solution)/shard_map/all_to_all | solution.py:121
  502.7 2.1 copy-start.3
  569.6 2.1 copy-start.1
Sparse Core Ops, SparseCore 0:
  82.9 119.4 all-reduce.7
  321.2 119.4 all-reduce.9

commit v2 on v1

--- a/solution.py
+++ b/solution.py
@@ -140,12 +140,14 @@
         owned = jnp.einsum(
             "cnk,nt->ctk", arrived, owner_onehot, preferred_element_type=jnp.float32
         ).reshape(columns, TILE_DEV * CB)
-        total = lax.psum(owned, "ray")
-        return total
+        return lax.psum_scatter(owned, "ray", scatter_dimension=1, tiled=True)
+
+    def gather_bf(field):
+        return lax.all_gather(field.astype(jnp.bfloat16), "ray", axis=1, tiled=True)
 
     def cell_norm(field):
         local = jnp.sum(field * field, axis=1)
-        total = group_sum(mesh, ("tile",), 1, local)
+        total = group_sum(mesh, ("ray", "tile"), 0, local)
         return jnp.sqrt(total + eps_norm)
 
     def ray_norm(rays):
@@ -162,8 +164,7 @@
     phi_bar = beta_now
     rho_bar = alpha_now
     for step in range(ITERS):
-        rounded = model_dir.astype(jnp.bfloat16)
-        rays_dir = forward(rounded) - alpha_now[:, None] * rays_dir
+        rays_dir = forward(gather_bf(model_dir)) - alpha_now[:, None] * rays_dir
         beta_now = ray_norm(rays_dir)
         rays_dir = rays_dir / beta_now[:, None]
         rho_now = jnp.sqrt(rho_bar * rho_bar + beta_now * beta_now)
@@ -179,6 +180,7 @@
             theta_now = sine_part * alpha_now
             rho_bar = -cosine * alpha_now
             search = model_dir - (theta_now / rho_now)[:, None] * search
+    solution = lax.all_gather(solution, "ray", axis=1, tiled=True)
     residual = data - forward(solution.astype(jnp.bfloat16))
     return (solution, residual)
 

time: 581 us -> 657 us (1.13)
  waiting for transfers between devices: 290 us -> 358 us
  other arithmetic: 41.2 us -> 26.3 us
  Pallas kernels: 58.7 us -> 72.3 us
  local copies, waits for them, and re-layouts: 27.4 us -> 34 us
    psum x2 -> x0, waiting for transfers between devices: 239 us -> none  [adjoint(): total = lax.psum(owned, 'ray')]
    reduce_scatter x0 -> x2, waiting for transfers between devices: none -> 155 us  [adjoint(): return lax.psum_scatter(owned, 'ray', scatter_dimension=1, tiled=True)]
    all_gather x0 -> x3, waiting for transfers between devices: none -> 153 us  [the longest x2 92.2 us: gather_bf(): return lax.all_gather(field.astype(jnp.bfloat16), 'ray', axis=1, tiled=True)]
    pallas_call x5, Pallas kernels: 58.7 us -> 72.3 us  [group_sum(): pl.pallas_call(functools.partial(reduce_kernel, plan), out_shape=jax.Shap...]
    reduce_sum x2, other arithmetic: 9.08 us -> 2.36 us  [cell_norm(): local = jnp.sum(field * field, axis=1)]
    unnamed x15 -> x32, local copies, waits for them, and re-layouts: 15.1 us -> 17.9 us
  transfers between devices with their start and end apart: 5 -> 8, of which waited for: 4 -> 7; matrix products, arithmetic and copies ran while one was open for 2% -> 2% of each run, Pallas kernels for 3% -> 3%
where the time goes in v2:
time: 657 us; the launch traced here: 656 us
  waiting for transfers between devices  358 us (54%)
  blocking collectives  94.4 us (14%)
  Pallas kernels  72.3 us (11%)
  matrix products  38.9 us (6%)
  local copies, waits for them, and re-layouts  34 us (5%)
  other arithmetic  26.3 us (4%)
  starting transfers between devices  17.6 us (3%)
  between operations  14.1 us (2%)
    reduce_scatter x2, waiting for transfers between devices, adjoint(): return lax.psum_scatter(owned, 'ray', scatter_dimension=1, tiled=True)  155 us
    all_gather x2, waiting for transfers between devices, gather_bf(): return lax.all_gather(field.astype(jnp.bfloat16), 'ray', axis=1, tiled=True)  92.2 us
    pallas_call x5, Pallas kernels, group_sum(): pl.pallas_call(functools.partial(reduce_kernel, plan), out_shape=jax.Shap...  72.3 us
    all_to_all x2, blocking collectives, fetch(): lax.all_to_all(outgoing, 'tile', split_axis=1, concat_axis=1, tiled=True)  63 us
    all_gather x1, waiting for transfers between devices, per_device(): solution = lax.all_gather(solution, 'ray', axis=1, tiled=True)  60.4 us
    all_to_all x1, blocking collectives, adjoint(): lax.all_to_all(terms, 'tile', split_axis=1, concat_axis=1, tiled=True)  31.3 us
    all_to_all x1, waiting for transfers between devices, fetch(): lax.all_to_all(outgoing, 'tile', split_axis=1, concat_axis=1, tiled=True)  25.6 us
    all_to_all x1, waiting for transfers between devices, adjoint(): lax.all_to_all(terms, 'tile', split_axis=1, concat_axis=1, tiled=True)  25.1 us
  transfers between devices with their start and end apart: 8, of which 7 were waited for; matrix products, arithmetic and copies ran while one was open for 2% of the time, Pallas kernels for 3%

profile of v2, /device:TPU:1, one launch (start us, length us, event | category | flops | bytes accessed | tf_op | source)
XLA Modules:
  0.0 655.8 jit_solution(8162690014933639291)
XLA Ops:
  7.2 1.3 copy.22
  8.5 6.0 all-to-all-start
  15.3 1.2 multiply_reduce_fusion.2
  17.1 16.5 %shard_map.59 = f32[8,128]{1,0:T(8,128)} custom-call(f32[8,128]{1,0:T(8,128)} %scatter.16.x_ref), custom_call_target="tpu_custom_call" | custom-call | tf_op jit(solution)/shard_map/pallas_call | solution.py:87
  34.3 1.1 fusion.18
  36.1 6.3 convert_bitcast_fusion.1
  42.4 6.0 all-to-all-start.1
  49.7 25.1 %all-to-all-done.1 = bf16[64,32,512]{2,0,1:T(8,128)(2,1)S(1)} async-done(((bf16[64,32,512]{2,0,1:T(8,128)(2,1)}), bf16[64,32,512]{2,0,1:T(8,128)(2,1)S(1)}, u32[]{:S(2)}, u32[]{:S(2)}) %all-to-all-start.1) | async-done | bytes 2097184 | tf_op jit(solution)/shard_map/all_to_all | solution.py:139
  74.8 1.7 fusion.8
  76.5 6.3 copy.39
  82.8 77.5 %reduce-scatter.3.cloned.1.call-done = f32[64,1536]{1,0:T(8,128)} async-done(((f32[64,24576]{1,0:T(8,128)}), f32[64,1536]{1,0:T(8,128)}) %reduce-scatter.3.cloned.1.call-update) | async-done | bytes 393232 | tf_op jit(solution)/shard_map/reduce_scatter | solution.py:143
  160.3 1.1 multiply_reduce_fusion.4
  162.1 15.4 %shard_map.60 = f32[8,128]{1,0:T(8,128)} custom-call(f32[8,128]{1,0:T(8,128)} %scatter.19.x_ref), custom_call_target="tpu_custom_call" | custom-call | tf_op jit(solution)/shard_map/pallas_call | solution.py:87
  178.1 1.8 fusion.38
  180.0 46.1 %all-gather.4.cloned.1.call-done = bf16[64,24576]{1,0:T(8,128)(2,1)} async-done(((bf16[64,1536]{1,0:T(8,128)(2,1)}), bf16[64,24576]{1,0:T(8,128)(2,1)}) %all-gather.4.cloned.1.call-update) | async-done | bytes 3145744 | tf_op jit(solution)/shard_map/all_gather | solution.py:146
  226.1 2.3 copy.61
  228.4 2.0 gather_fusion.1
  230.4 1.8 select_bitcast_fusion.2
  232.3 31.5 %all_to_all.30 = bf16[64,32,512]{2,0,1:T(8,128)(2,1)S(1)} all-to-all(bf16[64,32,512]{2,0,1:T(8,128)(2,1)S(1)} %select_bitcast_fusion.2), channel_id=1, replica_groups=mesh['ray'=16,'tile'=8] {'tile'}, dimensions={1} | all-to-all | bytes 4194304 | tf_op jit(solution)/shard_map/all_to_all | solution.py:121
  263.8 6.0 fusion.41
  269.9 2.0 fusion.6
  272.9 12.6 %shard_map.61 = f32[8,128]{1,0:T(8,128)} custom-call(f32[8,128]{1,0:T(8,128)} %scatter.20.x_ref), custom_call_target="tpu_custom_call" | custom-call | tf_op jit(solution)/shard_map/pallas_call | solution.py:87
  287.0 5.0 convert_bitcast_fusion
  292.0 31.3 %all_to_all.31 = bf16[64,32,512]{2,0,1:T(8,128)(2,1)S(1)} all-to-all(bf16[64,32,512]{2,0,1:T(8,128)(2,1)S(1)} %convert_bitcast_fusion), channel_id=1, replica_groups=mesh['ray'=16,'tile'=8] {'tile'}, dimensions={1} | all-to-all | bytes 4194304 | tf_op jit(solution)/shard_map/all_to_all | solution.py:139
  323.4 1.7 fusion.4
  325.1 6.3 copy.41
  331.7 77.4 %reduce-scatter.5.cloned.1.call-done = f32[64,1536]{1,0:T(8,128)} async-done(((f32[64,24576]{1,0:T(8,128)}), f32[64,1536]{1,0:T(8,128)}) %reduce-scatter.5.cloned.1.call-update) | async-done | bytes 393232 | tf_op jit(solution)/shard_map/reduce_scatter | solution.py:143
  409.1 1.2 multiply_reduce_fusion.3
  410.9 15.4 %shard_map.62 = f32[8,128]{1,0:T(8,128)} custom-call(f32[8,128]{1,0:T(8,128)} %scatter.21.x_ref), custom_call_target="tpu_custom_call" | custom-call | tf_op jit(solution)/shard_map/pallas_call | solution.py:87
  427.0 1.8 fusion.20
  428.8 46.2 %all-gather.6.cloned.1.call-done = bf16[64,24576]{1,0:T(8,128)(2,1)} async-done(((bf16[64,1536]{1,0:T(8,128)(2,1)}), bf16[64,24576]{1,0:T(8,128)(2,1)}) %all-gather.6.cloned.1.call-update) | async-done | bytes 3145744 | tf_op jit(solution)/shard_map/all_gather | solution.py:146
  475.0 2.3 copy.60
  477.3 2.0 gather_fusion.3
  479.3 3.2 select_bitcast_fusion.1
  482.5 5.3 all-to-all-start.4
  488.5 25.6 %all-to-all-done.4 = bf16[64,32,512]{2,0,1:T(8,128)(2,1)S(1)} async-done(((bf16[64,32,512]{2,0,1:T(8,128)(2,1)}), bf16[64,32,512]{2,0,1:T(8,128)(2,1)S(1)}, u32[]{:S(2)}, u32[]{:S(2)}) %all-to-all-start.4) | async-done | bytes 2097184 | tf_op jit(solution)/shard_map/all_to_all | solution.py:121
  514.1 6.0 fusion.42
  520.1 2.0 fusion.2
  523.1 12.5 %shard_map.63 = f32[8,128]{1,0:T(8,128)} custom-call(f32[8,128]{1,0:T(8,128)} %scatter.24.x_ref), custom_call_target="tpu_custom_call" | custom-call | tf_op jit(solution)/shard_map/pallas_call | solution.py:87
  537.0 1.0 multiply_add_fusion
  538.0 60.4 %all-gather.8.cloned.1.call-done = f32[64,24576]{1,0:T(8,128)} async-done(((f32[64,1536]{1,0:T(8,128)}), f32[64,24576]{1,0:T(8,128)}) %all-gather.8.cloned.1.call-update) | async-done | bytes 6291472 | tf_op jit(solution)/shard_map/all_gather | solution.py:183
  598.4 3.1 convert_element_type.37
  601.9 2.0 gather_fusion.4
  603.9 1.8 select_bitcast_fusion
  605.8 31.5 %all_to_all.32 = bf16[64,32,512]{2,0,1:T(8,128)(2,1)S(1)} all-to-all(bf16[64,32,512]{2,0,1:T(8,128)(2,1)S(1)} %select_bitcast_fusion), channel_id=1, replica_groups=mesh['ray'=16,'tile'=8] {'tile'}, dimensions={1} | all-to-all | bytes 4194304 | tf_op jit(solution)/shard_map/all_to_all | solution.py:121
  637.3 6.2 fusion.43
  643.5 2.0 fusion
  646.5 2.7 copy.65
  (71 shorter events, 14.3 us)
Async XLA Ops:
  8.5 33.9 %all-to-all-start = ((s32[1,8,4]{2,0,1:T(1,128)}), s32[1,8,4]{2,0,1:T(1,128)S(1)}, u32[]{:S(2)}, u32[]{:S(2)}) async-start(s32[1,8,4]{2,0,1:T(1,128)} %copy.22), calls=%async_computation | async-start | bytes 8192 | tf_op jit(solution)/shard_map/all_to_all | solution.py:108
  42.4 32.3 %all-to-all-start.1 = ((bf16[64,32,512]{2,0,1:T(8,128)(2,1)}), bf16[64,32,512]{2,0,1:T(8,128)(2,1)S(1)}, u32[]{:S(2)}, u32[]{:S(2)}) async-start(bf16[64,32,512]{2,0,1:T(8,128)(2,1)} %convert_bitcast_fusion.1), calls=%async_computation.1 | async-start | bytes 4194304 | tf_op jit(solution)/shard_map/all_to_all | solution.py:139
  48.4 111.9 %reduce-scatter.3.cloned.1.call-start = ((), (), s32[]{:S(2)}) async-start(), calls=%async_computation.8 | async-start | bytes 6684672 | tf_op jit(solution)/shard_map/reduce_scatter | solution.py:143
  82.8 143.3 %all-gather.4.cloned.1.call-start = ((), (), s32[]{:S(2)}) async-start(), calls=%async_computation.9 | async-start | bytes 3342336 | tf_op jit(solution)/shard_map/all_gather | solution.py:146
  179.9 229.1 %reduce-scatter.5.cloned.1.call-start = ((), (), s32[]{:S(2)}) async-start(), calls=%async_computation.10 | async-start | bytes 6684672 | tf_op jit(solution)/shard_map/reduce_scatter | solution.py:143
  180.0 50.4 %copy-start.6 = (pred[32]{0:T(512)(128)(4,1)}, pred[32]{0:T(512)(128)(4,1)S(1)}, u32[]{:S(2)}) copy-start(pred[32]{0:T(512)(128)(4,1)S(1)} %compare_and_fusion) | copy-start | bytes 100
  269.9 2.1 copy-start.1
  272.3 14.1 %copy-start.3 = (f32[64,2048]{1,0:T(8,128)}, f32[64,2048]{1,0:T(8,128)S(1)}, u32[]{:S(2)}) copy-start(f32[64,2048]{1,0:T(8,128)S(1)} %get-tuple-element.70) | copy-start | bytes 1572868
  331.4 77.7 %copy-start = (f32[64,1536]{1,0:T(8,128)S(1)}, f32[64,1536]{1,0:T(8,128)}, u32[]{:S(2)}) copy-start(f32[64,1536]{1,0:T(8,128)} %reduce-scatter.3.cloned.1.call-done) | copy-start | bytes 1179652
  331.4 143.6 %all-gather.6.cloned.1.call-start = ((), (), s32[]{:S(2)}) async-start(), calls=%async_computation.11 | async-start | bytes 3342336 | tf_op jit(solution)/shard_map/all_gather | solution.py:146
  427.0 48.0 %copy-start.8 = (f32[64]{0:T(128)}, f32[64]{0:T(128)S(1)}, u32[]{:S(2)}) copy-start(f32[64]{0:T(128)S(1)} %sqrt_bitcast_fusion) | copy-start | bytes 772
  482.5 31.6 %all-to-all-start.4 = ((bf16[64,32,512]{2,0,1:T(8,128)(2,1)}), bf16[64,32,512]{2,0,1:T(8,128)(2,1)S(1)}, u32[]{:S(2)}, u32[]{:S(2)}) async-start(bf16[64,32,512]{2,0,1:T(8,128)(2,1)} %select_bitcast_fusion.1), calls=%async_computation.6 | async-start | bytes 4194304 | tf_op jit(solution)/shard_map/all_to_all | solution.py:121
  487.7 110.7 %all-gather.8.cloned.1.call-start = ((), (), s32[]{:S(2)}) async-start(), calls=%async_computation.12 | async-start | bytes 6684672 | tf_op jit(solution)/shard_map/all_gather | solution.py:183
  520.1 2.2 copy-start.4
  520.1 2.2 copy-start.9
  520.1 16.9 %copy-start.5 = (f32[64,1536]{1,0:T(8,128)S(1)}, f32[64,1536]{1,0:T(8,128)}, u32[]{:S(2)}) copy-start(f32[64,1536]{1,0:T(8,128)} %reduce-scatter.5.cloned.1.call-done) | copy-start | bytes 1179652
  601.9 2.0 copy-start.7
  605.8 40.7 %slice-start = ((s8[6291456]{0:T(1024)(128)(4,1)}), s8[4194304]{0:T(1024)(128)(4,1)S(1)}, s32[]{:S(2)}) async-start(s8[6291456]{0:T(1024)(128)(4,1)} %bitcast.108), calls=%async_computation.13 | async-start | bytes 8388608
  637.3 9.2 %slice-start.1 = ((s8[6291456]{0:T(1024)(128)(4,1)}), s8[2097152]{0:T(1024)(128)(4,1)S(1)}, s32[]{:S(2)}) async-start(s8[6291456]{0:T(1024)(128)(4,1)} %bitcast.108), calls=%async_computation.14 | async-start | bytes 4194304
  643.5 2.1 copy-start.2
Sparse Core Ops, SparseCore 0:
  82.9 77.3 reduce-scatter.2
  180.1 46.0 all-gather.3
  331.5 77.4 reduce-scatter.4
  428.9 45.9 all-gather.5
  538.2 60.1 all-gather.7

commit v3 on v1

--- a/solution.py
+++ b/solution.py
@@ -18,14 +18,7 @@
 
 
 def stage_plan(mesh, axes):
-    plan = []
-    if "tile" in axes:
-        tiles = mesh.shape["tile"]
-        plan += [("tile", 2, 1), ("tile", tiles // 2, 2)]
-    if "ray" in axes:
-        rays = mesh.shape["ray"]
-        inner = 4 if rays % 4 == 0 else 1
-        plan += [("ray", inner, 1), ("ray", rays // inner, inner)]
+    plan = [(axis, mesh.shape[axis], 1) for axis in ("tile", "ray") if axis in axes]
     return tuple(stage for stage in plan if stage[1] > 1)
 
 

time: 581 us -> 578 us (level)
  no operation moved by 1% of the time
where the time goes in v3:
time: 578 us; the launch traced here: 577 us
  waiting for transfers between devices  291 us (50%)
  blocking collectives  93.4 us (16%)
  Pallas kernels  56.3 us (10%)
  other arithmetic  41.2 us (7%)
  matrix products  38.7 us (7%)
  local copies, waits for them, and re-layouts  27.4 us (5%)
  starting transfers between devices  15 us (3%)
  between operations  14.3 us (2%)
    psum x2, waiting for transfers between devices, adjoint(): total = lax.psum(owned, 'ray')  240 us
    all_to_all x2, blocking collectives, fetch(): lax.all_to_all(outgoing, 'tile', split_axis=1, concat_axis=1, tiled=True)  61.8 us
    pallas_call x5, Pallas kernels, group_sum(): pl.pallas_call(functools.partial(reduce_kernel, plan), out_shape=jax.Shap...  56.3 us
    all_to_all x1, blocking collectives, adjoint(): lax.all_to_all(terms, 'tile', split_axis=1, concat_axis=1, tiled=True)  31.5 us
    all_to_all x1, waiting for transfers between devices, fetch(): lax.all_to_all(outgoing, 'tile', split_axis=1, concat_axis=1, tiled=True)  25.6 us
    all_to_all x1, waiting for transfers between devices, adjoint(): lax.all_to_all(terms, 'tile', split_axis=1, concat_axis=1, tiled=True)  25.1 us
    dot_general x3, matrix products, forward(): jnp.einsum('cnk,nrk->ncr', tiles, sensitivity, preferred_element_type=jnp...  18.1 us
    unnamed x15, local copies, waits for them, and re-layouts  15.1 us
  transfers between devices with their start and end apart: 5, of which 4 were waited for; matrix products, arithmetic and copies ran while one was open for 2% of the time, Pallas kernels for 3%

profile of v3, /device:TPU:1, one launch (start us, length us, event | category | flops | bytes accessed | tf_op | source)
XLA Modules:
  0.0 577.0 jit_solution(2716750430350704385)
XLA Ops:
  7.2 1.3 copy.22
  8.5 6.0 %all-to-all-start = ((s32[1,8,4]{2,0,1:T(1,128)}), s32[1,8,4]{2,0,1:T(1,128)S(1)}, u32[]{:S(2)}, u32[]{:S(2)}) async-start(s32[1,8,4]{2,0,1:T(1,128)} %copy.22), calls=%async_computation | async-start | bytes 8192 | tf_op jit(solution)/shard_map/all_to_all | solution.py:101
  14.5 0.8 copy.23
  15.3 1.2 multiply_reduce_fusion.4
  17.1 16.2 %shard_map.59 = f32[8,128]{1,0:T(8,128)} custom-call(f32[8,128]{1,0:T(8,128)} %scatter.16.x_ref), custom_call_target="tpu_custom_call" | custom-call | tf_op jit(solution)/shard_map/pallas_call | solution.py:80
  34.0 1.1 fusion.19
  35.8 6.3 %convert_bitcast_fusion.1 = bf16[64,32,512]{2,0,1:T(8,128)(2,1)} fusion(bf16[32,256,512]{2,1,0:T(8,128)(2,1)} %param.19, bf16[32,64,256]{2,1,0:T(8,128)(2,1)S(1)} %gather_fusion, pred[32]{0:T(512)(128)(4,1)S(1)} %compare_and_fusion.1), kind=kOutput, calls=%fused_computation.28 | convolution fusion | flops 538443776 | bytes 11534368 | tf_op jit(solution)/shard_map/cnr,nrk->cnk/dot_general | solution.py:129
  42.1 4.9 all-to-all-start.1
  48.3 25.1 %all-to-all-done.1 = bf16[64,32,512]{2,0,1:T(8,128)(2,1)S(1)} async-done(((bf16[64,32,512]{2,0,1:T(8,128)(2,1)}), bf16[64,32,512]{2,0,1:T(8,128)(2,1)S(1)}, u32[]{:S(2)}, u32[]{:S(2)}) %all-to-all-start.1) | async-done | bytes 2097184 | tf_op jit(solution)/shard_map/all_to_all | solution.py:132
  73.4 1.7 fusion.8
  75.1 6.3 %copy.39 = f32[8,8,48,512]{3,1,2,0:T(8,128)} copy(f32[8,8,48,512]{3,2,1,0:T(8,128)S(1)} %bitcast.111) | data formatting | bytes 12582912
  81.5 120.1 %all-reduce.8.cloned.1.call-done = f32[64,24576]{1,0:T(8,128)} async-done(((f32[64,24576]{1,0:T(8,128)}), f32[64,24576]{1,0:T(8,128)}) %all-reduce.8.cloned.1.call-update) | async-done | bytes 6291472 | tf_op jit(solution)/shard_map/psum | solution.py:136
  201.6 3.3 multiply_reduce_fusion.1
  205.5 7.5 %shard_map.60 = f32[8,128]{1,0:T(8,128)} custom-call(f32[8,128]{1,0:T(8,128)} %scatter.19.x_ref), custom_call_target="tpu_custom_call" | custom-call | tf_op jit(solution)/shard_map/pallas_call | solution.py:80
  213.7 3.2 fusion.38
  217.3 2.0 gather_fusion.1
  219.4 1.8 select_bitcast_fusion.2
  221.2 30.4 %all_to_all.30 = bf16[64,32,512]{2,0,1:T(8,128)(2,1)S(1)} all-to-all(bf16[64,32,512]{2,0,1:T(8,128)(2,1)S(1)} %select_bitcast_fusion.2), channel_id=1, replica_groups=mesh['ray'=16,'tile'=8] {'tile'}, dimensions={1} | all-to-all | bytes 4194304 | tf_op jit(solution)/shard_map/all_to_all | solution.py:114
  251.6 6.0 %fusion.42 = f32[32,64,256]{2,1,0:T(8,128)S(1)} fusion(bf16[64,32,512]{2,0,1:T(8,128)(2,1)S(1)} %all_to_all.30, bf16[32,256,512]{2,1,0:T(8,128)(2,1)} %param.19), kind=kOutput, calls=%fused_computation.79 | convolution fusion | flops 536870912 | bytes 12582912 | tf_op jit(solution)/shard_map/cnk,nrk->ncr/dot_general | solution.py:119
  257.6 2.0 fusion.6
  260.7 12.6 %shard_map.61 = f32[8,128]{1,0:T(8,128)} custom-call(f32[8,128]{1,0:T(8,128)} %scatter.20.x_ref), custom_call_target="tpu_custom_call" | custom-call | tf_op jit(solution)/shard_map/pallas_call | solution.py:80
  273.3 0.7 sqrt_bitcast_fusion.1
  274.8 5.0 convert_bitcast_fusion
  279.8 31.5 %all_to_all.31 = bf16[64,32,512]{2,0,1:T(8,128)(2,1)S(1)} all-to-all(bf16[64,32,512]{2,0,1:T(8,128)(2,1)S(1)} %convert_bitcast_fusion), channel_id=1, replica_groups=mesh['ray'=16,'tile'=8] {'tile'}, dimensions={1} | all-to-all | bytes 4194304 | tf_op jit(solution)/shard_map/all_to_all | solution.py:132
  311.3 1.7 fusion.4
  313.1 6.3 %copy.41 = f32[8,8,48,512]{3,1,2,0:T(8,128)} copy(f32[8,8,48,512]{3,2,1,0:T(8,128)S(1)} %bitcast.110) | data formatting | bytes 12582912
  319.3 119.8 %all-reduce.10.cloned.1.call-done = f32[64,24576]{1,0:T(8,128)} async-done(((f32[64,24576]{1,0:T(8,128)}), f32[64,24576]{1,0:T(8,128)}) %all-reduce.10.cloned.1.call-update) | async-done | bytes 6291472 | tf_op jit(solution)/shard_map/psum | solution.py:136
  439.2 5.8 %multiply_reduce_fusion = f32[64]{0:T(128)S(1)} fusion(f32[64,24576]{1,0:T(8,128)} %all-reduce.10.cloned.1.call-done, f32[64]{0:T(128)S(1)} %sqrt_bitcast_fusion.1, f32[64,24576]{1,0:T(8,128)} %all-reduce.8.cloned.1.call-done, f32[64]{0:T(128)S(1)} %sqrt_bitcast_fusion.2), kind=kLoop, calls=%fused_computation.6 | loop fusion | flops 7864256 | bytes 12583680 | tf_op jit(solution)/shard_map/reduce_sum | solution.py:140
  445.6 7.5 %shard_map.62 = f32[8,128]{1,0:T(8,128)} custom-call(f32[8,128]{1,0:T(8,128)} %scatter.21.x_ref), custom_call_target="tpu_custom_call" | custom-call | tf_op jit(solution)/shard_map/pallas_call | solution.py:80
  453.0 0.7 sqrt_bitcast_fusion
  453.7 5.2 fusion.10
  459.4 2.0 gather_fusion.3
  461.4 3.2 select_bitcast_fusion.1
  464.6 4.1 all-to-all-start.4
  468.7 0.7 multiply_divide_fusion.2
  469.4 25.6 %all-to-all-done.4 = bf16[64,32,512]{2,0,1:T(8,128)(2,1)S(1)} async-done(((bf16[64,32,512]{2,0,1:T(8,128)(2,1)}), bf16[64,32,512]{2,0,1:T(8,128)(2,1)S(1)}, u32[]{:S(2)}, u32[]{:S(2)}) %all-to-all-start.4) | async-done | bytes 2097184 | tf_op jit(solution)/shard_map/all_to_all | solution.py:114
  495.0 6.0 %fusion.43 = f32[32,64,256]{2,1,0:T(8,128)S(1)} fusion(bf16[64,32,512]{2,0,1:T(8,128)(2,1)S(1)} %all-to-all-done.4, bf16[32,256,512]{2,1,0:T(8,128)(2,1)} %param.19), kind=kOutput, calls=%fused_computation.80 | convolution fusion | flops 536870912 | bytes 12582912 | tf_op jit(solution)/shard_map/cnk,nrk->ncr/dot_general | solution.py:119
  501.0 2.0 fusion.2
  504.0 12.5 %shard_map.63 = f32[8,128]{1,0:T(8,128)} custom-call(f32[8,128]{1,0:T(8,128)} %scatter.24.x_ref), custom_call_target="tpu_custom_call" | custom-call | tf_op jit(solution)/shard_map/pallas_call | solution.py:80
  516.5 0.7 multiply_divide_fusion.1
  517.3 0.7 multiply_divide_fusion
  518.0 7.4 %fusion.39 = (bf16[64,24576]{1,0:T(8,128)(2,1)S(1)}, f32[64,24576]{1,0:T(8,128)}) fusion(f32[64]{0:T(128)S(1)} %multiply_divide_fusion, f32[64]{0:T(128)S(1)} %sqrt_bitcast_fusion, f32[64,24576]{1,0:T(8,128)} %all-reduce.10.cloned.1.call-done, f32[64]{0:T(128)S(1)} %sqrt_bitcast_fusion.1, f32[64]{0:T(128)S(1)} %get-tuple-element.69, ...), kind=kLoop, calls=%fused_computation.78 | loop fusion | flops 15728640 | bytes 22021632 | tf_op jit(solution)/shard_map/convert_element_type | solution.py:175
  525.7 2.0 gather_fusion.4
  527.8 1.8 select_bitcast_fusion
  529.6 31.5 %all_to_all.32 = bf16[64,32,512]{2,0,1:T(8,128)(2,1)S(1)} all-to-all(bf16[64,32,512]{2,0,1:T(8,128)(2,1)S(1)} %select_bitcast_fusion), channel_id=1, replica_groups=mesh['ray'=16,'tile'=8] {'tile'}, dimensions={1} | all-to-all | bytes 4194304 | tf_op jit(solution)/shard_map/all_to_all | solution.py:114
  561.1 6.0 %fusion.44 = f32[32,64,256]{2,1,0:T(8,128)S(1)} fusion(bf16[64,32,512]{2,0,1:T(8,128)(2,1)S(1)} %all_to_all.32, bf16[32,256,512]{2,1,0:T(8,128)(2,1)} %param.19), kind=kOutput, calls=%fused_computation.81 | convolution fusion | flops 536870912 | bytes 12582912 | tf_op jit(solution)/shard_map/cnk,nrk->ncr/dot_general | solution.py:119
  567.1 2.0 fusion
  569.3 0.9 sub.19
  (43 shorter events, 9.5 us)
Async XLA Ops:
  8.5 33.6 %all-to-all-start = ((s32[1,8,4]{2,0,1:T(1,128)}), s32[1,8,4]{2,0,1:T(1,128)S(1)}, u32[]{:S(2)}, u32[]{:S(2)}) async-start(s32[1,8,4]{2,0,1:T(1,128)} %copy.22), calls=%async_computation | async-start | bytes 8192 | tf_op jit(solution)/shard_map/all_to_all | solution.py:101
  42.1 31.2 %all-to-all-start.1 = ((bf16[64,32,512]{2,0,1:T(8,128)(2,1)}), bf16[64,32,512]{2,0,1:T(8,128)(2,1)S(1)}, u32[]{:S(2)}, u32[]{:S(2)}) async-start(bf16[64,32,512]{2,0,1:T(8,128)(2,1)} %convert_bitcast_fusion.1), calls=%async_computation.1 | async-start | bytes 4194304 | tf_op jit(solution)/shard_map/all_to_all | solution.py:132
  47.0 154.6 %all-reduce.8.cloned.1.call-start = ((), (), s32[]{:S(2)}) async-start(), calls=%async_computation.6 | async-start | bytes 12582912 | tf_op jit(solution)/shard_map/psum | solution.py:136
  81.4 357.8 %all-reduce.10.cloned.1.call-start = ((), (), s32[]{:S(2)}) async-start(), calls=%async_computation.7 | async-start | bytes 12582912 | tf_op jit(solution)/shard_map/psum | solution.py:136
  257.6 2.1 copy-start
  260.0 14.1 %copy-start.2 = (f32[64,2048]{1,0:T(8,128)}, f32[64,2048]{1,0:T(8,128)S(1)}, u32[]{:S(2)}) copy-start(f32[64,2048]{1,0:T(8,128)S(1)} %get-tuple-element.72) | copy-start | bytes 1572868
  464.6 30.4 %all-to-all-start.4 = ((bf16[64,32,512]{2,0,1:T(8,128)(2,1)}), bf16[64,32,512]{2,0,1:T(8,128)(2,1)S(1)}, u32[]{:S(2)}, u32[]{:S(2)}) async-start(bf16[64,32,512]{2,0,1:T(8,128)(2,1)} %select_bitcast_fusion.1), calls=%async_computation.4 | async-start | bytes 4194304 | tf_op jit(solution)/shard_map/all_to_all | solution.py:114
  501.0 2.1 copy-start.3
  567.1 2.1 copy-start.1
Sparse Core Ops, SparseCore 0:
  81.5 120.0 all-reduce.7
  319.5 119.6 all-reduce.9

commit v4 on v3

--- a/solution.py
+++ b/solution.py
@@ -92,6 +92,143 @@
     return out[0, :width]
 
 
+def ray_axes(mesh):
+    rays = mesh.shape["ray"]
+    inner = 4 if rays % 4 == 0 else rays
+    return ((inner, 1), (rays // inner, inner))
+
+
+def allreduce_kernel(axes, x_ref, o_ref, recv1, recv2, part, send_sems, recv_sems):
+    me = lax.axis_index("ray")
+    tile = lax.axis_index("tile")
+    rows = x_ref.shape[0]
+    half = x_ref.shape[1] // 2
+    w1 = half // axes[0][0]
+    w2 = w1 // axes[1][0]
+
+    def pos(axis):
+        size, stride = axis
+        return (me // stride) % size
+
+    def peer(axis, k):
+        size, stride = axis
+        p = pos(axis)
+        return (me + (((p - k + size) % size) - p) * stride, tile)
+
+    def cols(start, width):
+        return pl.ds(pl.multiple_of(start, 128), width)
+
+    def add_rows(dst, srcs):
+        def body(r, carry):
+            block = pl.ds(pl.multiple_of(r * 8, 8), 8)
+            total = srcs[0][block, :]
+            for ref in srcs[1:]:
+                total = total + ref[block, :]
+            dst[block, :] = total
+            return carry
+        lax.fori_loop(0, rows // 8, body, 0)
+
+    barrier = pltpu.get_barrier_semaphore()
+    greeted = 0
+    for axis in axes:
+        for k in range(1, axis[0]):
+            pl.semaphore_signal(barrier, inc=1, device_id=peer(axis, k), device_id_type=MESH)
+            greeted += 1
+    pl.semaphore_wait(barrier, greeted)
+
+    plans = [(axes[0], axes[1]), (axes[1], axes[0])]
+    sends = []
+
+    def exchange(stage, h, axis, src_of, dst_of, landing_of):
+        out = []
+        for k in range(1, axis[0]):
+            copy = pltpu.make_async_remote_copy(
+                src_ref=src_of(k), dst_ref=dst_of(k),
+                send_sem=send_sems.at[stage, h, k], recv_sem=recv_sems.at[stage, h, k],
+                device_id=peer(axis, k), device_id_type=MESH)
+            copy.start()
+            sends.append(copy)
+            out.append(pltpu.make_async_remote_copy(
+                src_ref=src_of(k), dst_ref=landing_of(k),
+                send_sem=send_sems.at[stage, h, k], recv_sem=recv_sems.at[stage, h, k],
+                device_id=peer(axis, k), device_id_type=MESH))
+        return out
+
+    waits = []
+    for h, (a1, a2) in enumerate(plans):
+        n1, p1 = a1[0], pos(a1)
+        recv1[h, 0] = x_ref[:, cols(h * half + p1 * w1, w1)]
+        waits += exchange(
+            0, h, a1,
+            lambda k, h=h, n1=n1, p1=p1: x_ref.at[:, cols(h * half + ((p1 - k + n1) % n1) * w1, w1)],
+            lambda k, h=h: recv1.at[h, k],
+            lambda k, h=h: recv1.at[h, k])
+    for copy in waits:
+        copy.wait_recv()
+    waits = []
+    for h, (a1, a2) in enumerate(plans):
+        n1, p1 = a1[0], pos(a1)
+        n2, p2 = a2[0], pos(a2)
+        add_rows(part.at[h], [recv1.at[h, (q - p1 + n1) % n1] for q in range(n1)])
+        recv2[h, 0] = part[h, :, cols(p2 * w2, w2)]
+        waits += exchange(
+            1, h, a2,
+            lambda k, h=h, n2=n2, p2=p2: part.at[h, :, cols(((p2 - k + n2) % n2) * w2, w2)],
+            lambda k, h=h: recv2.at[h, k],
+            lambda k, h=h: recv2.at[h, k])
+    for copy in waits:
+        copy.wait_recv()
+    waits = []
+    for h, (a1, a2) in enumerate(plans):
+        n1, p1 = a1[0], pos(a1)
+        n2, p2 = a2[0], pos(a2)
+        base = h * half + p1 * w1
+        add_rows(o_ref.at[:, cols(base + p2 * w2, w2)], [recv2.at[h, (q - p2 + n2) % n2] for q in range(n2)])
+        waits += exchange(
+            2, h, a2,
+            lambda k, base=base, p2=p2: o_ref.at[:, cols(base + p2 * w2, w2)],
+            lambda k, base=base, p2=p2: o_ref.at[:, cols(base + p2 * w2, w2)],
+            lambda k, base=base, n2=n2, p2=p2: o_ref.at[:, cols(base + ((p2 + k) % n2) * w2, w2)])
+    for copy in waits:
+        copy.wait_recv()
+    waits = []
+    for h, (a1, a2) in enumerate(plans):
+        n1, p1 = a1[0], pos(a1)
+        waits += exchange(
+            3, h, a1,
+            lambda k, h=h, p1=p1: o_ref.at[:, cols(h * half + p1 * w1, w1)],
+            lambda k, h=h, p1=p1: o_ref.at[:, cols(h * half + p1 * w1, w1)],
+            lambda k, h=h, n1=n1, p1=p1: o_ref.at[:, cols(h * half + ((p1 + k) % n1) * w1, w1)])
+    for copy in waits:
+        copy.wait_recv()
+    for copy in sends:
+        copy.wait_send()
+
+
+def ray_allreduce(mesh, owned):
+    axes = ray_axes(mesh)
+    rows, width = owned.shape
+    half = width // 2
+    w1 = half // axes[0][0]
+    w2 = w1 // axes[1][0]
+    depth = max(axes[0][0], axes[1][0])
+    return pl.pallas_call(
+        functools.partial(allreduce_kernel, axes),
+        out_shape=jax.ShapeDtypeStruct((rows, width), jnp.float32),
+        in_specs=[pl.BlockSpec(memory_space=pltpu.VMEM)],
+        out_specs=pl.BlockSpec(memory_space=pltpu.VMEM),
+        scratch_shapes=[
+            pltpu.VMEM((2, depth, rows, w1), jnp.float32),
+            pltpu.VMEM((2, depth, rows, w2), jnp.float32),
+            pltpu.VMEM((2, rows, w1), jnp.float32),
+            pltpu.SemaphoreType.DMA((4, 2, depth)),
+            pltpu.SemaphoreType.DMA((4, 2, depth)),
+        ],
+        compiler_params=pltpu.CompilerParams(
+            collective_id=2, has_side_effects=True, vmem_limit_bytes=60 * 1024 * 1024),
+    )(owned)
+
+
 eps_norm = 1e-06
 
 
@@ -133,7 +270,7 @@
         owned = jnp.einsum(
             "cnk,nt->ctk", arrived, owner_onehot, preferred_element_type=jnp.float32
         ).reshape(columns, TILE_DEV * CB)
-        total = lax.psum(owned, "ray")
+        total = ray_allreduce(mesh, owned)
         return total
 
     def cell_norm(field):

time: 578 us -> 524 us (0.907)
  waiting for transfers between devices: 291 us -> 50.7 us
  Pallas kernels: 56.3 us -> 256 us
  between operations: 14.3 us -> 0.96 us
    psum x2 -> x0, waiting for transfers between devices: 240 us -> none  [adjoint(): total = lax.psum(owned, 'ray')]
    pallas_call x0 -> x2, Pallas kernels: none -> 201 us  [ray_allreduce(): pl.pallas_call(functools.partial(allreduce_kernel, axes), out_shape=jax.S...]
  transfers between devices with their start and end apart: 5 -> 3, of which waited for: 4 -> 2; matrix products, arithmetic and copies ran while one was open for 2% -> 3% of each run, Pallas kernels for 3% -> 3%
where the time goes in v4:
time: 524 us; the launch traced here: 523 us
  Pallas kernels  256 us (49%)
  blocking collectives  92.7 us (18%)
  waiting for transfers between devices  50.7 us (10%)
  other arithmetic  41.2 us (8%)
  matrix products  38.7 us (7%)
  local copies, waits for them, and re-layouts  27.4 us (5%)
  starting transfers between devices  15.1 us (3%)
    pallas_call x2, Pallas kernels, ray_allreduce(): pl.pallas_call(functools.partial(allreduce_kernel, axes), out_shape=jax.S...  201 us
    all_to_all x2, blocking collectives, fetch(): lax.all_to_all(outgoing, 'tile', split_axis=1, concat_axis=1, tiled=True)  61.2 us
    pallas_call x5, Pallas kernels, group_sum(): pl.pallas_call(functools.partial(reduce_kernel, plan), out_shape=jax.Shap...  54.6 us
    all_to_all x1, blocking collectives, adjoint(): lax.all_to_all(terms, 'tile', split_axis=1, concat_axis=1, tiled=True)  31.5 us
    all_to_all x1, waiting for transfers between devices, fetch(): lax.all_to_all(outgoing, 'tile', split_axis=1, concat_axis=1, tiled=True)  25.6 us
    all_to_all x1, waiting for transfers between devices, adjoint(): lax.all_to_all(terms, 'tile', split_axis=1, concat_axis=1, tiled=True)  25.1 us
    dot_general x3, matrix products, forward(): jnp.einsum('cnk,nrk->ncr', tiles, sensitivity, preferred_element_type=jnp...  18.1 us
    unnamed x15, local copies, waits for them, and re-layouts  15.1 us
  transfers between devices with their start and end apart: 3, of which 2 were waited for; matrix products, arithmetic and copies ran while one was open for 3% of the time, Pallas kernels for 3%

profile of v4, /device:TPU:1, one launch (start us, length us, event | category | flops | bytes accessed | tf_op | source)
XLA Modules:
  0.0 522.7 jit_solution(5359515020255937831)
XLA Ops:
  0.6 1.3 copy.25
  2.0 6.0 %all-to-all-start = ((s32[1,8,4]{2,0,1:T(1,128)}), s32[1,8,4]{2,0,1:T(1,128)S(1)}, u32[]{:S(2)}, u32[]{:S(2)}) async-start(s32[1,8,4]{2,0,1:T(1,128)} %copy.25), calls=%async_computation | async-start | bytes 8192 | tf_op jit(solution)/shard_map/all_to_all | solution.py:238
  7.9 0.8 copy.26
  8.8 1.2 multiply_reduce_fusion.4
  10.6 16.2 %shard_map.59 = f32[8,128]{1,0:T(8,128)} custom-call(f32[8,128]{1,0:T(8,128)} %scatter.16.x_ref), custom_call_target="tpu_custom_call" | custom-call | tf_op jit(solution)/shard_map/pallas_call | solution.py:80
  27.5 1.1 fusion.19
  29.3 6.3 %convert_bitcast_fusion.1 = bf16[64,32,512]{2,0,1:T(8,128)(2,1)} fusion(bf16[32,256,512]{2,1,0:T(8,128)(2,1)} %param.19, bf16[32,64,256]{2,1,0:T(8,128)(2,1)S(1)} %gather_fusion, pred[32]{0:T(512)(128)(4,1)S(1)} %compare_and_fusion.1), kind=kOutput, calls=%fused_computation.28 | convolution fusion | flops 538443776 | bytes 11534368 | tf_op jit(solution)/shard_map/cnr,nrk->cnk/dot_general | solution.py:266
  35.6 4.9 all-to-all-start.1
  41.8 25.1 %all-to-all-done.1 = bf16[64,32,512]{2,0,1:T(8,128)(2,1)S(1)} async-done(((bf16[64,32,512]{2,0,1:T(8,128)(2,1)}), bf16[64,32,512]{2,0,1:T(8,128)(2,1)S(1)}, u32[]{:S(2)}, u32[]{:S(2)}) %all-to-all-start.1) | async-done | bytes 2097184 | tf_op jit(solution)/shard_map/all_to_all | solution.py:269
  66.8 1.7 fusion.8
  68.6 6.3 %copy.42 = f32[8,8,48,512]{3,1,2,0:T(8,128)} copy(f32[8,8,48,512]{3,2,1,0:T(8,128)S(1)} %bitcast.109) | data formatting | bytes 12582912
  74.8 100.9 %shard_map.60 = f32[64,24576]{1,0:T(8,128)} custom-call(f32[64,24576]{1,0:T(8,128)} %bitcast.110), custom_call_target="tpu_custom_call" | custom-call | tf_op jit(solution)/shard_map/pallas_call | solution.py:215
  175.8 3.3 multiply_reduce_fusion.1
  179.7 6.4 %shard_map.61 = f32[8,128]{1,0:T(8,128)} custom-call(f32[8,128]{1,0:T(8,128)} %scatter.19.x_ref), custom_call_target="tpu_custom_call" | custom-call | tf_op jit(solution)/shard_map/pallas_call | solution.py:80
  186.7 3.2 fusion.38
  190.4 2.0 gather_fusion.1
  192.4 1.8 select_bitcast_fusion.2
  194.2 29.6 %all_to_all.30 = bf16[64,32,512]{2,0,1:T(8,128)(2,1)S(1)} all-to-all(bf16[64,32,512]{2,0,1:T(8,128)(2,1)S(1)} %select_bitcast_fusion.2), channel_id=1, replica_groups=mesh['ray'=16,'tile'=8] {'tile'}, dimensions={1} | all-to-all | bytes 4194304 | tf_op jit(solution)/shard_map/all_to_all | solution.py:251
  223.9 6.0 %fusion.42 = f32[32,64,256]{2,1,0:T(8,128)S(1)} fusion(bf16[64,32,512]{2,0,1:T(8,128)(2,1)S(1)} %all_to_all.30, bf16[32,256,512]{2,1,0:T(8,128)(2,1)} %param.19), kind=kOutput, calls=%fused_computation.79 | convolution fusion | flops 536870912 | bytes 12582912 | tf_op jit(solution)/shard_map/cnk,nrk->ncr/dot_general | solution.py:256
  229.9 2.0 fusion.6
  233.0 13.0 %shard_map.62 = f32[8,128]{1,0:T(8,128)} custom-call(f32[8,128]{1,0:T(8,128)} %scatter.20.x_ref), custom_call_target="tpu_custom_call" | custom-call | tf_op jit(solution)/shard_map/pallas_call | solution.py:80
  246.0 0.7 sqrt_bitcast_fusion.1
  247.5 5.0 convert_bitcast_fusion
  252.5 31.5 %all_to_all.31 = bf16[64,32,512]{2,0,1:T(8,128)(2,1)S(1)} all-to-all(bf16[64,32,512]{2,0,1:T(8,128)(2,1)S(1)} %convert_bitcast_fusion), channel_id=1, replica_groups=mesh['ray'=16,'tile'=8] {'tile'}, dimensions={1} | all-to-all | bytes 4194304 | tf_op jit(solution)/shard_map/all_to_all | solution.py:269
  284.0 1.7 fusion.4
  285.8 6.3 %copy.44 = f32[8,8,48,512]{3,1,2,0:T(8,128)} copy(f32[8,8,48,512]{3,2,1,0:T(8,128)S(1)} %bitcast.108) | data formatting | bytes 12582912
  292.0 100.4 %shard_map.63 = f32[64,24576]{1,0:T(8,128)} custom-call(f32[64,24576]{1,0:T(8,128)} %bitcast.111), custom_call_target="tpu_custom_call" | custom-call | tf_op jit(solution)/shard_map/pallas_call | solution.py:215
  392.5 5.8 %multiply_reduce_fusion = f32[64]{0:T(128)S(1)} fusion(f32[64,24576]{1,0:T(8,128)} %shard_map.63, f32[64]{0:T(128)S(1)} %sqrt_bitcast_fusion.1, f32[64,24576]{1,0:T(8,128)} %shard_map.60, f32[64]{0:T(128)S(1)} %sqrt_bitcast_fusion.2), kind=kLoop, calls=%fused_computation.6 | loop fusion | flops 7864256 | bytes 12583680 | tf_op jit(solution)/shard_map/reduce_sum | solution.py:277
  398.9 6.4 %shard_map.64 = f32[8,128]{1,0:T(8,128)} custom-call(f32[8,128]{1,0:T(8,128)} %scatter.21.x_ref), custom_call_target="tpu_custom_call" | custom-call | tf_op jit(solution)/shard_map/pallas_call | solution.py:80
  405.2 0.7 sqrt_bitcast_fusion
  405.9 5.2 fusion.10
  411.6 2.0 gather_fusion.3
  413.6 3.2 select_bitcast_fusion.1
  416.8 4.2 all-to-all-start.4
  421.0 0.7 multiply_divide_fusion.2
  421.7 25.6 %all-to-all-done.4 = bf16[64,32,512]{2,0,1:T(8,128)(2,1)S(1)} async-done(((bf16[64,32,512]{2,0,1:T(8,128)(2,1)}), bf16[64,32,512]{2,0,1:T(8,128)(2,1)S(1)}, u32[]{:S(2)}, u32[]{:S(2)}) %all-to-all-start.4) | async-done | bytes 2097184 | tf_op jit(solution)/shard_map/all_to_all | solution.py:251
  447.4 6.0 %fusion.43 = f32[32,64,256]{2,1,0:T(8,128)S(1)} fusion(bf16[64,32,512]{2,0,1:T(8,128)(2,1)S(1)} %all-to-all-done.4, bf16[32,256,512]{2,1,0:T(8,128)(2,1)} %param.19), kind=kOutput, calls=%fused_computation.80 | convolution fusion | flops 536870912 | bytes 12582912 | tf_op jit(solution)/shard_map/cnk,nrk->ncr/dot_general | solution.py:256
  453.4 2.0 fusion.2
  456.4 12.7 %shard_map.65 = f32[8,128]{1,0:T(8,128)} custom-call(f32[8,128]{1,0:T(8,128)} %scatter.24.x_ref), custom_call_target="tpu_custom_call" | custom-call | tf_op jit(solution)/shard_map/pallas_call | solution.py:80
  469.0 0.7 multiply_divide_fusion.1
  469.8 0.7 multiply_divide_fusion
  470.5 7.4 %fusion.39 = (bf16[64,24576]{1,0:T(8,128)(2,1)S(1)}, f32[64,24576]{1,0:T(8,128)}) fusion(f32[64]{0:T(128)S(1)} %multiply_divide_fusion, f32[64]{0:T(128)S(1)} %sqrt_bitcast_fusion, f32[64,24576]{1,0:T(8,128)} %shard_map.63, f32[64]{0:T(128)S(1)} %sqrt_bitcast_fusion.1, f32[64]{0:T(128)S(1)} %get-tuple-element.69, f32[64,24576]{1,0:T(8,128)} %shard_map.60, ...), kind=kLoop, calls=%fused_computation.78 | loop fusion | flops 15728640 | bytes 22021632 | tf_op jit(solution)/shard_map/convert_element_type | solution.py:312
  478.2 2.0 gather_fusion.4
  480.3 1.8 select_bitcast_fusion
  482.1 31.5 %all_to_all.32 = bf16[64,32,512]{2,0,1:T(8,128)(2,1)S(1)} all-to-all(bf16[64,32,512]{2,0,1:T(8,128)(2,1)S(1)} %select_bitcast_fusion), channel_id=1, replica_groups=mesh['ray'=16,'tile'=8] {'tile'}, dimensions={1} | all-to-all | bytes 4194304 | tf_op jit(solution)/shard_map/all_to_all | solution.py:251
  513.6 6.0 %fusion.44 = f32[32,64,256]{2,1,0:T(8,128)S(1)} fusion(bf16[64,32,512]{2,0,1:T(8,128)(2,1)S(1)} %all_to_all.32, bf16[32,256,512]{2,1,0:T(8,128)(2,1)} %param.19), kind=kOutput, calls=%fused_computation.81 | convolution fusion | flops 536870912 | bytes 12582912 | tf_op jit(solution)/shard_map/cnk,nrk->ncr/dot_general | solution.py:256
  519.7 2.0 fusion
  521.8 0.9 sub.19
  (39 shorter events, 9.4 us)
Async XLA Ops:
  2.0 33.6 %all-to-all-start = ((s32[1,8,4]{2,0,1:T(1,128)}), s32[1,8,4]{2,0,1:T(1,128)S(1)}, u32[]{:S(2)}, u32[]{:S(2)}) async-start(s32[1,8,4]{2,0,1:T(1,128)} %copy.25), calls=%async_computation | async-start | bytes 8192 | tf_op jit(solution)/shard_map/all_to_all | solution.py:238
  35.6 31.2 %all-to-all-start.1 = ((bf16[64,32,512]{2,0,1:T(8,128)(2,1)}), bf16[64,32,512]{2,0,1:T(8,128)(2,1)S(1)}, u32[]{:S(2)}, u32[]{:S(2)}) async-start(bf16[64,32,512]{2,0,1:T(8,128)(2,1)} %convert_bitcast_fusion.1), calls=%async_computation.1 | async-start | bytes 4194304 | tf_op jit(solution)/shard_map/all_to_all | solution.py:269
  229.9 2.1 copy-start
  232.3 14.5 %copy-start.2 = (f32[64,2048]{1,0:T(8,128)}, f32[64,2048]{1,0:T(8,128)S(1)}, u32[]{:S(2)}) copy-start(f32[64,2048]{1,0:T(8,128)S(1)} %get-tuple-element.72) | copy-start | bytes 1572868
  416.8 30.6 %all-to-all-start.4 = ((bf16[64,32,512]{2,0,1:T(8,128)(2,1)}), bf16[64,32,512]{2,0,1:T(8,128)(2,1)S(1)}, u32[]{:S(2)}, u32[]{:S(2)}) async-start(bf16[64,32,512]{2,0,1:T(8,128)(2,1)} %select_bitcast_fusion.1), calls=%async_computation.4 | async-start | bytes 4194304 | tf_op jit(solution)/shard_map/all_to_all | solution.py:251
  453.4 2.1 copy-start.3
  519.7 2.1 copy-start.1

commit v5 on v3

--- a/solution.py
+++ b/solution.py
@@ -92,6 +92,141 @@
     return out[0, :width]
 
 
+def ray_axes(mesh):
+    rays = mesh.shape["ray"]
+    inner = 4 if rays % 4 == 0 else rays
+    return ((inner, 1), (rays // inner, inner))
+
+
+def allreduce_kernel(axes, x_ref, o_ref, part, rbuf1, acc1, rbuf2, acc2, send_sems, recv_sems):
+    me = lax.axis_index("ray")
+    tile = lax.axis_index("tile")
+    rows = x_ref.shape[0]
+    half = x_ref.shape[1] // 2
+    w1 = half // axes[0][0]
+    w2 = w1 // axes[1][0]
+
+    def pos(axis):
+        size, stride = axis
+        return (me // stride) % size
+
+    def peer(axis, k):
+        size, stride = axis
+        p = pos(axis)
+        return (me + (((p - k + size) % size) - p) * stride, tile)
+
+    def cols(start, width):
+        return pl.ds(pl.multiple_of(start, 128), width)
+
+    def add_rows(dst, a, b):
+        def body(r, carry):
+            block = pl.ds(pl.multiple_of(r * 8, 8), 8)
+            dst[block, :] = a[block, :] + b[block, :]
+            return carry
+        lax.fori_loop(0, rows // 8, body, 0)
+
+    barrier = pltpu.get_barrier_semaphore()
+    greeted = 0
+    for axis in axes:
+        for k in (1, axis[0] - 1) if axis[0] > 2 else (1,):
+            pl.semaphore_signal(barrier, inc=1, device_id=peer(axis, k), device_id_type=MESH)
+            greeted += 1
+    pl.semaphore_wait(barrier, greeted)
+
+    plans = [(axes[0], axes[1]), (axes[1], axes[0])]
+    sends = []
+
+    def send(stage, h, d, s, axis, src, dst, landing):
+        size = axis[0]
+        k = size - 1 if d == 0 else 1
+        sems = dict(send_sem=send_sems.at[stage, h, d, s], recv_sem=recv_sems.at[stage, h, d, s],
+                    device_id=peer(axis, k), device_id_type=MESH)
+        copy = pltpu.make_async_remote_copy(src_ref=src, dst_ref=dst, **sems)
+        copy.start()
+        sends.append(copy)
+        return pltpu.make_async_remote_copy(src_ref=src, dst_ref=landing, **sems)
+
+    def reduce_scatter(stage, segs, rbuf, acc):
+        steps = segs[0][0][0] - 1
+        for s in range(steps):
+            waits = []
+            for h, (axis, own, final) in enumerate(segs):
+                size, p = axis[0], pos(axis)
+                for d in range(2):
+                    sign = 1 if d == 0 else -1
+                    src = own((p - sign * (s + 1) + 2 * size) % size, d) if s == 0 else acc.at[h, d, s - 1]
+                    waits.append((h, d, send(stage, h, d, s, axis, src, rbuf.at[h, d, s], rbuf.at[h, d, s])))
+            for h, d, copy in waits:
+                copy.wait_recv()
+            for h, (axis, own, final) in enumerate(segs):
+                size, p = axis[0], pos(axis)
+                for d in range(2):
+                    sign = 1 if d == 0 else -1
+                    mine = own((p - sign * (s + 2) + 2 * size) % size, d)
+                    dst = final(d) if s == steps - 1 else acc.at[h, d, s]
+                    add_rows(dst, rbuf.at[h, d, s], mine)
+
+    def all_gather(stage, segs):
+        steps = segs[0][0][0] - 1
+        for s in range(steps):
+            waits = []
+            for h, (axis, region) in enumerate(segs):
+                size, p = axis[0], pos(axis)
+                for d in range(2):
+                    sign = 1 if d == 0 else -1
+                    src = region((p - sign * s + 2 * size) % size, d)
+                    landing = region((p - sign * (s + 1) + 2 * size) % size, d)
+                    waits.append(send(stage, h, d, s, axis, src, src, landing))
+            for copy in waits:
+                copy.wait_recv()
+
+    q1, q2 = w1 // 2, w2 // 2
+    seg1, seg2, seg3, seg4 = [], [], [], []
+    for h, (a1, a2) in enumerate(plans):
+        p1, p2 = pos(a1), pos(a2)
+        base = h * half + p1 * w1
+        seg1.append((a1,
+                     lambda j, d, h=h: x_ref.at[:, cols(h * half + j * w1 + d * q1, q1)],
+                     lambda d, h=h: part.at[h, :, cols(d * q1, q1)]))
+        seg2.append((a2,
+                     lambda j, d, h=h: part.at[h, :, cols(j * w2 + d * q2, q2)],
+                     lambda d, base=base, p2=p2: o_ref.at[:, cols(base + p2 * w2 + d * q2, q2)]))
+        seg3.append((a2, lambda j, d, base=base: o_ref.at[:, cols(base + j * w2 + d * q2, q2)]))
+        seg4.append((a1, lambda j, d, h=h: o_ref.at[:, cols(h * half + j * w1 + d * q1, q1)]))
+    reduce_scatter(0, seg1, rbuf1, acc1)
+    reduce_scatter(1, seg2, rbuf2, acc2)
+    all_gather(2, seg3)
+    all_gather(3, seg4)
+    for copy in sends:
+        copy.wait_send()
+
+
+def ray_allreduce(mesh, owned):
+    axes = ray_axes(mesh)
+    rows, width = owned.shape
+    half = width // 2
+    w1 = half // axes[0][0]
+    w2 = w1 // axes[1][0]
+    steps = max(axes[0][0], axes[1][0]) - 1
+    return pl.pallas_call(
+        functools.partial(allreduce_kernel, axes),
+        out_shape=jax.ShapeDtypeStruct((rows, width), jnp.float32),
+        in_specs=[pl.BlockSpec(memory_space=pltpu.VMEM)],
+        out_specs=pl.BlockSpec(memory_space=pltpu.VMEM),
+        scratch_shapes=[
+            pltpu.VMEM((2, rows, w1), jnp.float32),
+            pltpu.VMEM((2, 2, steps, rows, w1 // 2), jnp.float32),
+            pltpu.VMEM((2, 2, steps, rows, w1 // 2), jnp.float32),
+            pltpu.VMEM((2, 2, steps, rows, w2 // 2), jnp.float32),
+            pltpu.VMEM((2, 2, steps, rows, w2 // 2), jnp.float32),
+            pltpu.SemaphoreType.DMA((4, 2, 2, steps)),
+            pltpu.SemaphoreType.DMA((4, 2, 2, steps)),
+        ],
+        compiler_params=pltpu.CompilerParams(
+            collective_id=2, has_side_effects=True, vmem_limit_bytes=60 * 1024 * 1024),
+    )(owned)
+
+
 eps_norm = 1e-06
 
 
@@ -133,7 +268,7 @@
         owned = jnp.einsum(
             "cnk,nt->ctk", arrived, owner_onehot, preferred_element_type=jnp.float32
         ).reshape(columns, TILE_DEV * CB)
-        total = lax.psum(owned, "ray")
+        total = ray_allreduce(mesh, owned)
         return total
 
     def cell_norm(field):

time: 578 us -> 513 us (0.89)
  waiting for transfers between devices: 291 us -> 50.7 us
  Pallas kernels: 56.3 us -> 244 us
  between operations: 14.3 us -> 0.95 us
    psum x2 -> x0, waiting for transfers between devices: 240 us -> none  [adjoint(): total = lax.psum(owned, 'ray')]
    pallas_call x0 -> x2, Pallas kernels: none -> 171 us  [ray_allreduce(): pl.pallas_call(functools.partial(allreduce_kernel, axes), out_shape=jax.S...]
    pallas_call x5, Pallas kernels: 56.3 us -> 73.7 us  [group_sum(): pl.pallas_call(functools.partial(reduce_kernel, plan), out_shape=jax.Shap...]
  transfers between devices with their start and end apart: 5 -> 3, of which waited for: 4 -> 2; matrix products, arithmetic and copies ran while one was open for 2% -> 3% of each run, Pallas kernels for 3% -> 3%
where the time goes in v5:
time: 513 us; the launch traced here: 511 us
  Pallas kernels  244 us (48%)
  blocking collectives  92.7 us (18%)
  waiting for transfers between devices  50.7 us (10%)
  other arithmetic  41.2 us (8%)
  matrix products  38.7 us (8%)
  local copies, waits for them, and re-layouts  27.4 us (5%)
  starting transfers between devices  15.1 us (3%)
    pallas_call x2, Pallas kernels, ray_allreduce(): pl.pallas_call(functools.partial(allreduce_kernel, axes), out_shape=jax.S...  171 us
    pallas_call x5, Pallas kernels, group_sum(): pl.pallas_call(functools.partial(reduce_kernel, plan), out_shape=jax.Shap...  73.7 us
    all_to_all x2, blocking collectives, fetch(): lax.all_to_all(outgoing, 'tile', split_axis=1, concat_axis=1, tiled=True)  61.2 us
    all_to_all x1, blocking collectives, adjoint(): lax.all_to_all(terms, 'tile', split_axis=1, concat_axis=1, tiled=True)  31.6 us
    all_to_all x1, waiting for transfers between devices, fetch(): lax.all_to_all(outgoing, 'tile', split_axis=1, concat_axis=1, tiled=True)  25.6 us
    all_to_all x1, waiting for transfers between devices, adjoint(): lax.all_to_all(terms, 'tile', split_axis=1, concat_axis=1, tiled=True)  25.1 us
    dot_general x3, matrix products, forward(): jnp.einsum('cnk,nrk->ncr', tiles, sensitivity, preferred_element_type=jnp...  18.1 us
    unnamed x15, local copies, waits for them, and re-layouts  15.1 us
  transfers between devices with their start and end apart: 3, of which 2 were waited for; matrix products, arithmetic and copies ran while one was open for 3% of the time, Pallas kernels for 3%

profile of v5, /device:TPU:1, one launch (start us, length us, event | category | flops | bytes accessed | tf_op | source)
XLA Modules:
  0.0 511.2 jit_solution(15033428814404464373)
XLA Ops:
  0.6 1.3 copy.25
  2.0 6.0 %all-to-all-start = ((s32[1,8,4]{2,0,1:T(1,128)}), s32[1,8,4]{2,0,1:T(1,128)S(1)}, u32[]{:S(2)}, u32[]{:S(2)}) async-start(s32[1,8,4]{2,0,1:T(1,128)} %copy.25), calls=%async_computation | async-start | bytes 8192 | tf_op jit(solution)/shard_map/all_to_all | solution.py:236
  7.9 0.8 copy.26
  8.8 1.2 multiply_reduce_fusion.4
  10.6 16.2 %shard_map.59 = f32[8,128]{1,0:T(8,128)} custom-call(f32[8,128]{1,0:T(8,128)} %scatter.16.x_ref), custom_call_target="tpu_custom_call" | custom-call | tf_op jit(solution)/shard_map/pallas_call | solution.py:80
  27.5 1.1 fusion.19
  29.3 6.3 %convert_bitcast_fusion.1 = bf16[64,32,512]{2,0,1:T(8,128)(2,1)} fusion(bf16[32,256,512]{2,1,0:T(8,128)(2,1)} %param.19, bf16[32,64,256]{2,1,0:T(8,128)(2,1)S(1)} %gather_fusion, pred[32]{0:T(512)(128)(4,1)S(1)} %compare_and_fusion.1), kind=kOutput, calls=%fused_computation.28 | convolution fusion | flops 538443776 | bytes 11534368 | tf_op jit(solution)/shard_map/cnr,nrk->cnk/dot_general | solution.py:264
  35.6 4.9 all-to-all-start.1
  41.8 25.1 %all-to-all-done.1 = bf16[64,32,512]{2,0,1:T(8,128)(2,1)S(1)} async-done(((bf16[64,32,512]{2,0,1:T(8,128)(2,1)}), bf16[64,32,512]{2,0,1:T(8,128)(2,1)S(1)}, u32[]{:S(2)}, u32[]{:S(2)}) %all-to-all-start.1) | async-done | bytes 2097184 | tf_op jit(solution)/shard_map/all_to_all | solution.py:267
  66.8 1.7 fusion.8
  68.6 6.3 %copy.42 = f32[8,8,48,512]{3,1,2,0:T(8,128)} copy(f32[8,8,48,512]{3,2,1,0:T(8,128)S(1)} %bitcast.109) | data formatting | bytes 12582912
  74.8 85.7 %shard_map.60 = f32[64,24576]{1,0:T(8,128)} custom-call(f32[64,24576]{1,0:T(8,128)} %bitcast.110), custom_call_target="tpu_custom_call" | custom-call | tf_op jit(solution)/shard_map/pallas_call | solution.py:211
  160.6 3.3 multiply_reduce_fusion.1
  164.5 17.1 %shard_map.61 = f32[8,128]{1,0:T(8,128)} custom-call(f32[8,128]{1,0:T(8,128)} %scatter.19.x_ref), custom_call_target="tpu_custom_call" | custom-call | tf_op jit(solution)/shard_map/pallas_call | solution.py:80
  182.2 3.2 fusion.38
  185.9 2.0 gather_fusion.1
  187.9 1.8 select_bitcast_fusion.2
  189.7 29.6 %all_to_all.30 = bf16[64,32,512]{2,0,1:T(8,128)(2,1)S(1)} all-to-all(bf16[64,32,512]{2,0,1:T(8,128)(2,1)S(1)} %select_bitcast_fusion.2), channel_id=1, replica_groups=mesh['ray'=16,'tile'=8] {'tile'}, dimensions={1} | all-to-all | bytes 4194304 | tf_op jit(solution)/shard_map/all_to_all | solution.py:249
  219.4 6.0 %fusion.42 = f32[32,64,256]{2,1,0:T(8,128)S(1)} fusion(bf16[64,32,512]{2,0,1:T(8,128)(2,1)S(1)} %all_to_all.30, bf16[32,256,512]{2,1,0:T(8,128)(2,1)} %param.19), kind=kOutput, calls=%fused_computation.79 | convolution fusion | flops 536870912 | bytes 12582912 | tf_op jit(solution)/shard_map/cnk,nrk->ncr/dot_general | solution.py:254
  225.4 2.0 fusion.6
  228.5 11.8 %shard_map.62 = f32[8,128]{1,0:T(8,128)} custom-call(f32[8,128]{1,0:T(8,128)} %scatter.20.x_ref), custom_call_target="tpu_custom_call" | custom-call | tf_op jit(solution)/shard_map/pallas_call | solution.py:80
  240.3 0.7 sqrt_bitcast_fusion.1
  241.8 5.0 convert_bitcast_fusion
  246.8 31.6 %all_to_all.31 = bf16[64,32,512]{2,0,1:T(8,128)(2,1)S(1)} all-to-all(bf16[64,32,512]{2,0,1:T(8,128)(2,1)S(1)} %convert_bitcast_fusion), channel_id=1, replica_groups=mesh['ray'=16,'tile'=8] {'tile'}, dimensions={1} | all-to-all | bytes 4194304 | tf_op jit(solution)/shard_map/all_to_all | solution.py:267
  278.3 1.7 fusion.4
  280.1 6.3 %copy.44 = f32[8,8,48,512]{3,1,2,0:T(8,128)} copy(f32[8,8,48,512]{3,2,1,0:T(8,128)S(1)} %bitcast.108) | data formatting | bytes 12582912
  286.3 85.0 %shard_map.63 = f32[64,24576]{1,0:T(8,128)} custom-call(f32[64,24576]{1,0:T(8,128)} %bitcast.111), custom_call_target="tpu_custom_call" | custom-call | tf_op jit(solution)/shard_map/pallas_call | solution.py:211
  371.3 5.8 %multiply_reduce_fusion = f32[64]{0:T(128)S(1)} fusion(f32[64,24576]{1,0:T(8,128)} %shard_map.63, f32[64]{0:T(128)S(1)} %sqrt_bitcast_fusion.1, f32[64,24576]{1,0:T(8,128)} %shard_map.60, f32[64]{0:T(128)S(1)} %sqrt_bitcast_fusion.2), kind=kLoop, calls=%fused_computation.6 | loop fusion | flops 7864256 | bytes 12583680 | tf_op jit(solution)/shard_map/reduce_sum | solution.py:275
  377.7 17.0 %shard_map.64 = f32[8,128]{1,0:T(8,128)} custom-call(f32[8,128]{1,0:T(8,128)} %scatter.21.x_ref), custom_call_target="tpu_custom_call" | custom-call | tf_op jit(solution)/shard_map/pallas_call | solution.py:80
  394.7 0.7 sqrt_bitcast_fusion
  395.4 5.2 %fusion.10 = bf16[64,24576]{1,0:T(8,128)(2,1)S(1)} fusion(f32[64]{0:T(128)S(1)} %sqrt_bitcast_fusion, f32[64,24576]{1,0:T(8,128)} %shard_map.63, f32[64]{0:T(128)S(1)} %sqrt_bitcast_fusion.1, f32[64,24576]{1,0:T(8,128)} %shard_map.60, f32[64]{0:T(128)S(1)} %sqrt_bitcast_fusion.2), kind=kLoop, calls=%fused_computation.29 | loop fusion | flops 7864320 | bytes 15729408 | tf_op jit(solution)/shard_map/convert_element_type | solution.py:293
  401.1 2.0 gather_fusion.3
  403.1 3.2 select_bitcast_fusion.1
  406.2 4.2 all-to-all-start.4
  410.5 0.7 multiply_divide_fusion.2
  411.2 25.6 %all-to-all-done.4 = bf16[64,32,512]{2,0,1:T(8,128)(2,1)S(1)} async-done(((bf16[64,32,512]{2,0,1:T(8,128)(2,1)}), bf16[64,32,512]{2,0,1:T(8,128)(2,1)S(1)}, u32[]{:S(2)}, u32[]{:S(2)}) %all-to-all-start.4) | async-done | bytes 2097184 | tf_op jit(solution)/shard_map/all_to_all | solution.py:249
  436.8 6.0 %fusion.43 = f32[32,64,256]{2,1,0:T(8,128)S(1)} fusion(bf16[64,32,512]{2,0,1:T(8,128)(2,1)S(1)} %all-to-all-done.4, bf16[32,256,512]{2,1,0:T(8,128)(2,1)} %param.19), kind=kOutput, calls=%fused_computation.80 | convolution fusion | flops 536870912 | bytes 12582912 | tf_op jit(solution)/shard_map/cnk,nrk->ncr/dot_general | solution.py:254
  442.8 2.0 fusion.2
  445.8 11.7 %shard_map.65 = f32[8,128]{1,0:T(8,128)} custom-call(f32[8,128]{1,0:T(8,128)} %scatter.24.x_ref), custom_call_target="tpu_custom_call" | custom-call | tf_op jit(solution)/shard_map/pallas_call | solution.py:80
  457.5 0.7 multiply_divide_fusion.1
  458.3 0.7 multiply_divide_fusion
  458.9 7.4 %fusion.39 = (bf16[64,24576]{1,0:T(8,128)(2,1)S(1)}, f32[64,24576]{1,0:T(8,128)}) fusion(f32[64]{0:T(128)S(1)} %multiply_divide_fusion, f32[64]{0:T(128)S(1)} %sqrt_bitcast_fusion, f32[64,24576]{1,0:T(8,128)} %shard_map.63, f32[64]{0:T(128)S(1)} %sqrt_bitcast_fusion.1, f32[64]{0:T(128)S(1)} %get-tuple-element.69, f32[64,24576]{1,0:T(8,128)} %shard_map.60, ...), kind=kLoop, calls=%fused_computation.78 | loop fusion | flops 15728640 | bytes 22021632 | tf_op jit(solution)/shard_map/convert_element_type | solution.py:310
  466.7 2.0 gather_fusion.4
  468.7 1.8 select_bitcast_fusion
  470.6 31.5 %all_to_all.32 = bf16[64,32,512]{2,0,1:T(8,128)(2,1)S(1)} all-to-all(bf16[64,32,512]{2,0,1:T(8,128)(2,1)S(1)} %select_bitcast_fusion), channel_id=1, replica_groups=mesh['ray'=16,'tile'=8] {'tile'}, dimensions={1} | all-to-all | bytes 4194304 | tf_op jit(solution)/shard_map/all_to_all | solution.py:249
  502.1 6.0 %fusion.44 = f32[32,64,256]{2,1,0:T(8,128)S(1)} fusion(bf16[64,32,512]{2,0,1:T(8,128)(2,1)S(1)} %all_to_all.32, bf16[32,256,512]{2,1,0:T(8,128)(2,1)} %param.19), kind=kOutput, calls=%fused_computation.81 | convolution fusion | flops 536870912 | bytes 12582912 | tf_op jit(solution)/shard_map/cnk,nrk->ncr/dot_general | solution.py:254
  508.2 2.0 fusion
  510.3 0.9 sub.19
  (39 shorter events, 9.4 us)
Async XLA Ops:
  2.0 33.6 %all-to-all-start = ((s32[1,8,4]{2,0,1:T(1,128)}), s32[1,8,4]{2,0,1:T(1,128)S(1)}, u32[]{:S(2)}, u32[]{:S(2)}) async-start(s32[1,8,4]{2,0,1:T(1,128)} %copy.25), calls=%async_computation | async-start | bytes 8192 | tf_op jit(solution)/shard_map/all_to_all | solution.py:236
  35.6 31.2 %all-to-all-start.1 = ((bf16[64,32,512]{2,0,1:T(8,128)(2,1)}), bf16[64,32,512]{2,0,1:T(8,128)(2,1)S(1)}, u32[]{:S(2)}, u32[]{:S(2)}) async-start(bf16[64,32,512]{2,0,1:T(8,128)(2,1)} %convert_bitcast_fusion.1), calls=%async_computation.1 | async-start | bytes 4194304 | tf_op jit(solution)/shard_map/all_to_all | solution.py:267
  225.4 2.1 copy-start
  227.8 13.3 %copy-start.2 = (f32[64,2048]{1,0:T(8,128)}, f32[64,2048]{1,0:T(8,128)S(1)}, u32[]{:S(2)}) copy-start(f32[64,2048]{1,0:T(8,128)S(1)} %get-tuple-element.72) | copy-start | bytes 1572868
  406.2 30.6 %all-to-all-start.4 = ((bf16[64,32,512]{2,0,1:T(8,128)(2,1)}), bf16[64,32,512]{2,0,1:T(8,128)(2,1)S(1)}, u32[]{:S(2)}, u32[]{:S(2)}) async-start(bf16[64,32,512]{2,0,1:T(8,128)(2,1)} %select_bitcast_fusion.1), calls=%async_computation.4 | async-start | bytes 4194304 | tf_op jit(solution)/shard_map/all_to_all | solution.py:249
  442.8 2.1 copy-start.3
  508.2 2.1 copy-start.1

commit v6 on v5

--- a/solution.py
+++ b/solution.py
@@ -98,7 +98,7 @@
     return ((inner, 1), (rays // inner, inner))
 
 
-def allreduce_kernel(axes, x_ref, o_ref, part, rbuf1, acc1, rbuf2, acc2, send_sems, recv_sems):
+def allreduce_kernel(axes, x_ref, o_ref, part, rbuf1, acc1, rbuf2, send_sems, recv_sems):
     me = lax.axis_index("ray")
     tile = lax.axis_index("tile")
     rows = x_ref.shape[0]
@@ -128,7 +128,7 @@
     barrier = pltpu.get_barrier_semaphore()
     greeted = 0
     for axis in axes:
-        for k in (1, axis[0] - 1) if axis[0] > 2 else (1,):
+        for k in range(1, axis[0]):
             pl.semaphore_signal(barrier, inc=1, device_id=peer(axis, k), device_id_type=MESH)
             greeted += 1
     pl.semaphore_wait(barrier, greeted)
@@ -180,6 +180,54 @@
             for copy in waits:
                 copy.wait_recv()
 
+    def direct_reduce_scatter(stage, segs, rbuf, width):
+        waits = []
+        for h, (axis, own, final) in enumerate(segs):
+            size, p = axis[0], pos(axis)
+            for k in range(1, size):
+                slot = rbuf.at[h, k - 1]
+                copy = pltpu.make_async_remote_copy(
+                    src_ref=own((p - k + size) % size), dst_ref=slot,
+                    send_sem=send_sems.at[stage, h, 0, k - 1], recv_sem=recv_sems.at[stage, h, 0, k - 1],
+                    device_id=peer(axis, k), device_id_type=MESH)
+                copy.start()
+                sends.append(copy)
+                waits.append(copy)
+        for copy in waits:
+            copy.wait_recv()
+        for h, (axis, own, final) in enumerate(segs):
+            size, p = axis[0], pos(axis)
+            def body(r, carry, h=h, size=size, p=p, own=own, final=final):
+                block = pl.ds(pl.multiple_of(r * 8, 8), 8)
+                total = None
+                for q in range(size):
+                    k = (q - p + size) % size
+                    mine = own(p)[block, :]
+                    other = rbuf[h, jnp.maximum(k - 1, 0), block, :]
+                    val = jnp.where(k == 0, mine, other)
+                    total = val if total is None else total + val
+                final[block, :] = total
+                return carry
+            lax.fori_loop(0, rows // 8, body, 0)
+
+    def direct_all_gather(stage, segs):
+        waits = []
+        for h, (axis, region) in enumerate(segs):
+            size, p = axis[0], pos(axis)
+            for k in range(1, size):
+                copy = pltpu.make_async_remote_copy(
+                    src_ref=region(p), dst_ref=region(p),
+                    send_sem=send_sems.at[stage, h, 0, k - 1], recv_sem=recv_sems.at[stage, h, 0, k - 1],
+                    device_id=peer(axis, k), device_id_type=MESH)
+                copy.start()
+                sends.append(copy)
+                waits.append(pltpu.make_async_remote_copy(
+                    src_ref=region(p), dst_ref=region((p + k) % size),
+                    send_sem=send_sems.at[stage, h, 0, k - 1], recv_sem=recv_sems.at[stage, h, 0, k - 1],
+                    device_id=peer(axis, k), device_id_type=MESH))
+        for copy in waits:
+            copy.wait_recv()
+
     q1, q2 = w1 // 2, w2 // 2
     seg1, seg2, seg3, seg4 = [], [], [], []
     for h, (a1, a2) in enumerate(plans):
@@ -189,13 +237,13 @@
                      lambda j, d, h=h: x_ref.at[:, cols(h * half + j * w1 + d * q1, q1)],
                      lambda d, h=h: part.at[h, :, cols(d * q1, q1)]))
         seg2.append((a2,
-                     lambda j, d, h=h: part.at[h, :, cols(j * w2 + d * q2, q2)],
-                     lambda d, base=base, p2=p2: o_ref.at[:, cols(base + p2 * w2 + d * q2, q2)]))
-        seg3.append((a2, lambda j, d, base=base: o_ref.at[:, cols(base + j * w2 + d * q2, q2)]))
+                     lambda j, h=h: part.at[h, :, cols(j * w2, w2)],
+                     o_ref.at[:, cols(base + p2 * w2, w2)]))
+        seg3.append((a2, lambda j, base=base: o_ref.at[:, cols(base + j * w2, w2)]))
         seg4.append((a1, lambda j, d, h=h: o_ref.at[:, cols(h * half + j * w1 + d * q1, q1)]))
     reduce_scatter(0, seg1, rbuf1, acc1)
-    reduce_scatter(1, seg2, rbuf2, acc2)
-    all_gather(2, seg3)
+    direct_reduce_scatter(1, seg2, rbuf2, w2)
+    direct_all_gather(2, seg3)
     all_gather(3, seg4)
     for copy in sends:
         copy.wait_send()
@@ -217,8 +265,7 @@
             pltpu.VMEM((2, rows, w1), jnp.float32),
             pltpu.VMEM((2, 2, steps, rows, w1 // 2), jnp.float32),
             pltpu.VMEM((2, 2, steps, rows, w1 // 2), jnp.float32),
-            pltpu.VMEM((2, 2, steps, rows, w2 // 2), jnp.float32),
-            pltpu.VMEM((2, 2, steps, rows, w2 // 2), jnp.float32),
+            pltpu.VMEM((2, steps, rows, w2), jnp.float32),
             pltpu.SemaphoreType.DMA((4, 2, 2, steps)),
             pltpu.SemaphoreType.DMA((4, 2, 2, steps)),
         ],

time: 513 us -> 495 us (0.965)
  Pallas kernels: 244 us -> 226 us
    pallas_call x5, Pallas kernels: 73.7 us -> 58.6 us  [group_sum(): pl.pallas_call(functools.partial(reduce_kernel, plan), out_shape=jax.Shap...]
where the time goes in v6:
time: 495 us; the launch traced here: 494 us
  Pallas kernels  226 us (46%)
  blocking collectives  93.2 us (19%)
  waiting for transfers between devices  50.7 us (10%)
  other arithmetic  41.2 us (8%)
  matrix products  38.7 us (8%)
  local copies, waits for them, and re-layouts  27.4 us (6%)
  starting transfers between devices  15.8 us (3%)
    pallas_call x2, Pallas kernels, ray_allreduce(): pl.pallas_call(functools.partial(allreduce_kernel, axes), out_shape=jax.S...  167 us
    all_to_all x2, blocking collectives, fetch(): lax.all_to_all(outgoing, 'tile', split_axis=1, concat_axis=1, tiled=True)  61.7 us
    pallas_call x5, Pallas kernels, group_sum(): pl.pallas_call(functools.partial(reduce_kernel, plan), out_shape=jax.Shap...  58.6 us
    all_to_all x1, blocking collectives, adjoint(): lax.all_to_all(terms, 'tile', split_axis=1, concat_axis=1, tiled=True)  31.6 us
    all_to_all x1, waiting for transfers between devices, fetch(): lax.all_to_all(outgoing, 'tile', split_axis=1, concat_axis=1, tiled=True)  25.6 us
    all_to_all x1, waiting for transfers between devices, adjoint(): lax.all_to_all(terms, 'tile', split_axis=1, concat_axis=1, tiled=True)  25.1 us
    dot_general x3, matrix products, forward(): jnp.einsum('cnk,nrk->ncr', tiles, sensitivity, preferred_element_type=jnp...  18.1 us
    unnamed x15, local copies, waits for them, and re-layouts  15.1 us
  transfers between devices with their start and end apart: 3, of which 2 were waited for; matrix products, arithmetic and copies ran while one was open for 3% of the time, Pallas kernels for 3%

profile of v6, /device:TPU:1, one launch (start us, length us, event | category | flops | bytes accessed | tf_op | source)
XLA Modules:
  0.0 493.8 jit_solution(16744313761945779635)
XLA Ops:
  0.6 1.3 copy.25
  2.0 6.0 %all-to-all-start = ((s32[1,8,4]{2,0,1:T(1,128)}), s32[1,8,4]{2,0,1:T(1,128)S(1)}, u32[]{:S(2)}, u32[]{:S(2)}) async-start(s32[1,8,4]{2,0,1:T(1,128)} %copy.25), calls=%async_computation | async-start | bytes 8192 | tf_op jit(solution)/shard_map/all_to_all | solution.py:283
  7.9 0.8 copy.26
  8.8 1.2 multiply_reduce_fusion.4
  10.6 16.2 %shard_map.59 = f32[8,128]{1,0:T(8,128)} custom-call(f32[8,128]{1,0:T(8,128)} %scatter.16.x_ref), custom_call_target="tpu_custom_call" | custom-call | tf_op jit(solution)/shard_map/pallas_call | solution.py:80
  27.5 1.1 fusion.19
  29.3 6.3 %convert_bitcast_fusion.1 = bf16[64,32,512]{2,0,1:T(8,128)(2,1)} fusion(bf16[32,256,512]{2,1,0:T(8,128)(2,1)} %param.19, bf16[32,64,256]{2,1,0:T(8,128)(2,1)S(1)} %gather_fusion, pred[32]{0:T(512)(128)(4,1)S(1)} %compare_and_fusion.1), kind=kOutput, calls=%fused_computation.28 | convolution fusion | flops 538443776 | bytes 11534368 | tf_op jit(solution)/shard_map/cnr,nrk->cnk/dot_general | solution.py:311
  35.6 4.9 all-to-all-start.1
  41.8 25.1 %all-to-all-done.1 = bf16[64,32,512]{2,0,1:T(8,128)(2,1)S(1)} async-done(((bf16[64,32,512]{2,0,1:T(8,128)(2,1)}), bf16[64,32,512]{2,0,1:T(8,128)(2,1)S(1)}, u32[]{:S(2)}, u32[]{:S(2)}) %all-to-all-start.1) | async-done | bytes 2097184 | tf_op jit(solution)/shard_map/all_to_all | solution.py:314
  66.8 1.7 fusion.8
  68.6 6.3 %copy.42 = f32[8,8,48,512]{3,1,2,0:T(8,128)} copy(f32[8,8,48,512]{3,2,1,0:T(8,128)S(1)} %bitcast.109) | data formatting | bytes 12582912
  74.8 85.1 %shard_map.60 = f32[64,24576]{1,0:T(8,128)} custom-call(f32[64,24576]{1,0:T(8,128)} %bitcast.110), custom_call_target="tpu_custom_call" | custom-call | tf_op jit(solution)/shard_map/pallas_call | solution.py:259
  160.0 3.3 multiply_reduce_fusion.1
  163.9 8.0 %shard_map.61 = f32[8,128]{1,0:T(8,128)} custom-call(f32[8,128]{1,0:T(8,128)} %scatter.19.x_ref), custom_call_target="tpu_custom_call" | custom-call | tf_op jit(solution)/shard_map/pallas_call | solution.py:80
  172.5 3.2 fusion.38
  176.2 2.0 gather_fusion.1
  178.2 1.8 select_bitcast_fusion.2
  180.1 30.2 %all_to_all.30 = bf16[64,32,512]{2,0,1:T(8,128)(2,1)S(1)} all-to-all(bf16[64,32,512]{2,0,1:T(8,128)(2,1)S(1)} %select_bitcast_fusion.2), channel_id=1, replica_groups=mesh['ray'=16,'tile'=8] {'tile'}, dimensions={1} | all-to-all | bytes 4194304 | tf_op jit(solution)/shard_map/all_to_all | solution.py:296
  210.3 6.0 %fusion.42 = f32[32,64,256]{2,1,0:T(8,128)S(1)} fusion(bf16[64,32,512]{2,0,1:T(8,128)(2,1)S(1)} %all_to_all.30, bf16[32,256,512]{2,1,0:T(8,128)(2,1)} %param.19), kind=kOutput, calls=%fused_computation.79 | convolution fusion | flops 536870912 | bytes 12582912 | tf_op jit(solution)/shard_map/cnk,nrk->ncr/dot_general | solution.py:301
  216.3 2.0 fusion.6
  219.4 12.0 %shard_map.62 = f32[8,128]{1,0:T(8,128)} custom-call(f32[8,128]{1,0:T(8,128)} %scatter.20.x_ref), custom_call_target="tpu_custom_call" | custom-call | tf_op jit(solution)/shard_map/pallas_call | solution.py:80
  231.4 0.7 sqrt_bitcast_fusion.1
  232.9 5.0 %convert_bitcast_fusion = bf16[64,32,512]{2,0,1:T(8,128)(2,1)S(1)} fusion(bf16[32,256,512]{2,1,0:T(8,128)(2,1)} %param.19, bf16[32,64,256]{2,1,0:T(8,128)(2,1)S(1)} %gather_fusion.2, pred[32]{0:T(512)(128)(4,1)S(1)} %compare_and_fusion.1), kind=kOutput, calls=%fused_computation.27 | convolution fusion | flops 538443776 | bytes 11534368 | tf_op jit(solution)/shard_map/cnr,nrk->cnk/dot_general | solution.py:311
  237.9 31.6 %all_to_all.31 = bf16[64,32,512]{2,0,1:T(8,128)(2,1)S(1)} all-to-all(bf16[64,32,512]{2,0,1:T(8,128)(2,1)S(1)} %convert_bitcast_fusion), channel_id=1, replica_groups=mesh['ray'=16,'tile'=8] {'tile'}, dimensions={1} | all-to-all | bytes 4194304 | tf_op jit(solution)/shard_map/all_to_all | solution.py:314
  269.4 1.7 fusion.4
  271.2 6.3 %copy.44 = f32[8,8,48,512]{3,1,2,0:T(8,128)} copy(f32[8,8,48,512]{3,2,1,0:T(8,128)S(1)} %bitcast.108) | data formatting | bytes 12582912
  277.4 82.0 %shard_map.63 = f32[64,24576]{1,0:T(8,128)} custom-call(f32[64,24576]{1,0:T(8,128)} %bitcast.111), custom_call_target="tpu_custom_call" | custom-call | tf_op jit(solution)/shard_map/pallas_call | solution.py:259
  359.5 5.8 %multiply_reduce_fusion = f32[64]{0:T(128)S(1)} fusion(f32[64,24576]{1,0:T(8,128)} %shard_map.63, f32[64]{0:T(128)S(1)} %sqrt_bitcast_fusion.1, f32[64,24576]{1,0:T(8,128)} %shard_map.60, f32[64]{0:T(128)S(1)} %sqrt_bitcast_fusion.2), kind=kLoop, calls=%fused_computation.6 | loop fusion | flops 7864256 | bytes 12583680 | tf_op jit(solution)/shard_map/reduce_sum | solution.py:322
  365.9 10.3 %shard_map.64 = f32[8,128]{1,0:T(8,128)} custom-call(f32[8,128]{1,0:T(8,128)} %scatter.21.x_ref), custom_call_target="tpu_custom_call" | custom-call | tf_op jit(solution)/shard_map/pallas_call | solution.py:80
  376.2 0.7 sqrt_bitcast_fusion
  376.8 5.2 %fusion.10 = bf16[64,24576]{1,0:T(8,128)(2,1)S(1)} fusion(f32[64]{0:T(128)S(1)} %sqrt_bitcast_fusion, f32[64,24576]{1,0:T(8,128)} %shard_map.63, f32[64]{0:T(128)S(1)} %sqrt_bitcast_fusion.1, f32[64,24576]{1,0:T(8,128)} %shard_map.60, f32[64]{0:T(128)S(1)} %sqrt_bitcast_fusion.2), kind=kLoop, calls=%fused_computation.29 | loop fusion | flops 7864320 | bytes 15729408 | tf_op jit(solution)/shard_map/convert_element_type | solution.py:340
  382.5 2.0 gather_fusion.3
  384.5 3.2 select_bitcast_fusion.1
  387.7 5.0 %all-to-all-start.4 = ((bf16[64,32,512]{2,0,1:T(8,128)(2,1)}), bf16[64,32,512]{2,0,1:T(8,128)(2,1)S(1)}, u32[]{:S(2)}, u32[]{:S(2)}) async-start(bf16[64,32,512]{2,0,1:T(8,128)(2,1)} %select_bitcast_fusion.1), calls=%async_computation.4 | async-start | bytes 4194304 | tf_op jit(solution)/shard_map/all_to_all | solution.py:296
  392.6 0.7 multiply_divide_fusion.2
  393.4 25.6 %all-to-all-done.4 = bf16[64,32,512]{2,0,1:T(8,128)(2,1)S(1)} async-done(((bf16[64,32,512]{2,0,1:T(8,128)(2,1)}), bf16[64,32,512]{2,0,1:T(8,128)(2,1)S(1)}, u32[]{:S(2)}, u32[]{:S(2)}) %all-to-all-start.4) | async-done | bytes 2097184 | tf_op jit(solution)/shard_map/all_to_all | solution.py:296
  419.0 6.0 %fusion.43 = f32[32,64,256]{2,1,0:T(8,128)S(1)} fusion(bf16[64,32,512]{2,0,1:T(8,128)(2,1)S(1)} %all-to-all-done.4, bf16[32,256,512]{2,1,0:T(8,128)(2,1)} %param.19), kind=kOutput, calls=%fused_computation.80 | convolution fusion | flops 536870912 | bytes 12582912 | tf_op jit(solution)/shard_map/cnk,nrk->ncr/dot_general | solution.py:301
  425.0 2.0 fusion.2
  428.0 12.1 %shard_map.65 = f32[8,128]{1,0:T(8,128)} custom-call(f32[8,128]{1,0:T(8,128)} %scatter.24.x_ref), custom_call_target="tpu_custom_call" | custom-call | tf_op jit(solution)/shard_map/pallas_call | solution.py:80
  440.1 0.7 multiply_divide_fusion.1
  440.9 0.7 multiply_divide_fusion
  441.6 7.4 %fusion.39 = (bf16[64,24576]{1,0:T(8,128)(2,1)S(1)}, f32[64,24576]{1,0:T(8,128)}) fusion(f32[64]{0:T(128)S(1)} %multiply_divide_fusion, f32[64]{0:T(128)S(1)} %sqrt_bitcast_fusion, f32[64,24576]{1,0:T(8,128)} %shard_map.63, f32[64]{0:T(128)S(1)} %sqrt_bitcast_fusion.1, f32[64]{0:T(128)S(1)} %get-tuple-element.69, f32[64,24576]{1,0:T(8,128)} %shard_map.60, ...), kind=kLoop, calls=%fused_computation.78 | loop fusion | flops 15728640 | bytes 22021632 | tf_op jit(solution)/shard_map/convert_element_type | solution.py:357
  449.3 2.0 gather_fusion.4
  451.4 1.8 select_bitcast_fusion
  453.2 31.5 %all_to_all.32 = bf16[64,32,512]{2,0,1:T(8,128)(2,1)S(1)} all-to-all(bf16[64,32,512]{2,0,1:T(8,128)(2,1)S(1)} %select_bitcast_fusion), channel_id=1, replica_groups=mesh['ray'=16,'tile'=8] {'tile'}, dimensions={1} | all-to-all | bytes 4194304 | tf_op jit(solution)/shard_map/all_to_all | solution.py:296
  484.7 6.0 %fusion.44 = f32[32,64,256]{2,1,0:T(8,128)S(1)} fusion(bf16[64,32,512]{2,0,1:T(8,128)(2,1)S(1)} %all_to_all.32, bf16[32,256,512]{2,1,0:T(8,128)(2,1)} %param.19), kind=kOutput, calls=%fused_computation.81 | convolution fusion | flops 536870912 | bytes 12582912 | tf_op jit(solution)/shard_map/cnk,nrk->ncr/dot_general | solution.py:301
  490.8 2.0 fusion
  492.9 0.9 sub.19
  (39 shorter events, 9.4 us)
Async XLA Ops:
  2.0 33.6 %all-to-all-start = ((s32[1,8,4]{2,0,1:T(1,128)}), s32[1,8,4]{2,0,1:T(1,128)S(1)}, u32[]{:S(2)}, u32[]{:S(2)}) async-start(s32[1,8,4]{2,0,1:T(1,128)} %copy.25), calls=%async_computation | async-start | bytes 8192 | tf_op jit(solution)/shard_map/all_to_all | solution.py:283
  35.6 31.2 %all-to-all-start.1 = ((bf16[64,32,512]{2,0,1:T(8,128)(2,1)}), bf16[64,32,512]{2,0,1:T(8,128)(2,1)S(1)}, u32[]{:S(2)}, u32[]{:S(2)}) async-start(bf16[64,32,512]{2,0,1:T(8,128)(2,1)} %convert_bitcast_fusion.1), calls=%async_computation.1 | async-start | bytes 4194304 | tf_op jit(solution)/shard_map/all_to_all | solution.py:314
  216.3 2.1 copy-start
  218.7 13.5 %copy-start.2 = (f32[64,2048]{1,0:T(8,128)}, f32[64,2048]{1,0:T(8,128)S(1)}, u32[]{:S(2)}) copy-start(f32[64,2048]{1,0:T(8,128)S(1)} %get-tuple-element.72) | copy-start | bytes 1572868
  387.7 31.3 %all-to-all-start.4 = ((bf16[64,32,512]{2,0,1:T(8,128)(2,1)}), bf16[64,32,512]{2,0,1:T(8,128)(2,1)S(1)}, u32[]{:S(2)}, u32[]{:S(2)}) async-start(bf16[64,32,512]{2,0,1:T(8,128)(2,1)} %select_bitcast_fusion.1), calls=%async_computation.4 | async-start | bytes 4194304 | tf_op jit(solution)/shard_map/all_to_all | solution.py:296
  425.0 2.1 copy-start.3
  490.7 2.1 copy-start.1

commit v7 on v6

--- a/solution.py
+++ b/solution.py
@@ -101,8 +101,7 @@
 def allreduce_kernel(axes, x_ref, o_ref, part, rbuf1, acc1, rbuf2, send_sems, recv_sems):
     me = lax.axis_index("ray")
     tile = lax.axis_index("tile")
-    rows = x_ref.shape[0]
-    half = x_ref.shape[1] // 2
+    half = x_ref.shape[0] // 2
     w1 = half // axes[0][0]
     w2 = w1 // axes[1][0]
 
@@ -116,14 +115,13 @@
         return (me + (((p - k + size) % size) - p) * stride, tile)
 
     def cols(start, width):
-        return pl.ds(pl.multiple_of(start, 128), width)
+        return pl.ds(start, width)
 
     def add_rows(dst, a, b):
         def body(r, carry):
-            block = pl.ds(pl.multiple_of(r * 8, 8), 8)
-            dst[block, :] = a[block, :] + b[block, :]
+            dst[r] = a[r] + b[r]
             return carry
-        lax.fori_loop(0, rows // 8, body, 0)
+        lax.fori_loop(0, dst.shape[0], body, 0)
 
     barrier = pltpu.get_barrier_semaphore()
     greeted = 0
@@ -198,17 +196,16 @@
         for h, (axis, own, final) in enumerate(segs):
             size, p = axis[0], pos(axis)
             def body(r, carry, h=h, size=size, p=p, own=own, final=final):
-                block = pl.ds(pl.multiple_of(r * 8, 8), 8)
                 total = None
                 for q in range(size):
                     k = (q - p + size) % size
-                    mine = own(p)[block, :]
-                    other = rbuf[h, jnp.maximum(k - 1, 0), block, :]
+                    mine = own(p)[r]
+                    other = rbuf[h, jnp.maximum(k - 1, 0), r]
                     val = jnp.where(k == 0, mine, other)
                     total = val if total is None else total + val
-                final[block, :] = total
+                final[r] = total
                 return carry
-            lax.fori_loop(0, rows // 8, body, 0)
+            lax.fori_loop(0, width, body, 0)
 
     def direct_all_gather(stage, segs):
         waits = []
@@ -234,13 +231,13 @@
         p1, p2 = pos(a1), pos(a2)
         base = h * half + p1 * w1
         seg1.append((a1,
-                     lambda j, d, h=h: x_ref.at[:, cols(h * half + j * w1 + d * q1, q1)],
-                     lambda d, h=h: part.at[h, :, cols(d * q1, q1)]))
+                     lambda j, d, h=h: x_ref.at[cols(h * half + j * w1 + d * q1, q1)],
+                     lambda d, h=h: part.at[h, cols(d * q1, q1)]))
         seg2.append((a2,
-                     lambda j, h=h: part.at[h, :, cols(j * w2, w2)],
-                     o_ref.at[:, cols(base + p2 * w2, w2)]))
-        seg3.append((a2, lambda j, base=base: o_ref.at[:, cols(base + j * w2, w2)]))
-        seg4.append((a1, lambda j, d, h=h: o_ref.at[:, cols(h * half + j * w1 + d * q1, q1)]))
+                     lambda j, h=h: part.at[h, cols(j * w2, w2)],
+                     o_ref.at[cols(base + p2 * w2, w2)]))
+        seg3.append((a2, lambda j, base=base: o_ref.at[cols(base + j * w2, w2)]))
+        seg4.append((a1, lambda j, d, h=h: o_ref.at[cols(h * half + j * w1 + d * q1, q1)]))
     reduce_scatter(0, seg1, rbuf1, acc1)
     direct_reduce_scatter(1, seg2, rbuf2, w2)
     direct_all_gather(2, seg3)
@@ -251,21 +248,22 @@
 
 def ray_allreduce(mesh, owned):
     axes = ray_axes(mesh)
-    rows, width = owned.shape
-    half = width // 2
+    rows = owned.shape[0]
+    inner = owned.shape[1:]
+    half = rows // 2
     w1 = half // axes[0][0]
     w2 = w1 // axes[1][0]
     steps = max(axes[0][0], axes[1][0]) - 1
     return pl.pallas_call(
         functools.partial(allreduce_kernel, axes),
-        out_shape=jax.ShapeDtypeStruct((rows, width), jnp.float32),
+        out_shape=jax.ShapeDtypeStruct(owned.shape, jnp.float32),
         in_specs=[pl.BlockSpec(memory_space=pltpu.VMEM)],
         out_specs=pl.BlockSpec(memory_space=pltpu.VMEM),
         scratch_shapes=[
-            pltpu.VMEM((2, rows, w1), jnp.float32),
-            pltpu.VMEM((2, 2, steps, rows, w1 // 2), jnp.float32),
-            pltpu.VMEM((2, 2, steps, rows, w1 // 2), jnp.float32),
-            pltpu.VMEM((2, steps, rows, w2), jnp.float32),
+            pltpu.VMEM((2, w1) + inner, jnp.float32),
+            pltpu.VMEM((2, 2, steps, w1 // 2) + inner, jnp.float32),
+            pltpu.VMEM((2, 2, steps, w1 // 2) + inner, jnp.float32),
+            pltpu.VMEM((2, steps, w2) + inner, jnp.float32),
             pltpu.SemaphoreType.DMA((4, 2, 2, steps)),
             pltpu.SemaphoreType.DMA((4, 2, 2, steps)),
         ],
@@ -314,12 +312,12 @@
         arrived = lax.all_to_all(terms, "tile", split_axis=1, concat_axis=1, tiled=True)
         owned = jnp.einsum(
             "cnk,nt->ctk", arrived, owner_onehot, preferred_element_type=jnp.float32
-        ).reshape(columns, TILE_DEV * CB)
+        )
         total = ray_allreduce(mesh, owned)
         return total
 
     def cell_norm(field):
-        local = jnp.sum(field * field, axis=1)
+        local = jnp.sum(field * field, axis=(1, 2))
         total = group_sum(mesh, ("tile",), 1, local)
         return jnp.sqrt(total + eps_norm)
 
@@ -331,7 +329,7 @@
     rays_dir = data / beta_now[:, None]
     model_dir = adjoint(rays_dir.astype(jnp.bfloat16))
     alpha_now = cell_norm(model_dir)
-    model_dir = model_dir / alpha_now[:, None]
+    model_dir = model_dir / alpha_now[:, None, None]
     search = model_dir
     solution = jnp.zeros_like(model_dir)
     phi_bar = beta_now
@@ -346,16 +344,16 @@
         sine_part = beta_now / rho_now
         phi_now = cosine * phi_bar
         phi_bar = sine_part * phi_bar
-        solution = solution + (phi_now / rho_now)[:, None] * search
+        solution = solution + (phi_now / rho_now)[:, None, None] * search
         if step + 1 < ITERS:
-            model_dir = adjoint(rays_dir.astype(jnp.bfloat16)) - beta_now[:, None] * model_dir
+            model_dir = adjoint(rays_dir.astype(jnp.bfloat16)) - beta_now[:, None, None] * model_dir
             alpha_now = cell_norm(model_dir)
-            model_dir = model_dir / alpha_now[:, None]
+            model_dir = model_dir / alpha_now[:, None, None]
             theta_now = sine_part * alpha_now
             rho_bar = -cosine * alpha_now
-            search = model_dir - (theta_now / rho_now)[:, None] * search
+            search = model_dir - (theta_now / rho_now)[:, None, None] * search
     residual = data - forward(solution.astype(jnp.bfloat16))
-    return (solution, residual)
+    return (solution.reshape(columns, TILE_DEV * CB), residual)
 
 
 def solution(mesh):

time: 495 us -> 502 us (1.014); the launches traced: 494 us -> 494 us
  blocking collectives: 93.2 us -> 63.2 us
  waiting for transfers between devices: 50.7 us -> 67.8 us
  starting transfers between devices: 15.8 us -> 21.5 us
  matrix products: 38.7 us -> 44.1 us
    all_to_all x2 -> x1, blocking collectives: 61.7 us -> 31.1 us  [fetch(): lax.all_to_all(outgoing, 'tile', split_axis=1, concat_axis=1, tiled=True)]
    all_to_all x1 -> x2, waiting for transfers between devices: 25.6 us -> 42.7 us  [fetch(): lax.all_to_all(outgoing, 'tile', split_axis=1, concat_axis=1, tiled=True)]
    all_to_all x1 -> x2, starting transfers between devices: 4.97 us -> 10.6 us  [fetch(): lax.all_to_all(outgoing, 'tile', split_axis=1, concat_axis=1, tiled=True)]
    dot_general x2, matrix products: 3.49 us -> 8.9 us  [adjoint(): jnp.einsum('cnk,nt->ctk', arrived, owner_onehot, preferred_element_type=j...]
    convert_element_type x0 -> x3, local copies, waits for them, and re-layouts: none -> 5.3 us  [the longest x2 3.53 us: per_device(): rounded = model_dir.astype(jnp.bfloat16)]
    unnamed x15 -> x14, local copies, waits for them, and re-layouts: 15.1 us -> 11.8 us
  transfers between devices with their start and end apart: 3 -> 4, of which waited for: 2 -> 3; matrix products, arithmetic and copies ran while one was open for 3% -> 5% of each run, Pallas kernels for 3% -> 3%
where the time goes in v7:
time: 502 us; the launch traced here: 494 us
  Pallas kernels  224 us (45%)
  waiting for transfers between devices  67.8 us (14%)
  blocking collectives  63.2 us (13%)
  matrix products  44.1 us (9%)
  other arithmetic  43.9 us (9%)
  local copies, waits for them, and re-layouts  28.1 us (6%)
  starting transfers between devices  21.5 us (4%)
    pallas_call x2, Pallas kernels, ray_allreduce(): pl.pallas_call(functools.partial(allreduce_kernel, axes), out_shape=jax.S...  162 us
    pallas_call x5, Pallas kernels, group_sum(): pl.pallas_call(functools.partial(reduce_kernel, plan), out_shape=jax.Shap...  61.6 us
    all_to_all x2, waiting for transfers between devices, fetch(): lax.all_to_all(outgoing, 'tile', split_axis=1, concat_axis=1, tiled=True)  42.7 us
    all_to_all x1, blocking collectives, adjoint(): lax.all_to_all(terms, 'tile', split_axis=1, concat_axis=1, tiled=True)  32.1 us
    all_to_all x1, blocking collectives, fetch(): lax.all_to_all(outgoing, 'tile', split_axis=1, concat_axis=1, tiled=True)  31.1 us
    all_to_all x1, waiting for transfers between devices, adjoint(): lax.all_to_all(terms, 'tile', split_axis=1, concat_axis=1, tiled=True)  25.1 us
    dot_general x3, matrix products, forward(): jnp.einsum('cnk,nrk->ncr', tiles, sensitivity, preferred_element_type=jnp...  18 us
    unnamed x14, local copies, waits for them, and re-layouts  11.8 us
  transfers between devices with their start and end apart: 4, of which 3 were waited for; matrix products, arithmetic and copies ran while one was open for 5% of the time, Pallas kernels for 3%

profile of v7, /device:TPU:1, one launch (start us, length us, event | category | flops | bytes accessed | tf_op | source)
XLA Modules:
  0.0 493.6 jit_solution(16253070137939199054)
XLA Ops:
  0.6 1.3 copy.25
  2.0 6.0 %all-to-all-start = ((s32[1,8,4]{2,0,1:T(1,128)}), s32[1,8,4]{2,0,1:T(1,128)S(1)}, u32[]{:S(2)}, u32[]{:S(2)}) async-start(s32[1,8,4]{2,0,1:T(1,128)} %copy.25), calls=%async_computation | async-start | bytes 8192 | tf_op jit(solution)/shard_map/all_to_all | solution.py:281
  7.9 0.8 copy.26
  8.8 1.2 multiply_reduce_fusion.4
  10.6 16.2 %shard_map.59 = f32[8,128]{1,0:T(8,128)} custom-call(f32[8,128]{1,0:T(8,128)} %scatter.16.x_ref), custom_call_target="tpu_custom_call" | custom-call | tf_op jit(solution)/shard_map/pallas_call | solution.py:80
  27.5 1.1 fusion.17
  29.3 6.3 %convert_bitcast_fusion.1 = bf16[64,32,512]{2,0,1:T(8,128)(2,1)} fusion(bf16[32,256,512]{2,1,0:T(8,128)(2,1)} %param.19, bf16[32,64,256]{2,1,0:T(8,128)(2,1)S(1)} %gather_fusion, pred[32]{0:T(512)(128)(4,1)S(1)} %compare_and_fusion.1), kind=kOutput, calls=%fused_computation.25 | convolution fusion | flops 538443776 | bytes 11534368 | tf_op jit(solution)/shard_map/cnr,nrk->cnk/dot_general | solution.py:309
  35.6 4.9 all-to-all-start.1
  41.8 25.1 %all-to-all-done.1 = bf16[64,32,512]{2,0,1:T(8,128)(2,1)S(1)} async-done(((bf16[64,32,512]{2,0,1:T(8,128)(2,1)}), bf16[64,32,512]{2,0,1:T(8,128)(2,1)S(1)}, u32[]{:S(2)}, u32[]{:S(2)}) %all-to-all-start.1) | async-done | bytes 2097184 | tf_op jit(solution)/shard_map/all_to_all | solution.py:312
  66.8 4.4 convolution_bitcast_fusion.1.x_ref
  71.3 82.7 %shard_map.60 = f32[64,48,512]{2,1,0:T(8,128)} custom-call(f32[64,48,512]{2,1,0:T(8,128)} %convolution_bitcast_fusion.1.x_ref), custom_call_target="tpu_custom_call" | custom-call | tf_op jit(solution)/shard_map/pallas_call | solution.py:257
  154.0 3.4 multiply_reduce_fusion.1
  158.0 9.2 %shard_map.61 = f32[8,128]{1,0:T(8,128)} custom-call(f32[8,128]{1,0:T(8,128)} %scatter.19.x_ref), custom_call_target="tpu_custom_call" | custom-call | tf_op jit(solution)/shard_map/pallas_call | solution.py:80
  167.9 3.8 fusion.36
  171.8 1.8 copy.29
  173.5 2.0 gather_fusion.1
  175.5 1.8 select_bitcast_fusion.2
  177.4 31.1 %all_to_all.30 = bf16[64,32,512]{2,0,1:T(8,128)(2,1)S(1)} all-to-all(bf16[64,32,512]{2,0,1:T(8,128)(2,1)S(1)} %select_bitcast_fusion.2), channel_id=1, replica_groups=mesh['ray'=16,'tile'=8] {'tile'}, dimensions={1} | all-to-all | bytes 4194304 | tf_op jit(solution)/shard_map/all_to_all | solution.py:294
  208.5 6.0 %fusion.40 = f32[32,64,256]{2,1,0:T(8,128)S(1)} fusion(bf16[64,32,512]{2,0,1:T(8,128)(2,1)S(1)} %all_to_all.30, bf16[32,256,512]{2,1,0:T(8,128)(2,1)} %param.19), kind=kOutput, calls=%fused_computation.76 | convolution fusion | flops 536870912 | bytes 12582912 | tf_op jit(solution)/shard_map/cnk,nrk->ncr/dot_general | solution.py:299
  214.6 2.0 fusion.5
  217.6 12.0 %shard_map.62 = f32[8,128]{1,0:T(8,128)} custom-call(f32[8,128]{1,0:T(8,128)} %scatter.20.x_ref), custom_call_target="tpu_custom_call" | custom-call | tf_op jit(solution)/shard_map/pallas_call | solution.py:80
  231.1 5.0 %convert_bitcast_fusion = bf16[64,32,512]{2,0,1:T(8,128)(2,1)S(1)} fusion(bf16[32,256,512]{2,1,0:T(8,128)(2,1)} %param.19, bf16[32,64,256]{2,1,0:T(8,128)(2,1)S(1)} %gather_fusion.2, pred[32]{0:T(512)(128)(4,1)S(1)} %compare_and_fusion.1), kind=kOutput, calls=%fused_computation.24 | convolution fusion | flops 538443776 | bytes 11534368 | tf_op jit(solution)/shard_map/cnr,nrk->cnk/dot_general | solution.py:309
  236.1 32.1 %all_to_all.31 = bf16[64,32,512]{2,0,1:T(8,128)(2,1)S(1)} all-to-all(bf16[64,32,512]{2,0,1:T(8,128)(2,1)S(1)} %convert_bitcast_fusion), channel_id=1, replica_groups=mesh['ray'=16,'tile'=8] {'tile'}, dimensions={1} | all-to-all | bytes 4194304 | tf_op jit(solution)/shard_map/all_to_all | solution.py:312
  268.2 4.4 convolution_bitcast_fusion.x_ref
  272.6 79.7 %shard_map.63 = f32[64,48,512]{2,1,0:T(8,128)} custom-call(f32[64,48,512]{2,1,0:T(8,128)} %convolution_bitcast_fusion.x_ref), custom_call_target="tpu_custom_call" | custom-call | tf_op jit(solution)/shard_map/pallas_call | solution.py:257
  352.4 5.4 %multiply_reduce_fusion = f32[64]{0:T(128)S(1)} fusion(f32[64,48,512]{2,1,0:T(8,128)} %shard_map.63, f32[64]{0:T(128)S(1)} %sqrt_bitcast_fusion.1, f32[64,48,512]{2,1,0:T(8,128)} %shard_map.60, f32[64]{0:T(128)S(1)} %sqrt_bitcast_fusion.2), kind=kLoop, calls=%fused_computation.6 | loop fusion | flops 7864256 | bytes 12583680 | tf_op jit(solution)/shard_map/reduce_sum | solution.py:320
  358.4 12.0 %shard_map.64 = f32[8,128]{1,0:T(8,128)} custom-call(f32[8,128]{1,0:T(8,128)} %scatter.21.x_ref), custom_call_target="tpu_custom_call" | custom-call | tf_op jit(solution)/shard_map/pallas_call | solution.py:80
  371.1 5.7 %fusion.8 = bf16[64,48,512]{2,1,0:T(8,128)(2,1)S(1)} fusion(f32[64]{0:T(128)S(1)} %sqrt_bitcast_fusion, f32[64,48,512]{2,1,0:T(8,128)} %shard_map.63, f32[64]{0:T(128)S(1)} %sqrt_bitcast_fusion.1, f32[64,48,512]{2,1,0:T(8,128)} %shard_map.60, f32[64]{0:T(128)S(1)} %sqrt_bitcast_fusion.2), kind=kLoop, calls=%fused_computation.26 | loop fusion | flops 7864320 | bytes 15729408 | tf_op jit(solution)/shard_map/convert_element_type | solution.py:338
  376.8 1.8 copy.33
  378.6 2.0 gather_fusion.3
  380.6 3.2 select_bitcast_fusion.1
  383.7 5.2 %all-to-all-start.4 = ((bf16[64,32,512]{2,0,1:T(8,128)(2,1)}), bf16[64,32,512]{2,0,1:T(8,128)(2,1)S(1)}, u32[]{:S(2)}, u32[]{:S(2)}) async-start(bf16[64,32,512]{2,0,1:T(8,128)(2,1)} %select_bitcast_fusion.1), calls=%async_computation.4 | async-start | bytes 4194304 | tf_op jit(solution)/shard_map/all_to_all | solution.py:294
  388.9 0.7 multiply_divide_fusion.2
  389.7 25.6 %all-to-all-done.4 = bf16[64,32,512]{2,0,1:T(8,128)(2,1)S(1)} async-done(((bf16[64,32,512]{2,0,1:T(8,128)(2,1)}), bf16[64,32,512]{2,0,1:T(8,128)(2,1)S(1)}, u32[]{:S(2)}, u32[]{:S(2)}) %all-to-all-start.4) | async-done | bytes 2097184 | tf_op jit(solution)/shard_map/all_to_all | solution.py:294
  415.2 6.0 %fusion.41 = f32[32,64,256]{2,1,0:T(8,128)S(1)} fusion(bf16[64,32,512]{2,0,1:T(8,128)(2,1)S(1)} %all-to-all-done.4, bf16[32,256,512]{2,1,0:T(8,128)(2,1)} %param.19), kind=kOutput, calls=%fused_computation.77 | convolution fusion | flops 536870912 | bytes 12582912 | tf_op jit(solution)/shard_map/cnk,nrk->ncr/dot_general | solution.py:299
  421.2 2.0 fusion.2
  424.2 12.1 %shard_map.65 = f32[8,128]{1,0:T(8,128)} custom-call(f32[8,128]{1,0:T(8,128)} %scatter.24.x_ref), custom_call_target="tpu_custom_call" | custom-call | tf_op jit(solution)/shard_map/pallas_call | solution.py:80
  436.4 0.7 multiply_divide_fusion.1
  437.8 7.8 %fusion.37 = (bf16[64,48,512]{2,1,0:T(8,128)(2,1)S(1)}, f32[64,48,512]{2,1,0:T(8,128)}) fusion(f32[64]{0:T(128)S(1)} %multiply_divide_fusion, f32[64]{0:T(128)S(1)} %sqrt_bitcast_fusion, f32[64,48,512]{2,1,0:T(8,128)} %shard_map.63, f32[64]{0:T(128)S(1)} %sqrt_bitcast_fusion.1, f32[64]{0:T(128)S(1)} %get-tuple-element.69, f32[64,48,512]{2,1,0:T(8,128)} %shard_map.60, ...), kind=kLoop, calls=%fused_computation.75 | loop fusion | flops 15728640 | bytes 22021632 | tf_op jit(solution)/shard_map/convert_element_type | solution.py:355
  445.6 1.8 copy.35
  447.4 2.0 gather_fusion.4
  449.4 3.2 select_bitcast_fusion
  452.6 5.5 %all-to-all-start.5 = ((bf16[64,32,512]{2,0,1:T(8,128)(2,1)}), bf16[64,32,512]{2,0,1:T(8,128)(2,1)S(1)}, u32[]{:S(2)}, u32[]{:S(2)}) async-start(bf16[64,32,512]{2,0,1:T(8,128)(2,1)} %select_bitcast_fusion), calls=%async_computation.5 | async-start | bytes 4194304 | tf_op jit(solution)/shard_map/all_to_all | solution.py:294
  458.1 9.1 %copy.41 = f32[8,8,48,512]{3,1,2,0:T(8,128)} copy(f32[8,8,48,512]{3,2,1,0:T(8,128)} %bitcast.96) | data formatting | bytes 12582912
  467.2 17.1 %all-to-all-done.5 = bf16[64,32,512]{2,0,1:T(8,128)(2,1)S(1)} async-done(((bf16[64,32,512]{2,0,1:T(8,128)(2,1)}), bf16[64,32,512]{2,0,1:T(8,128)(2,1)S(1)}, u32[]{:S(2)}, u32[]{:S(2)}) %all-to-all-start.5) | async-done | bytes 2097184 | tf_op jit(solution)/shard_map/all_to_all | solution.py:294
  484.4 6.0 %fusion.42 = f32[32,64,256]{2,1,0:T(8,128)S(1)} fusion(bf16[64,32,512]{2,0,1:T(8,128)(2,1)S(1)} %all-to-all-done.5, bf16[32,256,512]{2,1,0:T(8,128)(2,1)} %param.19), kind=kOutput, calls=%fused_computation.78 | convolution fusion | flops 536870912 | bytes 12582912 | tf_op jit(solution)/shard_map/cnk,nrk->ncr/dot_general | solution.py:299
  490.4 2.0 fusion
  492.5 0.9 sub.19
  (39 shorter events, 10.3 us)
Async XLA Ops:
  2.0 33.6 %all-to-all-start = ((s32[1,8,4]{2,0,1:T(1,128)}), s32[1,8,4]{2,0,1:T(1,128)S(1)}, u32[]{:S(2)}, u32[]{:S(2)}) async-start(s32[1,8,4]{2,0,1:T(1,128)} %copy.25), calls=%async_computation | async-start | bytes 8192 | tf_op jit(solution)/shard_map/all_to_all | solution.py:281
  35.6 31.2 %all-to-all-start.1 = ((bf16[64,32,512]{2,0,1:T(8,128)(2,1)}), bf16[64,32,512]{2,0,1:T(8,128)(2,1)S(1)}, u32[]{:S(2)}, u32[]{:S(2)}) async-start(bf16[64,32,512]{2,0,1:T(8,128)(2,1)} %convert_bitcast_fusion.1), calls=%async_computation.1 | async-start | bytes 4194304 | tf_op jit(solution)/shard_map/all_to_all | solution.py:312
  214.6 2.1 copy-start
  217.0 13.5 %copy-start.2 = (f32[64,2048]{1,0:T(8,128)}, f32[64,2048]{1,0:T(8,128)S(1)}, u32[]{:S(2)}) copy-start(f32[64,2048]{1,0:T(8,128)S(1)} %get-tuple-element.72) | copy-start | bytes 1572868
  383.7 31.5 %all-to-all-start.4 = ((bf16[64,32,512]{2,0,1:T(8,128)(2,1)}), bf16[64,32,512]{2,0,1:T(8,128)(2,1)S(1)}, u32[]{:S(2)}, u32[]{:S(2)}) async-start(bf16[64,32,512]{2,0,1:T(8,128)(2,1)} %select_bitcast_fusion.1), calls=%async_computation.4 | async-start | bytes 4194304 | tf_op jit(solution)/shard_map/all_to_all | solution.py:294
  421.2 2.1 copy-start.3
  452.6 31.8 %all-to-all-start.5 = ((bf16[64,32,512]{2,0,1:T(8,128)(2,1)}), bf16[64,32,512]{2,0,1:T(8,128)(2,1)S(1)}, u32[]{:S(2)}, u32[]{:S(2)}) async-start(bf16[64,32,512]{2,0,1:T(8,128)(2,1)} %select_bitcast_fusion), calls=%async_computation.5 | async-start | bytes 4194304 | tf_op jit(solution)/shard_map/all_to_all | solution.py:294
  490.4 2.1 copy-start.1

commit v8 on v6

--- a/solution.py
+++ b/solution.py
@@ -32,14 +32,6 @@
         coords = dict(here)
         coords[axis] = other
         return (coords["ray"], coords["tile"])
-
-    barrier = pltpu.get_barrier_semaphore()
-    count = 0
-    for axis, size, stride in plan:
-        for k in range(1, size):
-            pl.semaphore_signal(barrier, inc=1, device_id=peer(axis, size, stride, k), device_id_type=MESH)
-            count += 1
-    pl.semaphore_wait(barrier, count)
 
     vals[0, 0] = x_ref[...]
     copies = []
@@ -87,7 +79,7 @@
             pltpu.SemaphoreType.DMA((len(plan), depth)),
             pltpu.SemaphoreType.DMA((len(plan), depth)),
         ],
-        compiler_params=pltpu.CompilerParams(collective_id=collective_id, has_side_effects=True),
+        compiler_params=pltpu.CompilerParams(has_side_effects=True),
     )(block)
     return out[0, :width]
 

time: 495 us -> 523 us (1.057)
  Pallas kernels: 226 us -> 257 us
    pallas_call x5, Pallas kernels: 58.6 us -> 92.1 us  [group_sum(): pl.pallas_call(functools.partial(reduce_kernel, plan), out_shape=jax.Shap...]
  transfers between devices with their start and end apart: 3 -> 3, of which waited for: 2 -> 2; matrix products, arithmetic and copies ran while one was open for 3% -> 3% of each run, Pallas kernels for 3% -> 4%
where the time goes in v8:
time: 523 us; the launch traced here: 522 us
  Pallas kernels  257 us (49%)
  blocking collectives  90.5 us (17%)
  waiting for transfers between devices  50.7 us (10%)
  other arithmetic  41.2 us (8%)
  matrix products  38.7 us (7%)
  local copies, waits for them, and re-layouts  27.4 us (5%)
  starting transfers between devices  15.2 us (3%)
    pallas_call x2, Pallas kernels, ray_allreduce(): pl.pallas_call(functools.partial(allreduce_kernel, axes), out_shape=jax.S...  165 us
    pallas_call x5, Pallas kernels, group_sum(): pl.pallas_call(functools.partial(reduce_kernel, plan), out_shape=jax.Shap...  92.1 us
    all_to_all x2, blocking collectives, fetch(): lax.all_to_all(outgoing, 'tile', split_axis=1, concat_axis=1, tiled=True)  60 us
    all_to_all x1, blocking collectives, adjoint(): lax.all_to_all(terms, 'tile', split_axis=1, concat_axis=1, tiled=True)  30.4 us
    all_to_all x1, waiting for transfers between devices, fetch(): lax.all_to_all(outgoing, 'tile', split_axis=1, concat_axis=1, tiled=True)  25.6 us
    all_to_all x1, waiting for transfers between devices, adjoint(): lax.all_to_all(terms, 'tile', split_axis=1, concat_axis=1, tiled=True)  25.1 us
    dot_general x3, matrix products, forward(): jnp.einsum('cnk,nrk->ncr', tiles, sensitivity, preferred_element_type=jnp...  18.1 us
    unnamed x15, local copies, waits for them, and re-layouts  15.1 us
  transfers between devices with their start and end apart: 3, of which 2 were waited for; matrix products, arithmetic and copies ran while one was open for 3% of the time, Pallas kernels for 4%

profile of v8, /device:TPU:1, one launch (start us, length us, event | category | flops | bytes accessed | tf_op | source)
XLA Modules:
  0.0 522.1 jit_solution(9943722468596539150)
XLA Ops:
  0.6 1.3 copy.25
  2.0 6.0 %all-to-all-start = ((s32[1,8,4]{2,0,1:T(1,128)}), s32[1,8,4]{2,0,1:T(1,128)S(1)}, u32[]{:S(2)}, u32[]{:S(2)}) async-start(s32[1,8,4]{2,0,1:T(1,128)} %copy.25), calls=%async_computation | async-start | bytes 8192 | tf_op jit(solution)/shard_map/all_to_all | solution.py:275
  7.9 0.8 copy.26
  8.8 1.2 multiply_reduce_fusion.4
  10.6 22.7 %shard_map.59 = f32[8,128]{1,0:T(8,128)} custom-call(f32[8,128]{1,0:T(8,128)} %scatter.16.x_ref), custom_call_target="tpu_custom_call" | custom-call | tf_op jit(solution)/shard_map/pallas_call | solution.py:72
  34.0 1.1 fusion.19
  35.8 6.3 %convert_bitcast_fusion.1 = bf16[64,32,512]{2,0,1:T(8,128)(2,1)} fusion(bf16[32,256,512]{2,1,0:T(8,128)(2,1)} %param.19, bf16[32,64,256]{2,1,0:T(8,128)(2,1)S(1)} %gather_fusion, pred[32]{0:T(512)(128)(4,1)S(1)} %compare_and_fusion.1), kind=kOutput, calls=%fused_computation.28 | convolution fusion | flops 538443776 | bytes 11534368 | tf_op jit(solution)/shard_map/cnr,nrk->cnk/dot_general | solution.py:303
  42.1 5.0 all-to-all-start.1
  48.5 25.1 %all-to-all-done.1 = bf16[64,32,512]{2,0,1:T(8,128)(2,1)S(1)} async-done(((bf16[64,32,512]{2,0,1:T(8,128)(2,1)}), bf16[64,32,512]{2,0,1:T(8,128)(2,1)S(1)}, u32[]{:S(2)}, u32[]{:S(2)}) %all-to-all-start.1) | async-done | bytes 2097184 | tf_op jit(solution)/shard_map/all_to_all | solution.py:306
  73.5 1.7 fusion.8
  75.3 6.3 %copy.42 = f32[8,8,48,512]{3,1,2,0:T(8,128)} copy(f32[8,8,48,512]{3,2,1,0:T(8,128)S(1)} %bitcast.109) | data formatting | bytes 12582912
  81.5 84.5 %shard_map.60 = f32[64,24576]{1,0:T(8,128)} custom-call(f32[64,24576]{1,0:T(8,128)} %bitcast.110), custom_call_target="tpu_custom_call" | custom-call | tf_op jit(solution)/shard_map/pallas_call | solution.py:251
  166.0 3.3 multiply_reduce_fusion.1
  169.9 12.0 %shard_map.61 = f32[8,128]{1,0:T(8,128)} custom-call(f32[8,128]{1,0:T(8,128)} %scatter.19.x_ref), custom_call_target="tpu_custom_call" | custom-call | tf_op jit(solution)/shard_map/pallas_call | solution.py:72
  182.6 3.2 fusion.38
  186.3 2.0 gather_fusion.1
  188.3 1.8 select_bitcast_fusion.2
  190.2 29.6 %all_to_all.30 = bf16[64,32,512]{2,0,1:T(8,128)(2,1)S(1)} all-to-all(bf16[64,32,512]{2,0,1:T(8,128)(2,1)S(1)} %select_bitcast_fusion.2), channel_id=1, replica_groups=mesh['ray'=16,'tile'=8] {'tile'}, dimensions={1} | all-to-all | bytes 4194304 | tf_op jit(solution)/shard_map/all_to_all | solution.py:288
  219.8 6.0 %fusion.42 = f32[32,64,256]{2,1,0:T(8,128)S(1)} fusion(bf16[64,32,512]{2,0,1:T(8,128)(2,1)S(1)} %all_to_all.30, bf16[32,256,512]{2,1,0:T(8,128)(2,1)} %param.19), kind=kOutput, calls=%fused_computation.79 | convolution fusion | flops 536870912 | bytes 12582912 | tf_op jit(solution)/shard_map/cnk,nrk->ncr/dot_general | solution.py:293
  225.8 2.0 fusion.6
  228.9 20.8 %shard_map.62 = f32[8,128]{1,0:T(8,128)} custom-call(f32[8,128]{1,0:T(8,128)} %scatter.20.x_ref), custom_call_target="tpu_custom_call" | custom-call | tf_op jit(solution)/shard_map/pallas_call | solution.py:72
  249.6 0.7 sqrt_bitcast_fusion.1
  251.1 5.0 convert_bitcast_fusion
  256.1 30.4 %all_to_all.31 = bf16[64,32,512]{2,0,1:T(8,128)(2,1)S(1)} all-to-all(bf16[64,32,512]{2,0,1:T(8,128)(2,1)S(1)} %convert_bitcast_fusion), channel_id=1, replica_groups=mesh['ray'=16,'tile'=8] {'tile'}, dimensions={1} | all-to-all | bytes 4194304 | tf_op jit(solution)/shard_map/all_to_all | solution.py:306
  286.6 1.7 fusion.4
  288.3 6.3 %copy.44 = f32[8,8,48,512]{3,1,2,0:T(8,128)} copy(f32[8,8,48,512]{3,2,1,0:T(8,128)S(1)} %bitcast.108) | data formatting | bytes 12582912
  294.6 80.9 %shard_map.63 = f32[64,24576]{1,0:T(8,128)} custom-call(f32[64,24576]{1,0:T(8,128)} %bitcast.111), custom_call_target="tpu_custom_call" | custom-call | tf_op jit(solution)/shard_map/pallas_call | solution.py:251
  375.4 5.8 %multiply_reduce_fusion = f32[64]{0:T(128)S(1)} fusion(f32[64,24576]{1,0:T(8,128)} %shard_map.63, f32[64]{0:T(128)S(1)} %sqrt_bitcast_fusion.1, f32[64,24576]{1,0:T(8,128)} %shard_map.60, f32[64]{0:T(128)S(1)} %sqrt_bitcast_fusion.2), kind=kLoop, calls=%fused_computation.6 | loop fusion | flops 7864256 | bytes 12583680 | tf_op jit(solution)/shard_map/reduce_sum | solution.py:314
  381.8 15.9 %shard_map.64 = f32[8,128]{1,0:T(8,128)} custom-call(f32[8,128]{1,0:T(8,128)} %scatter.21.x_ref), custom_call_target="tpu_custom_call" | custom-call | tf_op jit(solution)/shard_map/pallas_call | solution.py:72
  397.7 0.7 sqrt_bitcast_fusion
  398.4 5.2 fusion.10
  404.1 2.0 gather_fusion.3
  406.1 3.2 select_bitcast_fusion.1
  409.3 4.2 all-to-all-start.4
  413.5 0.7 multiply_divide_fusion.2
  414.2 25.6 %all-to-all-done.4 = bf16[64,32,512]{2,0,1:T(8,128)(2,1)S(1)} async-done(((bf16[64,32,512]{2,0,1:T(8,128)(2,1)}), bf16[64,32,512]{2,0,1:T(8,128)(2,1)S(1)}, u32[]{:S(2)}, u32[]{:S(2)}) %all-to-all-start.4) | async-done | bytes 2097184 | tf_op jit(solution)/shard_map/all_to_all | solution.py:288
  439.8 6.0 %fusion.43 = f32[32,64,256]{2,1,0:T(8,128)S(1)} fusion(bf16[64,32,512]{2,0,1:T(8,128)(2,1)S(1)} %all-to-all-done.4, bf16[32,256,512]{2,1,0:T(8,128)(2,1)} %param.19), kind=kOutput, calls=%fused_computation.80 | convolution fusion | flops 536870912 | bytes 12582912 | tf_op jit(solution)/shard_map/cnk,nrk->ncr/dot_general | solution.py:293
  445.8 2.0 fusion.2
  448.8 20.6 %shard_map.65 = f32[8,128]{1,0:T(8,128)} custom-call(f32[8,128]{1,0:T(8,128)} %scatter.24.x_ref), custom_call_target="tpu_custom_call" | custom-call | tf_op jit(solution)/shard_map/pallas_call | solution.py:72
  469.5 0.7 multiply_divide_fusion.1
  470.2 0.7 multiply_divide_fusion
  470.9 7.4 %fusion.39 = (bf16[64,24576]{1,0:T(8,128)(2,1)S(1)}, f32[64,24576]{1,0:T(8,128)}) fusion(f32[64]{0:T(128)S(1)} %multiply_divide_fusion, f32[64]{0:T(128)S(1)} %sqrt_bitcast_fusion, f32[64,24576]{1,0:T(8,128)} %shard_map.63, f32[64]{0:T(128)S(1)} %sqrt_bitcast_fusion.1, f32[64]{0:T(128)S(1)} %get-tuple-element.69, f32[64,24576]{1,0:T(8,128)} %shard_map.60, ...), kind=kLoop, calls=%fused_computation.78 | loop fusion | flops 15728640 | bytes 22021632 | tf_op jit(solution)/shard_map/convert_element_type | solution.py:349
  478.7 2.0 gather_fusion.4
  480.7 1.8 select_bitcast_fusion
  482.6 30.4 %all_to_all.32 = bf16[64,32,512]{2,0,1:T(8,128)(2,1)S(1)} all-to-all(bf16[64,32,512]{2,0,1:T(8,128)(2,1)S(1)} %select_bitcast_fusion), channel_id=1, replica_groups=mesh['ray'=16,'tile'=8] {'tile'}, dimensions={1} | all-to-all | bytes 4194304 | tf_op jit(solution)/shard_map/all_to_all | solution.py:288
  513.0 6.0 %fusion.44 = f32[32,64,256]{2,1,0:T(8,128)S(1)} fusion(bf16[64,32,512]{2,0,1:T(8,128)(2,1)S(1)} %all_to_all.32, bf16[32,256,512]{2,1,0:T(8,128)(2,1)} %param.19), kind=kOutput, calls=%fused_computation.81 | convolution fusion | flops 536870912 | bytes 12582912 | tf_op jit(solution)/shard_map/cnk,nrk->ncr/dot_general | solution.py:293
  519.1 2.0 fusion
  521.2 0.9 sub.19
  (39 shorter events, 9.4 us)
Async XLA Ops:
  2.0 40.1 %all-to-all-start = ((s32[1,8,4]{2,0,1:T(1,128)}), s32[1,8,4]{2,0,1:T(1,128)S(1)}, u32[]{:S(2)}, u32[]{:S(2)}) async-start(s32[1,8,4]{2,0,1:T(1,128)} %copy.25), calls=%async_computation | async-start | bytes 8192 | tf_op jit(solution)/shard_map/all_to_all | solution.py:275
  42.1 31.4 %all-to-all-start.1 = ((bf16[64,32,512]{2,0,1:T(8,128)(2,1)}), bf16[64,32,512]{2,0,1:T(8,128)(2,1)S(1)}, u32[]{:S(2)}, u32[]{:S(2)}) async-start(bf16[64,32,512]{2,0,1:T(8,128)(2,1)} %convert_bitcast_fusion.1), calls=%async_computation.1 | async-start | bytes 4194304 | tf_op jit(solution)/shard_map/all_to_all | solution.py:306
  225.8 2.1 copy-start
  228.2 22.3 %copy-start.2 = (f32[64,2048]{1,0:T(8,128)}, f32[64,2048]{1,0:T(8,128)S(1)}, u32[]{:S(2)}) copy-start(f32[64,2048]{1,0:T(8,128)S(1)} %get-tuple-element.72) | copy-start | bytes 1572868
  409.3 30.5 %all-to-all-start.4 = ((bf16[64,32,512]{2,0,1:T(8,128)(2,1)}), bf16[64,32,512]{2,0,1:T(8,128)(2,1)S(1)}, u32[]{:S(2)}, u32[]{:S(2)}) async-start(bf16[64,32,512]{2,0,1:T(8,128)(2,1)} %select_bitcast_fusion.1), calls=%async_computation.4 | async-start | bytes 4194304 | tf_op jit(solution)/shard_map/all_to_all | solution.py:288
  445.8 2.1 copy-start.3
  519.0 2.1 copy-start.1

commit v9 on v6

--- a/solution.py
+++ b/solution.py
@@ -36,40 +36,48 @@
     barrier = pltpu.get_barrier_semaphore()
     count = 0
     for axis, size, stride in plan:
-        for k in range(1, size):
+        def greet(k, carry, axis=axis, size=size, stride=stride):
             pl.semaphore_signal(barrier, inc=1, device_id=peer(axis, size, stride, k), device_id_type=MESH)
-            count += 1
+            return carry
+        lax.fori_loop(1, size, greet, 0)
+        count += size - 1
     pl.semaphore_wait(barrier, count)
 
-    vals[0, 0] = x_ref[...]
-    copies = []
+    def copy_of(s, axis, size, stride, k):
+        src = x_ref if s == 0 else vals.at[s, 0]
+        return pltpu.make_async_remote_copy(
+            src_ref=src,
+            dst_ref=vals.at[s, k],
+            send_sem=send_sems.at[s, k],
+            recv_sem=recv_sems.at[s, k],
+            device_id=peer(axis, size, stride, (size - k) % size),
+            device_id_type=MESH,
+        )
+
     for s, (axis, size, stride) in enumerate(plan):
-        src = x_ref if s == 0 else vals.at[s, 0]
-        stage_copies = []
-        for k in range(1, size):
-            copy = pltpu.make_async_remote_copy(
-                src_ref=src,
-                dst_ref=vals.at[s, k],
-                send_sem=send_sems.at[s, k],
-                recv_sem=recv_sems.at[s, k],
-                device_id=peer(axis, size, stride, (size - k) % size),
-                device_id_type=MESH,
-            )
-            copy.start()
-            stage_copies.append(copy)
-        for copy in stage_copies:
-            copy.wait_recv()
-        copies += stage_copies
+        def start(k, carry, s=s, axis=axis, size=size, stride=stride):
+            copy_of(s, axis, size, stride, k).start()
+            return carry
+
+        def arrive(k, carry, s=s, axis=axis, size=size, stride=stride):
+            copy_of(s, axis, size, stride, k).wait_recv()
+            return carry
+        lax.fori_loop(1, size, start, 0)
+        lax.fori_loop(1, size, arrive, 0)
         pos = (here[axis] // stride) % size
-        total = vals[s, (size - pos) % size]
+        own = x_ref[...] if s == 0 else vals[s, 0]
+        total = jnp.where(pos == 0, own, vals[s, (size - pos) % size])
         for q in range(1, size):
-            total = total + vals[s, (q - pos + size) % size]
+            total = total + jnp.where(pos == q, own, vals[s, (q - pos + size) % size])
         if s + 1 < len(plan):
             vals[s + 1, 0] = total
         else:
             o_ref[...] = total
-    for copy in copies:
-        copy.wait_send()
+    for s, (axis, size, stride) in enumerate(plan):
+        def sent(k, carry, s=s, axis=axis, size=size, stride=stride):
+            copy_of(s, axis, size, stride, k).wait_send()
+            return carry
+        lax.fori_loop(1, size, sent, 0)
 
 
 def group_sum(mesh, axes, collective_id, partial):

time: 495 us -> 496 us (level)
  no operation moved by 1% of the time
where the time goes in v9:
time: 496 us; the launch traced here: 494 us
  Pallas kernels  226 us (46%)
  blocking collectives  93.4 us (19%)
  waiting for transfers between devices  50.7 us (10%)
  other arithmetic  41.2 us (8%)
  matrix products  38.7 us (8%)
  local copies, waits for them, and re-layouts  27.4 us (6%)
  starting transfers between devices  15.8 us (3%)
    pallas_call x2, Pallas kernels, ray_allreduce(): pl.pallas_call(functools.partial(allreduce_kernel, axes), out_shape=jax.S...  166 us
    all_to_all x2, blocking collectives, fetch(): lax.all_to_all(outgoing, 'tile', split_axis=1, concat_axis=1, tiled=True)  61.9 us
    pallas_call x5, Pallas kernels, group_sum(): pl.pallas_call(functools.partial(reduce_kernel, plan), out_shape=jax.Shap...  60.3 us
    all_to_all x1, blocking collectives, adjoint(): lax.all_to_all(terms, 'tile', split_axis=1, concat_axis=1, tiled=True)  31.6 us
    all_to_all x1, waiting for transfers between devices, fetch(): lax.all_to_all(outgoing, 'tile', split_axis=1, concat_axis=1, tiled=True)  25.6 us
    all_to_all x1, waiting for transfers between devices, adjoint(): lax.all_to_all(terms, 'tile', split_axis=1, concat_axis=1, tiled=True)  25.1 us
    dot_general x3, matrix products, forward(): jnp.einsum('cnk,nrk->ncr', tiles, sensitivity, preferred_element_type=jnp...  18.1 us
    unnamed x15, local copies, waits for them, and re-layouts  15.1 us
  transfers between devices with their start and end apart: 3, of which 2 were waited for; matrix products, arithmetic and copies ran while one was open for 3% of the time, Pallas kernels for 3%

profile of v9, /device:TPU:1, one launch (start us, length us, event | category | flops | bytes accessed | tf_op | source)
XLA Modules:
  0.0 494.3 jit_solution(17682292069274692049)
XLA Ops:
  0.6 1.3 copy.25
  2.0 6.0 %all-to-all-start = ((s32[1,8,4]{2,0,1:T(1,128)}), s32[1,8,4]{2,0,1:T(1,128)S(1)}, u32[]{:S(2)}, u32[]{:S(2)}) async-start(s32[1,8,4]{2,0,1:T(1,128)} %copy.25), calls=%async_computation | async-start | bytes 8192 | tf_op jit(solution)/shard_map/all_to_all | solution.py:291
  7.9 0.8 copy.26
  8.8 1.2 multiply_reduce_fusion.4
  10.6 16.4 %shard_map.59 = f32[8,128]{1,0:T(8,128)} custom-call(f32[8,128]{1,0:T(8,128)} %scatter.16.x_ref), custom_call_target="tpu_custom_call" | custom-call | tf_op jit(solution)/shard_map/pallas_call | solution.py:88
  27.7 1.1 fusion.19
  29.5 6.3 %convert_bitcast_fusion.1 = bf16[64,32,512]{2,0,1:T(8,128)(2,1)} fusion(bf16[32,256,512]{2,1,0:T(8,128)(2,1)} %param.19, bf16[32,64,256]{2,1,0:T(8,128)(2,1)S(1)} %gather_fusion, pred[32]{0:T(512)(128)(4,1)S(1)} %compare_and_fusion.1), kind=kOutput, calls=%fused_computation.28 | convolution fusion | flops 538443776 | bytes 11534368 | tf_op jit(solution)/shard_map/cnr,nrk->cnk/dot_general | solution.py:319
  35.9 4.9 all-to-all-start.1
  42.0 25.1 %all-to-all-done.1 = bf16[64,32,512]{2,0,1:T(8,128)(2,1)S(1)} async-done(((bf16[64,32,512]{2,0,1:T(8,128)(2,1)}), bf16[64,32,512]{2,0,1:T(8,128)(2,1)S(1)}, u32[]{:S(2)}, u32[]{:S(2)}) %all-to-all-start.1) | async-done | bytes 2097184 | tf_op jit(solution)/shard_map/all_to_all | solution.py:322
  67.1 1.7 fusion.8
  68.9 6.3 %copy.42 = f32[8,8,48,512]{3,1,2,0:T(8,128)} copy(f32[8,8,48,512]{3,2,1,0:T(8,128)S(1)} %bitcast.109) | data formatting | bytes 12582912
  75.1 84.5 %shard_map.60 = f32[64,24576]{1,0:T(8,128)} custom-call(f32[64,24576]{1,0:T(8,128)} %bitcast.110), custom_call_target="tpu_custom_call" | custom-call | tf_op jit(solution)/shard_map/pallas_call | solution.py:267
  159.6 3.3 multiply_reduce_fusion.1
  163.6 8.3 %shard_map.61 = f32[8,128]{1,0:T(8,128)} custom-call(f32[8,128]{1,0:T(8,128)} %scatter.19.x_ref), custom_call_target="tpu_custom_call" | custom-call | tf_op jit(solution)/shard_map/pallas_call | solution.py:88
  172.5 3.2 fusion.38
  176.2 2.0 gather_fusion.1
  178.2 1.8 select_bitcast_fusion.2
  180.1 30.4 %all_to_all.30 = bf16[64,32,512]{2,0,1:T(8,128)(2,1)S(1)} all-to-all(bf16[64,32,512]{2,0,1:T(8,128)(2,1)S(1)} %select_bitcast_fusion.2), channel_id=1, replica_groups=mesh['ray'=16,'tile'=8] {'tile'}, dimensions={1} | all-to-all | bytes 4194304 | tf_op jit(solution)/shard_map/all_to_all | solution.py:304
  210.4 6.0 %fusion.42 = f32[32,64,256]{2,1,0:T(8,128)S(1)} fusion(bf16[64,32,512]{2,0,1:T(8,128)(2,1)S(1)} %all_to_all.30, bf16[32,256,512]{2,1,0:T(8,128)(2,1)} %param.19), kind=kOutput, calls=%fused_computation.79 | convolution fusion | flops 536870912 | bytes 12582912 | tf_op jit(solution)/shard_map/cnk,nrk->ncr/dot_general | solution.py:309
  216.5 2.0 fusion.6
  219.5 12.2 %shard_map.62 = f32[8,128]{1,0:T(8,128)} custom-call(f32[8,128]{1,0:T(8,128)} %scatter.20.x_ref), custom_call_target="tpu_custom_call" | custom-call | tf_op jit(solution)/shard_map/pallas_call | solution.py:88
  231.8 0.7 sqrt_bitcast_fusion.1
  233.2 5.0 %convert_bitcast_fusion = bf16[64,32,512]{2,0,1:T(8,128)(2,1)S(1)} fusion(bf16[32,256,512]{2,1,0:T(8,128)(2,1)} %param.19, bf16[32,64,256]{2,1,0:T(8,128)(2,1)S(1)} %gather_fusion.2, pred[32]{0:T(512)(128)(4,1)S(1)} %compare_and_fusion.1), kind=kOutput, calls=%fused_computation.27 | convolution fusion | flops 538443776 | bytes 11534368 | tf_op jit(solution)/shard_map/cnr,nrk->cnk/dot_general | solution.py:319
  238.2 31.6 %all_to_all.31 = bf16[64,32,512]{2,0,1:T(8,128)(2,1)S(1)} all-to-all(bf16[64,32,512]{2,0,1:T(8,128)(2,1)S(1)} %convert_bitcast_fusion), channel_id=1, replica_groups=mesh['ray'=16,'tile'=8] {'tile'}, dimensions={1} | all-to-all | bytes 4194304 | tf_op jit(solution)/shard_map/all_to_all | solution.py:322
  269.8 1.7 fusion.4
  271.5 6.3 %copy.44 = f32[8,8,48,512]{3,1,2,0:T(8,128)} copy(f32[8,8,48,512]{3,2,1,0:T(8,128)S(1)} %bitcast.108) | data formatting | bytes 12582912
  277.8 81.2 %shard_map.63 = f32[64,24576]{1,0:T(8,128)} custom-call(f32[64,24576]{1,0:T(8,128)} %bitcast.111), custom_call_target="tpu_custom_call" | custom-call | tf_op jit(solution)/shard_map/pallas_call | solution.py:267
  359.0 5.8 %multiply_reduce_fusion = f32[64]{0:T(128)S(1)} fusion(f32[64,24576]{1,0:T(8,128)} %shard_map.63, f32[64]{0:T(128)S(1)} %sqrt_bitcast_fusion.1, f32[64,24576]{1,0:T(8,128)} %shard_map.60, f32[64]{0:T(128)S(1)} %sqrt_bitcast_fusion.2), kind=kLoop, calls=%fused_computation.6 | loop fusion | flops 7864256 | bytes 12583680 | tf_op jit(solution)/shard_map/reduce_sum | solution.py:330
  365.4 11.1 %shard_map.64 = f32[8,128]{1,0:T(8,128)} custom-call(f32[8,128]{1,0:T(8,128)} %scatter.21.x_ref), custom_call_target="tpu_custom_call" | custom-call | tf_op jit(solution)/shard_map/pallas_call | solution.py:88
  376.5 0.7 sqrt_bitcast_fusion
  377.1 5.2 %fusion.10 = bf16[64,24576]{1,0:T(8,128)(2,1)S(1)} fusion(f32[64]{0:T(128)S(1)} %sqrt_bitcast_fusion, f32[64,24576]{1,0:T(8,128)} %shard_map.63, f32[64]{0:T(128)S(1)} %sqrt_bitcast_fusion.1, f32[64,24576]{1,0:T(8,128)} %shard_map.60, f32[64]{0:T(128)S(1)} %sqrt_bitcast_fusion.2), kind=kLoop, calls=%fused_computation.29 | loop fusion | flops 7864320 | bytes 15729408 | tf_op jit(solution)/shard_map/convert_element_type | solution.py:348
  382.8 2.0 gather_fusion.3
  384.8 3.2 select_bitcast_fusion.1
  388.0 5.0 %all-to-all-start.4 = ((bf16[64,32,512]{2,0,1:T(8,128)(2,1)}), bf16[64,32,512]{2,0,1:T(8,128)(2,1)S(1)}, u32[]{:S(2)}, u32[]{:S(2)}) async-start(bf16[64,32,512]{2,0,1:T(8,128)(2,1)} %select_bitcast_fusion.1), calls=%async_computation.4 | async-start | bytes 4194304 | tf_op jit(solution)/shard_map/all_to_all | solution.py:304
  392.9 0.7 multiply_divide_fusion.2
  393.7 25.6 %all-to-all-done.4 = bf16[64,32,512]{2,0,1:T(8,128)(2,1)S(1)} async-done(((bf16[64,32,512]{2,0,1:T(8,128)(2,1)}), bf16[64,32,512]{2,0,1:T(8,128)(2,1)S(1)}, u32[]{:S(2)}, u32[]{:S(2)}) %all-to-all-start.4) | async-done | bytes 2097184 | tf_op jit(solution)/shard_map/all_to_all | solution.py:304
  419.3 6.0 %fusion.43 = f32[32,64,256]{2,1,0:T(8,128)S(1)} fusion(bf16[64,32,512]{2,0,1:T(8,128)(2,1)S(1)} %all-to-all-done.4, bf16[32,256,512]{2,1,0:T(8,128)(2,1)} %param.19), kind=kOutput, calls=%fused_computation.80 | convolution fusion | flops 536870912 | bytes 12582912 | tf_op jit(solution)/shard_map/cnk,nrk->ncr/dot_general | solution.py:309
  425.3 2.0 fusion.2
  428.3 12.3 %shard_map.65 = f32[8,128]{1,0:T(8,128)} custom-call(f32[8,128]{1,0:T(8,128)} %scatter.24.x_ref), custom_call_target="tpu_custom_call" | custom-call | tf_op jit(solution)/shard_map/pallas_call | solution.py:88
  440.6 0.7 multiply_divide_fusion.1
  441.4 0.7 multiply_divide_fusion
  442.1 7.4 %fusion.39 = (bf16[64,24576]{1,0:T(8,128)(2,1)S(1)}, f32[64,24576]{1,0:T(8,128)}) fusion(f32[64]{0:T(128)S(1)} %multiply_divide_fusion, f32[64]{0:T(128)S(1)} %sqrt_bitcast_fusion, f32[64,24576]{1,0:T(8,128)} %shard_map.63, f32[64]{0:T(128)S(1)} %sqrt_bitcast_fusion.1, f32[64]{0:T(128)S(1)} %get-tuple-element.69, f32[64,24576]{1,0:T(8,128)} %shard_map.60, ...), kind=kLoop, calls=%fused_computation.78 | loop fusion | flops 15728640 | bytes 22021632 | tf_op jit(solution)/shard_map/convert_element_type | solution.py:365
  449.8 2.0 gather_fusion.4
  451.9 1.8 select_bitcast_fusion
  453.7 31.5 %all_to_all.32 = bf16[64,32,512]{2,0,1:T(8,128)(2,1)S(1)} all-to-all(bf16[64,32,512]{2,0,1:T(8,128)(2,1)S(1)} %select_bitcast_fusion), channel_id=1, replica_groups=mesh['ray'=16,'tile'=8] {'tile'}, dimensions={1} | all-to-all | bytes 4194304 | tf_op jit(solution)/shard_map/all_to_all | solution.py:304
  485.2 6.0 %fusion.44 = f32[32,64,256]{2,1,0:T(8,128)S(1)} fusion(bf16[64,32,512]{2,0,1:T(8,128)(2,1)S(1)} %all_to_all.32, bf16[32,256,512]{2,1,0:T(8,128)(2,1)} %param.19), kind=kOutput, calls=%fused_computation.81 | convolution fusion | flops 536870912 | bytes 12582912 | tf_op jit(solution)/shard_map/cnk,nrk->ncr/dot_general | solution.py:309
  491.2 2.0 fusion
  493.4 0.9 sub.19
  (39 shorter events, 9.4 us)
Async XLA Ops:
  2.0 33.9 %all-to-all-start = ((s32[1,8,4]{2,0,1:T(1,128)}), s32[1,8,4]{2,0,1:T(1,128)S(1)}, u32[]{:S(2)}, u32[]{:S(2)}) async-start(s32[1,8,4]{2,0,1:T(1,128)} %copy.25), calls=%async_computation | async-start | bytes 8192 | tf_op jit(solution)/shard_map/all_to_all | solution.py:291
  35.9 31.3 %all-to-all-start.1 = ((bf16[64,32,512]{2,0,1:T(8,128)(2,1)}), bf16[64,32,512]{2,0,1:T(8,128)(2,1)S(1)}, u32[]{:S(2)}, u32[]{:S(2)}) async-start(bf16[64,32,512]{2,0,1:T(8,128)(2,1)} %convert_bitcast_fusion.1), calls=%async_computation.1 | async-start | bytes 4194304 | tf_op jit(solution)/shard_map/all_to_all | solution.py:322
  216.5 2.1 copy-start
  218.9 13.7 %copy-start.2 = (f32[64,2048]{1,0:T(8,128)}, f32[64,2048]{1,0:T(8,128)S(1)}, u32[]{:S(2)}) copy-start(f32[64,2048]{1,0:T(8,128)S(1)} %get-tuple-element.72) | copy-start | bytes 1572868
  388.0 31.3 %all-to-all-start.4 = ((bf16[64,32,512]{2,0,1:T(8,128)(2,1)}), bf16[64,32,512]{2,0,1:T(8,128)(2,1)S(1)}, u32[]{:S(2)}, u32[]{:S(2)}) async-start(bf16[64,32,512]{2,0,1:T(8,128)(2,1)} %select_bitcast_fusion.1), calls=%async_computation.4 | async-start | bytes 4194304 | tf_op jit(solution)/shard_map/all_to_all | solution.py:304
  425.3 2.1 copy-start.3
  491.2 2.1 copy-start.1

commit v10 on v6

--- a/solution.py
+++ b/solution.py
@@ -240,11 +240,11 @@
                      lambda j, h=h: part.at[h, :, cols(j * w2, w2)],
                      o_ref.at[:, cols(base + p2 * w2, w2)]))
         seg3.append((a2, lambda j, base=base: o_ref.at[:, cols(base + j * w2, w2)]))
-        seg4.append((a1, lambda j, d, h=h: o_ref.at[:, cols(h * half + j * w1 + d * q1, q1)]))
+        seg4.append((a1, lambda j, h=h: o_ref.at[:, cols(h * half + j * w1, w1)]))
     reduce_scatter(0, seg1, rbuf1, acc1)
     direct_reduce_scatter(1, seg2, rbuf2, w2)
     direct_all_gather(2, seg3)
-    all_gather(3, seg4)
+    direct_all_gather(3, seg4)
     for copy in sends:
         copy.wait_send()
 

time: 495 us -> 512 us (1.034)
  Pallas kernels: 226 us -> 244 us
    pallas_call x2, Pallas kernels: 167 us -> 181 us  [ray_allreduce(): pl.pallas_call(functools.partial(allreduce_kernel, axes), out_shape=jax.S...]
where the time goes in v10:
time: 512 us; the launch traced here: 511 us
  Pallas kernels  244 us (48%)
  blocking collectives  92 us (18%)
  waiting for transfers between devices  50.7 us (10%)
  other arithmetic  41.2 us (8%)
  matrix products  38.7 us (8%)
  local copies, waits for them, and re-layouts  27.4 us (5%)
  starting transfers between devices  15.8 us (3%)
    pallas_call x2, Pallas kernels, ray_allreduce(): pl.pallas_call(functools.partial(allreduce_kernel, axes), out_shape=jax.S...  181 us
    pallas_call x5, Pallas kernels, group_sum(): pl.pallas_call(functools.partial(reduce_kernel, plan), out_shape=jax.Shap...  63.2 us
    all_to_all x2, blocking collectives, fetch(): lax.all_to_all(outgoing, 'tile', split_axis=1, concat_axis=1, tiled=True)  61.1 us
    all_to_all x1, blocking collectives, adjoint(): lax.all_to_all(terms, 'tile', split_axis=1, concat_axis=1, tiled=True)  30.9 us
    all_to_all x1, waiting for transfers between devices, fetch(): lax.all_to_all(outgoing, 'tile', split_axis=1, concat_axis=1, tiled=True)  25.6 us
    all_to_all x1, waiting for transfers between devices, adjoint(): lax.all_to_all(terms, 'tile', split_axis=1, concat_axis=1, tiled=True)  25.1 us
    dot_general x3, matrix products, forward(): jnp.einsum('cnk,nrk->ncr', tiles, sensitivity, preferred_element_type=jnp...  18.1 us
    unnamed x15, local copies, waits for them, and re-layouts  15.1 us
  transfers between devices with their start and end apart: 3, of which 2 were waited for; matrix products, arithmetic and copies ran while one was open for 3% of the time, Pallas kernels for 3%

profile of v10, /device:TPU:1, one launch (start us, length us, event | category | flops | bytes accessed | tf_op | source)
XLA Modules:
  0.0 510.5 jit_solution(4089739363302289288)
XLA Ops:
  0.6 1.3 copy.25
  2.0 6.0 %all-to-all-start = ((s32[1,8,4]{2,0,1:T(1,128)}), s32[1,8,4]{2,0,1:T(1,128)S(1)}, u32[]{:S(2)}, u32[]{:S(2)}) async-start(s32[1,8,4]{2,0,1:T(1,128)} %copy.25), calls=%async_computation | async-start | bytes 8192 | tf_op jit(solution)/shard_map/all_to_all | solution.py:283
  7.9 0.8 copy.26
  8.8 1.2 multiply_reduce_fusion.4
  10.6 16.2 %shard_map.59 = f32[8,128]{1,0:T(8,128)} custom-call(f32[8,128]{1,0:T(8,128)} %scatter.16.x_ref), custom_call_target="tpu_custom_call" | custom-call | tf_op jit(solution)/shard_map/pallas_call | solution.py:80
  27.5 1.1 fusion.19
  29.3 6.3 %convert_bitcast_fusion.1 = bf16[64,32,512]{2,0,1:T(8,128)(2,1)} fusion(bf16[32,256,512]{2,1,0:T(8,128)(2,1)} %param.19, bf16[32,64,256]{2,1,0:T(8,128)(2,1)S(1)} %gather_fusion, pred[32]{0:T(512)(128)(4,1)S(1)} %compare_and_fusion.1), kind=kOutput, calls=%fused_computation.28 | convolution fusion | flops 538443776 | bytes 11534368 | tf_op jit(solution)/shard_map/cnr,nrk->cnk/dot_general | solution.py:311
  35.6 4.9 all-to-all-start.1
  41.8 25.1 %all-to-all-done.1 = bf16[64,32,512]{2,0,1:T(8,128)(2,1)S(1)} async-done(((bf16[64,32,512]{2,0,1:T(8,128)(2,1)}), bf16[64,32,512]{2,0,1:T(8,128)(2,1)S(1)}, u32[]{:S(2)}, u32[]{:S(2)}) %all-to-all-start.1) | async-done | bytes 2097184 | tf_op jit(solution)/shard_map/all_to_all | solution.py:314
  66.8 1.7 fusion.8
  68.6 6.3 %copy.42 = f32[8,8,48,512]{3,1,2,0:T(8,128)} copy(f32[8,8,48,512]{3,2,1,0:T(8,128)S(1)} %bitcast.109) | data formatting | bytes 12582912
  74.8 90.5 %shard_map.60 = f32[64,24576]{1,0:T(8,128)} custom-call(f32[64,24576]{1,0:T(8,128)} %bitcast.110), custom_call_target="tpu_custom_call" | custom-call | tf_op jit(solution)/shard_map/pallas_call | solution.py:259
  165.4 3.3 multiply_reduce_fusion.1
  169.3 8.0 %shard_map.61 = f32[8,128]{1,0:T(8,128)} custom-call(f32[8,128]{1,0:T(8,128)} %scatter.19.x_ref), custom_call_target="tpu_custom_call" | custom-call | tf_op jit(solution)/shard_map/pallas_call | solution.py:80
  178.0 3.2 fusion.38
  181.7 2.0 gather_fusion.1
  183.7 1.8 select_bitcast_fusion.2
  185.5 29.8 %all_to_all.30 = bf16[64,32,512]{2,0,1:T(8,128)(2,1)S(1)} all-to-all(bf16[64,32,512]{2,0,1:T(8,128)(2,1)S(1)} %select_bitcast_fusion.2), channel_id=1, replica_groups=mesh['ray'=16,'tile'=8] {'tile'}, dimensions={1} | all-to-all | bytes 4194304 | tf_op jit(solution)/shard_map/all_to_all | solution.py:296
  215.4 6.0 %fusion.42 = f32[32,64,256]{2,1,0:T(8,128)S(1)} fusion(bf16[64,32,512]{2,0,1:T(8,128)(2,1)S(1)} %all_to_all.30, bf16[32,256,512]{2,1,0:T(8,128)(2,1)} %param.19), kind=kOutput, calls=%fused_computation.79 | convolution fusion | flops 536870912 | bytes 12582912 | tf_op jit(solution)/shard_map/cnk,nrk->ncr/dot_general | solution.py:301
  221.4 2.0 fusion.6
  224.5 14.2 %shard_map.62 = f32[8,128]{1,0:T(8,128)} custom-call(f32[8,128]{1,0:T(8,128)} %scatter.20.x_ref), custom_call_target="tpu_custom_call" | custom-call | tf_op jit(solution)/shard_map/pallas_call | solution.py:80
  238.6 0.7 sqrt_bitcast_fusion.1
  240.1 5.0 convert_bitcast_fusion
  245.1 30.9 %all_to_all.31 = bf16[64,32,512]{2,0,1:T(8,128)(2,1)S(1)} all-to-all(bf16[64,32,512]{2,0,1:T(8,128)(2,1)S(1)} %convert_bitcast_fusion), channel_id=1, replica_groups=mesh['ray'=16,'tile'=8] {'tile'}, dimensions={1} | all-to-all | bytes 4194304 | tf_op jit(solution)/shard_map/all_to_all | solution.py:314
  276.0 1.7 fusion.4
  277.8 6.3 %copy.44 = f32[8,8,48,512]{3,1,2,0:T(8,128)} copy(f32[8,8,48,512]{3,2,1,0:T(8,128)S(1)} %bitcast.108) | data formatting | bytes 12582912
  284.0 90.0 %shard_map.63 = f32[64,24576]{1,0:T(8,128)} custom-call(f32[64,24576]{1,0:T(8,128)} %bitcast.111), custom_call_target="tpu_custom_call" | custom-call | tf_op jit(solution)/shard_map/pallas_call | solution.py:259
  374.0 5.8 %multiply_reduce_fusion = f32[64]{0:T(128)S(1)} fusion(f32[64,24576]{1,0:T(8,128)} %shard_map.63, f32[64]{0:T(128)S(1)} %sqrt_bitcast_fusion.1, f32[64,24576]{1,0:T(8,128)} %shard_map.60, f32[64]{0:T(128)S(1)} %sqrt_bitcast_fusion.2), kind=kLoop, calls=%fused_computation.6 | loop fusion | flops 7864256 | bytes 12583680 | tf_op jit(solution)/shard_map/reduce_sum | solution.py:322
  380.4 7.8 %shard_map.64 = f32[8,128]{1,0:T(8,128)} custom-call(f32[8,128]{1,0:T(8,128)} %scatter.21.x_ref), custom_call_target="tpu_custom_call" | custom-call | tf_op jit(solution)/shard_map/pallas_call | solution.py:80
  388.2 0.7 sqrt_bitcast_fusion
  388.9 5.2 %fusion.10 = bf16[64,24576]{1,0:T(8,128)(2,1)S(1)} fusion(f32[64]{0:T(128)S(1)} %sqrt_bitcast_fusion, f32[64,24576]{1,0:T(8,128)} %shard_map.63, f32[64]{0:T(128)S(1)} %sqrt_bitcast_fusion.1, f32[64,24576]{1,0:T(8,128)} %shard_map.60, f32[64]{0:T(128)S(1)} %sqrt_bitcast_fusion.2), kind=kLoop, calls=%fused_computation.29 | loop fusion | flops 7864320 | bytes 15729408 | tf_op jit(solution)/shard_map/convert_element_type | solution.py:340
  394.5 2.0 gather_fusion.3
  396.5 3.2 select_bitcast_fusion.1
  399.7 5.0 all-to-all-start.4
  404.7 0.7 multiply_divide_fusion.2
  405.4 25.6 %all-to-all-done.4 = bf16[64,32,512]{2,0,1:T(8,128)(2,1)S(1)} async-done(((bf16[64,32,512]{2,0,1:T(8,128)(2,1)}), bf16[64,32,512]{2,0,1:T(8,128)(2,1)S(1)}, u32[]{:S(2)}, u32[]{:S(2)}) %all-to-all-start.4) | async-done | bytes 2097184 | tf_op jit(solution)/shard_map/all_to_all | solution.py:296
  431.0 6.0 %fusion.43 = f32[32,64,256]{2,1,0:T(8,128)S(1)} fusion(bf16[64,32,512]{2,0,1:T(8,128)(2,1)S(1)} %all-to-all-done.4, bf16[32,256,512]{2,1,0:T(8,128)(2,1)} %param.19), kind=kOutput, calls=%fused_computation.80 | convolution fusion | flops 536870912 | bytes 12582912 | tf_op jit(solution)/shard_map/cnk,nrk->ncr/dot_general | solution.py:301
  437.0 2.0 fusion.2
  440.0 17.1 %shard_map.65 = f32[8,128]{1,0:T(8,128)} custom-call(f32[8,128]{1,0:T(8,128)} %scatter.24.x_ref), custom_call_target="tpu_custom_call" | custom-call | tf_op jit(solution)/shard_map/pallas_call | solution.py:80
  457.1 0.7 multiply_divide_fusion.1
  457.9 0.7 multiply_divide_fusion
  458.6 7.4 %fusion.39 = (bf16[64,24576]{1,0:T(8,128)(2,1)S(1)}, f32[64,24576]{1,0:T(8,128)}) fusion(f32[64]{0:T(128)S(1)} %multiply_divide_fusion, f32[64]{0:T(128)S(1)} %sqrt_bitcast_fusion, f32[64,24576]{1,0:T(8,128)} %shard_map.63, f32[64]{0:T(128)S(1)} %sqrt_bitcast_fusion.1, f32[64]{0:T(128)S(1)} %get-tuple-element.69, f32[64,24576]{1,0:T(8,128)} %shard_map.60, ...), kind=kLoop, calls=%fused_computation.78 | loop fusion | flops 15728640 | bytes 22021632 | tf_op jit(solution)/shard_map/convert_element_type | solution.py:357
  466.3 2.0 gather_fusion.4
  468.4 1.8 select_bitcast_fusion
  470.2 31.2 %all_to_all.32 = bf16[64,32,512]{2,0,1:T(8,128)(2,1)S(1)} all-to-all(bf16[64,32,512]{2,0,1:T(8,128)(2,1)S(1)} %select_bitcast_fusion), channel_id=1, replica_groups=mesh['ray'=16,'tile'=8] {'tile'}, dimensions={1} | all-to-all | bytes 4194304 | tf_op jit(solution)/shard_map/all_to_all | solution.py:296
  501.4 6.0 %fusion.44 = f32[32,64,256]{2,1,0:T(8,128)S(1)} fusion(bf16[64,32,512]{2,0,1:T(8,128)(2,1)S(1)} %all_to_all.32, bf16[32,256,512]{2,1,0:T(8,128)(2,1)} %param.19), kind=kOutput, calls=%fused_computation.81 | convolution fusion | flops 536870912 | bytes 12582912 | tf_op jit(solution)/shard_map/cnk,nrk->ncr/dot_general | solution.py:301
  507.5 2.0 fusion
  509.6 0.9 sub.19
  (39 shorter events, 9.4 us)
Async XLA Ops:
  2.0 33.6 %all-to-all-start = ((s32[1,8,4]{2,0,1:T(1,128)}), s32[1,8,4]{2,0,1:T(1,128)S(1)}, u32[]{:S(2)}, u32[]{:S(2)}) async-start(s32[1,8,4]{2,0,1:T(1,128)} %copy.25), calls=%async_computation | async-start | bytes 8192 | tf_op jit(solution)/shard_map/all_to_all | solution.py:283
  35.6 31.2 %all-to-all-start.1 = ((bf16[64,32,512]{2,0,1:T(8,128)(2,1)}), bf16[64,32,512]{2,0,1:T(8,128)(2,1)S(1)}, u32[]{:S(2)}, u32[]{:S(2)}) async-start(bf16[64,32,512]{2,0,1:T(8,128)(2,1)} %convert_bitcast_fusion.1), calls=%async_computation.1 | async-start | bytes 4194304 | tf_op jit(solution)/shard_map/all_to_all | solution.py:314
  221.4 2.1 copy-start
  223.8 15.7 %copy-start.2 = (f32[64,2048]{1,0:T(8,128)}, f32[64,2048]{1,0:T(8,128)S(1)}, u32[]{:S(2)}) copy-start(f32[64,2048]{1,0:T(8,128)S(1)} %get-tuple-element.72) | copy-start | bytes 1572868
  399.7 31.3 %all-to-all-start.4 = ((bf16[64,32,512]{2,0,1:T(8,128)(2,1)}), bf16[64,32,512]{2,0,1:T(8,128)(2,1)S(1)}, u32[]{:S(2)}, u32[]{:S(2)}) async-start(bf16[64,32,512]{2,0,1:T(8,128)(2,1)} %select_bitcast_fusion.1), calls=%async_computation.4 | async-start | bytes 4194304 | tf_op jit(solution)/shard_map/all_to_all | solution.py:296
  437.0 2.1 copy-start.3
  507.5 2.1 copy-start.1

commit v11 on v6

--- a/solution.py
+++ b/solution.py
@@ -136,9 +136,11 @@
     plans = [(axes[0], axes[1]), (axes[1], axes[0])]
     sends = []
 
+    pieces = 4
+
     def send(stage, h, d, s, axis, src, dst, landing):
         size = axis[0]
-        k = size - 1 if d == 0 else 1
+        k = size - 1 if d % 2 == 0 else 1
         sems = dict(send_sem=send_sems.at[stage, h, d, s], recv_sem=recv_sems.at[stage, h, d, s],
                     device_id=peer(axis, k), device_id_type=MESH)
         copy = pltpu.make_async_remote_copy(src_ref=src, dst_ref=dst, **sems)
@@ -146,39 +148,48 @@
         sends.append(copy)
         return pltpu.make_async_remote_copy(src_ref=src, dst_ref=landing, **sems)
 
+    order = [(h, d) for d in range(pieces) for h in range(2)]
+
     def reduce_scatter(stage, segs, rbuf, acc):
         steps = segs[0][0][0] - 1
+
+        def start(h, d, s):
+            axis, own, final = segs[h]
+            size, p = axis[0], pos(axis)
+            sign = 1 if d % 2 == 0 else -1
+            src = own((p - sign * (s + 1) + 2 * size) % size, d) if s == 0 else acc.at[h, d, s - 1]
+            return send(stage, h, d, s, axis, src, rbuf.at[h, d, s], rbuf.at[h, d, s])
+
+        pending = {hd: start(*hd, 0) for hd in order}
         for s in range(steps):
-            waits = []
-            for h, (axis, own, final) in enumerate(segs):
+            for h, d in order:
+                axis, own, final = segs[h]
                 size, p = axis[0], pos(axis)
-                for d in range(2):
-                    sign = 1 if d == 0 else -1
-                    src = own((p - sign * (s + 1) + 2 * size) % size, d) if s == 0 else acc.at[h, d, s - 1]
-                    waits.append((h, d, send(stage, h, d, s, axis, src, rbuf.at[h, d, s], rbuf.at[h, d, s])))
-            for h, d, copy in waits:
-                copy.wait_recv()
-            for h, (axis, own, final) in enumerate(segs):
-                size, p = axis[0], pos(axis)
-                for d in range(2):
-                    sign = 1 if d == 0 else -1
-                    mine = own((p - sign * (s + 2) + 2 * size) % size, d)
-                    dst = final(d) if s == steps - 1 else acc.at[h, d, s]
-                    add_rows(dst, rbuf.at[h, d, s], mine)
+                sign = 1 if d % 2 == 0 else -1
+                pending[(h, d)].wait_recv()
+                mine = own((p - sign * (s + 2) + 2 * size) % size, d)
+                dst = final(d) if s == steps - 1 else acc.at[h, d, s]
+                add_rows(dst, rbuf.at[h, d, s], mine)
+                if s + 1 < steps:
+                    pending[(h, d)] = start(h, d, s + 1)
 
     def all_gather(stage, segs):
         steps = segs[0][0][0] - 1
+
+        def start(h, d, s):
+            axis, region = segs[h]
+            size, p = axis[0], pos(axis)
+            sign = 1 if d % 2 == 0 else -1
+            src = region((p - sign * s + 2 * size) % size, d)
+            landing = region((p - sign * (s + 1) + 2 * size) % size, d)
+            return send(stage, h, d, s, axis, src, src, landing)
+
+        pending = {hd: start(*hd, 0) for hd in order}
         for s in range(steps):
-            waits = []
-            for h, (axis, region) in enumerate(segs):
-                size, p = axis[0], pos(axis)
-                for d in range(2):
-                    sign = 1 if d == 0 else -1
-                    src = region((p - sign * s + 2 * size) % size, d)
-                    landing = region((p - sign * (s + 1) + 2 * size) % size, d)
-                    waits.append(send(stage, h, d, s, axis, src, src, landing))
-            for copy in waits:
-                copy.wait_recv()
+            for h, d in order:
+                pending[(h, d)].wait_recv()
+                if s + 1 < steps:
+                    pending[(h, d)] = start(h, d, s + 1)
 
     def direct_reduce_scatter(stage, segs, rbuf, width):
         waits = []
@@ -228,7 +239,7 @@
         for copy in waits:
             copy.wait_recv()
 
-    q1, q2 = w1 // 2, w2 // 2
+    q1, q2 = w1 // pieces, w2 // 2
     seg1, seg2, seg3, seg4 = [], [], [], []
     for h, (a1, a2) in enumerate(plans):
         p1, p2 = pos(a1), pos(a2)
@@ -263,11 +274,11 @@
         out_specs=pl.BlockSpec(memory_space=pltpu.VMEM),
         scratch_shapes=[
             pltpu.VMEM((2, rows, w1), jnp.float32),
-            pltpu.VMEM((2, 2, steps, rows, w1 // 2), jnp.float32),
-            pltpu.VMEM((2, 2, steps, rows, w1 // 2), jnp.float32),
+            pltpu.VMEM((2, 4, steps, rows, w1 // 4), jnp.float32),
+            pltpu.VMEM((2, 4, steps, rows, w1 // 4), jnp.float32),
             pltpu.VMEM((2, steps, rows, w2), jnp.float32),
-            pltpu.SemaphoreType.DMA((4, 2, 2, steps)),
-            pltpu.SemaphoreType.DMA((4, 2, 2, steps)),
+            pltpu.SemaphoreType.DMA((4, 2, 4, steps)),
+            pltpu.SemaphoreType.DMA((4, 2, 4, steps)),
         ],
         compiler_params=pltpu.CompilerParams(
             collective_id=2, has_side_effects=True, vmem_limit_bytes=60 * 1024 * 1024),

time: 495 us -> 510 us (1.030); the launches traced: 494 us -> 501 us
  blocking collectives: 93.2 us -> 103 us
    all_to_all x2, blocking collectives: 61.7 us -> 71.6 us  [fetch(): lax.all_to_all(outgoing, 'tile', split_axis=1, concat_axis=1, tiled=True)]
where the time goes in v11:
time: 510 us; the launch traced here: 501 us
  Pallas kernels  223 us (44%)
  blocking collectives  103 us (20%)
  waiting for transfers between devices  50.7 us (10%)
  other arithmetic  41.2 us (8%)
  matrix products  38.7 us (8%)
  local copies, waits for them, and re-layouts  27.4 us (5%)
  starting transfers between devices  15.1 us (3%)
    pallas_call x2, Pallas kernels, ray_allreduce(): pl.pallas_call(functools.partial(allreduce_kernel, axes), out_shape=jax.S...  166 us
    all_to_all x2, blocking collectives, fetch(): lax.all_to_all(outgoing, 'tile', split_axis=1, concat_axis=1, tiled=True)  71.6 us
    pallas_call x5, Pallas kernels, group_sum(): pl.pallas_call(functools.partial(reduce_kernel, plan), out_shape=jax.Shap...  56.9 us
    all_to_all x1, blocking collectives, adjoint(): lax.all_to_all(terms, 'tile', split_axis=1, concat_axis=1, tiled=True)  31.5 us
    all_to_all x1, waiting for transfers between devices, fetch(): lax.all_to_all(outgoing, 'tile', split_axis=1, concat_axis=1, tiled=True)  25.6 us
    all_to_all x1, waiting for transfers between devices, adjoint(): lax.all_to_all(terms, 'tile', split_axis=1, concat_axis=1, tiled=True)  25.1 us
    dot_general x3, matrix products, forward(): jnp.einsum('cnk,nrk->ncr', tiles, sensitivity, preferred_element_type=jnp...  18.1 us
    unnamed x15, local copies, waits for them, and re-layouts  15.1 us
  transfers between devices with their start and end apart: 3, of which 2 were waited for; matrix products, arithmetic and copies ran while one was open for 3% of the time, Pallas kernels for 3%

profile of v11, /device:TPU:1, one launch (start us, length us, event | category | flops | bytes accessed | tf_op | source)
XLA Modules:
  0.0 500.7 jit_solution(14947077662007667790)
XLA Ops:
  0.6 1.3 copy.25
  2.0 6.0 %all-to-all-start = ((s32[1,8,4]{2,0,1:T(1,128)}), s32[1,8,4]{2,0,1:T(1,128)S(1)}, u32[]{:S(2)}, u32[]{:S(2)}) async-start(s32[1,8,4]{2,0,1:T(1,128)} %copy.25), calls=%async_computation | async-start | bytes 8192 | tf_op jit(solution)/shard_map/all_to_all | solution.py:294
  7.9 0.8 copy.26
  8.8 1.2 multiply_reduce_fusion.4
  10.6 16.2 %shard_map.59 = f32[8,128]{1,0:T(8,128)} custom-call(f32[8,128]{1,0:T(8,128)} %scatter.16.x_ref), custom_call_target="tpu_custom_call" | custom-call | tf_op jit(solution)/shard_map/pallas_call | solution.py:80
  27.5 1.1 fusion.19
  29.3 6.3 %convert_bitcast_fusion.1 = bf16[64,32,512]{2,0,1:T(8,128)(2,1)} fusion(bf16[32,256,512]{2,1,0:T(8,128)(2,1)} %param.19, bf16[32,64,256]{2,1,0:T(8,128)(2,1)S(1)} %gather_fusion, pred[32]{0:T(512)(128)(4,1)S(1)} %compare_and_fusion.1), kind=kOutput, calls=%fused_computation.28 | convolution fusion | flops 538443776 | bytes 11534368 | tf_op jit(solution)/shard_map/cnr,nrk->cnk/dot_general | solution.py:322
  35.6 4.9 all-to-all-start.1
  41.8 25.1 %all-to-all-done.1 = bf16[64,32,512]{2,0,1:T(8,128)(2,1)S(1)} async-done(((bf16[64,32,512]{2,0,1:T(8,128)(2,1)}), bf16[64,32,512]{2,0,1:T(8,128)(2,1)S(1)}, u32[]{:S(2)}, u32[]{:S(2)}) %all-to-all-start.1) | async-done | bytes 2097184 | tf_op jit(solution)/shard_map/all_to_all | solution.py:325
  66.8 1.7 fusion.8
  68.6 6.3 %copy.42 = f32[8,8,48,512]{3,1,2,0:T(8,128)} copy(f32[8,8,48,512]{3,2,1,0:T(8,128)S(1)} %bitcast.109) | data formatting | bytes 12582912
  74.8 83.7 %shard_map.60 = f32[64,24576]{1,0:T(8,128)} custom-call(f32[64,24576]{1,0:T(8,128)} %bitcast.110), custom_call_target="tpu_custom_call" | custom-call | tf_op jit(solution)/shard_map/pallas_call | solution.py:270
  158.5 3.3 multiply_reduce_fusion.1
  162.4 7.8 %shard_map.61 = f32[8,128]{1,0:T(8,128)} custom-call(f32[8,128]{1,0:T(8,128)} %scatter.19.x_ref), custom_call_target="tpu_custom_call" | custom-call | tf_op jit(solution)/shard_map/pallas_call | solution.py:80
  171.0 3.2 fusion.38
  174.6 2.0 gather_fusion.1
  176.6 1.8 select_bitcast_fusion.2
  178.5 40.1 %all_to_all.30 = bf16[64,32,512]{2,0,1:T(8,128)(2,1)S(1)} all-to-all(bf16[64,32,512]{2,0,1:T(8,128)(2,1)S(1)} %select_bitcast_fusion.2), channel_id=1, replica_groups=mesh['ray'=16,'tile'=8] {'tile'}, dimensions={1} | all-to-all | bytes 4194304 | tf_op jit(solution)/shard_map/all_to_all | solution.py:307
  218.5 6.0 %fusion.42 = f32[32,64,256]{2,1,0:T(8,128)S(1)} fusion(bf16[64,32,512]{2,0,1:T(8,128)(2,1)S(1)} %all_to_all.30, bf16[32,256,512]{2,1,0:T(8,128)(2,1)} %param.19), kind=kOutput, calls=%fused_computation.79 | convolution fusion | flops 536870912 | bytes 12582912 | tf_op jit(solution)/shard_map/cnk,nrk->ncr/dot_general | solution.py:312
  224.6 2.0 fusion.6
  227.6 12.4 %shard_map.62 = f32[8,128]{1,0:T(8,128)} custom-call(f32[8,128]{1,0:T(8,128)} %scatter.20.x_ref), custom_call_target="tpu_custom_call" | custom-call | tf_op jit(solution)/shard_map/pallas_call | solution.py:80
  240.1 0.7 sqrt_bitcast_fusion.1
  241.5 5.0 convert_bitcast_fusion
  246.5 31.5 %all_to_all.31 = bf16[64,32,512]{2,0,1:T(8,128)(2,1)S(1)} all-to-all(bf16[64,32,512]{2,0,1:T(8,128)(2,1)S(1)} %convert_bitcast_fusion), channel_id=1, replica_groups=mesh['ray'=16,'tile'=8] {'tile'}, dimensions={1} | all-to-all | bytes 4194304 | tf_op jit(solution)/shard_map/all_to_all | solution.py:325
  278.1 1.7 fusion.4
  279.8 6.3 %copy.44 = f32[8,8,48,512]{3,1,2,0:T(8,128)} copy(f32[8,8,48,512]{3,2,1,0:T(8,128)S(1)} %bitcast.108) | data formatting | bytes 12582912
  286.1 82.6 %shard_map.63 = f32[64,24576]{1,0:T(8,128)} custom-call(f32[64,24576]{1,0:T(8,128)} %bitcast.111), custom_call_target="tpu_custom_call" | custom-call | tf_op jit(solution)/shard_map/pallas_call | solution.py:270
  368.6 5.8 %multiply_reduce_fusion = f32[64]{0:T(128)S(1)} fusion(f32[64,24576]{1,0:T(8,128)} %shard_map.63, f32[64]{0:T(128)S(1)} %sqrt_bitcast_fusion.1, f32[64,24576]{1,0:T(8,128)} %shard_map.60, f32[64]{0:T(128)S(1)} %sqrt_bitcast_fusion.2), kind=kLoop, calls=%fused_computation.6 | loop fusion | flops 7864256 | bytes 12583680 | tf_op jit(solution)/shard_map/reduce_sum | solution.py:333
  375.0 8.0 %shard_map.64 = f32[8,128]{1,0:T(8,128)} custom-call(f32[8,128]{1,0:T(8,128)} %scatter.21.x_ref), custom_call_target="tpu_custom_call" | custom-call | tf_op jit(solution)/shard_map/pallas_call | solution.py:80
  383.0 0.7 sqrt_bitcast_fusion
  383.7 5.2 %fusion.10 = bf16[64,24576]{1,0:T(8,128)(2,1)S(1)} fusion(f32[64]{0:T(128)S(1)} %sqrt_bitcast_fusion, f32[64,24576]{1,0:T(8,128)} %shard_map.63, f32[64]{0:T(128)S(1)} %sqrt_bitcast_fusion.1, f32[64,24576]{1,0:T(8,128)} %shard_map.60, f32[64]{0:T(128)S(1)} %sqrt_bitcast_fusion.2), kind=kLoop, calls=%fused_computation.29 | loop fusion | flops 7864320 | bytes 15729408 | tf_op jit(solution)/shard_map/convert_element_type | solution.py:351
  389.4 2.0 gather_fusion.3
  391.4 3.2 select_bitcast_fusion.1
  394.5 4.2 all-to-all-start.4
  398.8 0.7 multiply_divide_fusion.2
  399.5 25.6 %all-to-all-done.4 = bf16[64,32,512]{2,0,1:T(8,128)(2,1)S(1)} async-done(((bf16[64,32,512]{2,0,1:T(8,128)(2,1)}), bf16[64,32,512]{2,0,1:T(8,128)(2,1)S(1)}, u32[]{:S(2)}, u32[]{:S(2)}) %all-to-all-start.4) | async-done | bytes 2097184 | tf_op jit(solution)/shard_map/all_to_all | solution.py:307
  425.1 6.0 %fusion.43 = f32[32,64,256]{2,1,0:T(8,128)S(1)} fusion(bf16[64,32,512]{2,0,1:T(8,128)(2,1)S(1)} %all-to-all-done.4, bf16[32,256,512]{2,1,0:T(8,128)(2,1)} %param.19), kind=kOutput, calls=%fused_computation.80 | convolution fusion | flops 536870912 | bytes 12582912 | tf_op jit(solution)/shard_map/cnk,nrk->ncr/dot_general | solution.py:312
  431.2 2.0 fusion.2
  434.2 12.5 %shard_map.65 = f32[8,128]{1,0:T(8,128)} custom-call(f32[8,128]{1,0:T(8,128)} %scatter.24.x_ref), custom_call_target="tpu_custom_call" | custom-call | tf_op jit(solution)/shard_map/pallas_call | solution.py:80
  446.6 0.7 multiply_divide_fusion.1
  447.4 0.7 multiply_divide_fusion
  448.1 7.4 %fusion.39 = (bf16[64,24576]{1,0:T(8,128)(2,1)S(1)}, f32[64,24576]{1,0:T(8,128)}) fusion(f32[64]{0:T(128)S(1)} %multiply_divide_fusion, f32[64]{0:T(128)S(1)} %sqrt_bitcast_fusion, f32[64,24576]{1,0:T(8,128)} %shard_map.63, f32[64]{0:T(128)S(1)} %sqrt_bitcast_fusion.1, f32[64]{0:T(128)S(1)} %get-tuple-element.69, f32[64,24576]{1,0:T(8,128)} %shard_map.60, ...), kind=kLoop, calls=%fused_computation.78 | loop fusion | flops 15728640 | bytes 22021632 | tf_op jit(solution)/shard_map/convert_element_type | solution.py:368
  455.8 2.0 gather_fusion.4
  457.9 1.8 select_bitcast_fusion
  459.7 31.5 %all_to_all.32 = bf16[64,32,512]{2,0,1:T(8,128)(2,1)S(1)} all-to-all(bf16[64,32,512]{2,0,1:T(8,128)(2,1)S(1)} %select_bitcast_fusion), channel_id=1, replica_groups=mesh['ray'=16,'tile'=8] {'tile'}, dimensions={1} | all-to-all | bytes 4194304 | tf_op jit(solution)/shard_map/all_to_all | solution.py:307
  491.2 6.0 %fusion.44 = f32[32,64,256]{2,1,0:T(8,128)S(1)} fusion(bf16[64,32,512]{2,0,1:T(8,128)(2,1)S(1)} %all_to_all.32, bf16[32,256,512]{2,1,0:T(8,128)(2,1)} %param.19), kind=kOutput, calls=%fused_computation.81 | convolution fusion | flops 536870912 | bytes 12582912 | tf_op jit(solution)/shard_map/cnk,nrk->ncr/dot_general | solution.py:312
  497.3 2.0 fusion
  499.4 0.9 sub.19
  (39 shorter events, 9.4 us)
Async XLA Ops:
  2.0 33.6 %all-to-all-start = ((s32[1,8,4]{2,0,1:T(1,128)}), s32[1,8,4]{2,0,1:T(1,128)S(1)}, u32[]{:S(2)}, u32[]{:S(2)}) async-start(s32[1,8,4]{2,0,1:T(1,128)} %copy.25), calls=%async_computation | async-start | bytes 8192 | tf_op jit(solution)/shard_map/all_to_all | solution.py:294
  35.6 31.2 %all-to-all-start.1 = ((bf16[64,32,512]{2,0,1:T(8,128)(2,1)}), bf16[64,32,512]{2,0,1:T(8,128)(2,1)S(1)}, u32[]{:S(2)}, u32[]{:S(2)}) async-start(bf16[64,32,512]{2,0,1:T(8,128)(2,1)} %convert_bitcast_fusion.1), calls=%async_computation.1 | async-start | bytes 4194304 | tf_op jit(solution)/shard_map/all_to_all | solution.py:325
  224.6 2.1 copy-start
  227.0 13.9 %copy-start.2 = (f32[64,2048]{1,0:T(8,128)}, f32[64,2048]{1,0:T(8,128)S(1)}, u32[]{:S(2)}) copy-start(f32[64,2048]{1,0:T(8,128)S(1)} %get-tuple-element.72) | copy-start | bytes 1572868
  394.5 30.6 %all-to-all-start.4 = ((bf16[64,32,512]{2,0,1:T(8,128)(2,1)}), bf16[64,32,512]{2,0,1:T(8,128)(2,1)S(1)}, u32[]{:S(2)}, u32[]{:S(2)}) async-start(bf16[64,32,512]{2,0,1:T(8,128)(2,1)} %select_bitcast_fusion.1), calls=%async_computation.4 | async-start | bytes 4194304 | tf_op jit(solution)/shard_map/all_to_all | solution.py:307
  431.1 2.1 copy-start.3
  497.3 2.1 copy-start.1

commit v12 on v6

--- a/solution.py
+++ b/solution.py
@@ -98,7 +98,12 @@
     return ((inner, 1), (rays // inner, inner))
 
 
-def allreduce_kernel(axes, x_ref, o_ref, part, rbuf1, acc1, rbuf2, send_sems, recv_sems):
+def allreduce_kernel(axes, tiles, has_prev, *refs):
+    if has_prev:
+        x_ref, prev_ref, scale_ref, o_ref, ss_ref = refs[:5]
+    else:
+        x_ref, o_ref, ss_ref = refs[:3]
+    part, rbuf1, acc1, rbuf2, tbuf, send_sems, recv_sems, tsend, trecv = refs[-9:]
     me = lax.axis_index("ray")
     tile = lax.axis_index("tile")
     rows = x_ref.shape[0]
@@ -131,6 +136,9 @@
         for k in range(1, axis[0]):
             pl.semaphore_signal(barrier, inc=1, device_id=peer(axis, k), device_id_type=MESH)
             greeted += 1
+    for k in range(1, tiles):
+        pl.semaphore_signal(barrier, inc=1, device_id=(me, (tile - k + tiles) % tiles), device_id_type=MESH)
+        greeted += 1
     pl.semaphore_wait(barrier, greeted)
 
     plans = [(axes[0], axes[1]), (axes[1], axes[0])]
@@ -248,30 +256,74 @@
     for copy in sends:
         copy.wait_send()
 
-
-def ray_allreduce(mesh, owned):
+    width = o_ref.shape[1]
+    span = 2048
+
+    def rows_body(r, carry):
+        block = pl.ds(pl.multiple_of(r * 8, 8), 8)
+
+        def cols_body(c, acc):
+            cs = pl.ds(pl.multiple_of(c * span, span), span)
+            v = o_ref[block, cs]
+            if has_prev:
+                v = v - scale_ref[block, 0:1] * prev_ref[block, cs]
+                o_ref[block, cs] = v
+            sq = v * v
+            for i in range(span // 128):
+                acc = acc + sq[:, i * 128:(i + 1) * 128]
+            return acc
+        acc = lax.fori_loop(0, width // span, cols_body, jnp.zeros((8, 128), jnp.float32))
+        tbuf[0, block, :] = jnp.broadcast_to(jnp.sum(acc, axis=1, keepdims=True), (8, 128))
+        return carry
+    lax.fori_loop(0, rows // 8, rows_body, 0)
+
+    copies = []
+    for k in range(1, tiles):
+        copy = pltpu.make_async_remote_copy(
+            src_ref=tbuf.at[0], dst_ref=tbuf.at[k], send_sem=tsend.at[k], recv_sem=trecv.at[k],
+            device_id=(me, (tile - k + tiles) % tiles), device_id_type=MESH)
+        copy.start()
+        copies.append(copy)
+    for copy in copies:
+        copy.wait_recv()
+    total = tbuf[(tiles - tile) % tiles]
+    for q in range(1, tiles):
+        total = total + tbuf[(q - tile + tiles) % tiles]
+    ss_ref[...] = total
+    for copy in copies:
+        copy.wait_send()
+
+
+def ray_allreduce(mesh, owned, prev=None, beta=None):
     axes = ray_axes(mesh)
     rows, width = owned.shape
     half = width // 2
     w1 = half // axes[0][0]
     w2 = w1 // axes[1][0]
     steps = max(axes[0][0], axes[1][0]) - 1
+    tiles = mesh.shape["tile"]
+    has_prev = prev is not None
+    operands = (owned, prev, jnp.broadcast_to(beta[:, None], (rows, 128))) if has_prev else (owned,)
     return pl.pallas_call(
-        functools.partial(allreduce_kernel, axes),
-        out_shape=jax.ShapeDtypeStruct((rows, width), jnp.float32),
-        in_specs=[pl.BlockSpec(memory_space=pltpu.VMEM)],
-        out_specs=pl.BlockSpec(memory_space=pltpu.VMEM),
+        functools.partial(allreduce_kernel, axes, tiles, has_prev),
+        out_shape=(jax.ShapeDtypeStruct((rows, width), jnp.float32),
+                   jax.ShapeDtypeStruct((rows, 128), jnp.float32)),
+        in_specs=[pl.BlockSpec(memory_space=pltpu.VMEM)] * len(operands),
+        out_specs=(pl.BlockSpec(memory_space=pltpu.VMEM), pl.BlockSpec(memory_space=pltpu.VMEM)),
         scratch_shapes=[
             pltpu.VMEM((2, rows, w1), jnp.float32),
             pltpu.VMEM((2, 2, steps, rows, w1 // 2), jnp.float32),
             pltpu.VMEM((2, 2, steps, rows, w1 // 2), jnp.float32),
             pltpu.VMEM((2, steps, rows, w2), jnp.float32),
+            pltpu.VMEM((tiles, rows, 128), jnp.float32),
             pltpu.SemaphoreType.DMA((4, 2, 2, steps)),
             pltpu.SemaphoreType.DMA((4, 2, 2, steps)),
+            pltpu.SemaphoreType.DMA((tiles,)),
+            pltpu.SemaphoreType.DMA((tiles,)),
         ],
         compiler_params=pltpu.CompilerParams(
-            collective_id=2, has_side_effects=True, vmem_limit_bytes=60 * 1024 * 1024),
-    )(owned)
+            collective_id=3 if has_prev else 2, has_side_effects=True, vmem_limit_bytes=60 * 1024 * 1024),
+    )(*operands)
 
 
 eps_norm = 1e-06
@@ -306,7 +358,7 @@
         )
         return summed.reshape(columns, BUND_DEV * RB)
 
-    def adjoint(rays_bf):
+    def adjoint(rays_bf, prev=None, beta=None):
         picked = jnp.take(rays_bf.reshape(columns, BUND_DEV, RB), bundles, axis=1)
         terms = jnp.einsum(
             "cnr,nrk->cnk", picked, sensitivity, preferred_element_type=jnp.float32
@@ -315,8 +367,8 @@
         owned = jnp.einsum(
             "cnk,nt->ctk", arrived, owner_onehot, preferred_element_type=jnp.float32
         ).reshape(columns, TILE_DEV * CB)
-        total = ray_allreduce(mesh, owned)
-        return total
+        field, squares = ray_allreduce(mesh, owned, prev, beta)
+        return field, jnp.sqrt(squares[:, 0] + eps_norm)
 
     def cell_norm(field):
         local = jnp.sum(field * field, axis=1)
@@ -329,8 +381,7 @@
 
     beta_now = ray_norm(data)
     rays_dir = data / beta_now[:, None]
-    model_dir = adjoint(rays_dir.astype(jnp.bfloat16))
-    alpha_now = cell_norm(model_dir)
+    model_dir, alpha_now = adjoint(rays_dir.astype(jnp.bfloat16))
     model_dir = model_dir / alpha_now[:, None]
     search = model_dir
     solution = jnp.zeros_like(model_dir)
@@ -348,8 +399,7 @@
         phi_bar = sine_part * phi_bar
         solution = solution + (phi_now / rho_now)[:, None] * search
         if step + 1 < ITERS:
-            model_dir = adjoint(rays_dir.astype(jnp.bfloat16)) - beta_now[:, None] * model_dir
-            alpha_now = cell_norm(model_dir)
+            model_dir, alpha_now = adjoint(rays_dir.astype(jnp.bfloat16), model_dir, beta_now)
             model_dir = model_dir / alpha_now[:, None]
             theta_now = sine_part * alpha_now
             rho_bar = -cosine * alpha_now

time: 495 us -> 505 us (1.020)
  Pallas kernels: 226 us -> 245 us
  other arithmetic: 41.2 us -> 32.1 us
    pallas_call x2, Pallas kernels: 167 us -> 203 us  [ray_allreduce(): pl.pallas_call(functools.partial(allreduce_kernel, axes, tiles, has_prev)...]
    pallas_call x5 -> x3, Pallas kernels: 58.6 us -> 42 us  [group_sum(): pl.pallas_call(functools.partial(reduce_kernel, plan), out_shape=jax.Shap...]
    reduce_sum x2 -> x0, other arithmetic: 9.08 us -> none  [cell_norm(): local = jnp.sum(field * field, axis=1)]
    unnamed x15 -> x19, local copies, waits for them, and re-layouts: 15.1 us -> 15.1 us
where the time goes in v12:
time: 505 us; the launch traced here: 504 us
  Pallas kernels  245 us (49%)
  blocking collectives  93 us (18%)
  waiting for transfers between devices  51.2 us (10%)
  matrix products  38.7 us (8%)
  other arithmetic  32.1 us (6%)
  local copies, waits for them, and re-layouts  27.2 us (5%)
  starting transfers between devices  15.7 us (3%)
    pallas_call x2, Pallas kernels, ray_allreduce(): pl.pallas_call(functools.partial(allreduce_kernel, axes, tiles, has_prev)...  203 us
    all_to_all x2, blocking collectives, fetch(): lax.all_to_all(outgoing, 'tile', split_axis=1, concat_axis=1, tiled=True)  61.6 us
    pallas_call x3, Pallas kernels, group_sum(): pl.pallas_call(functools.partial(reduce_kernel, plan), out_shape=jax.Shap...  42 us
    all_to_all x1, blocking collectives, adjoint(): lax.all_to_all(terms, 'tile', split_axis=1, concat_axis=1, tiled=True)  31.4 us
    all_to_all x1, waiting for transfers between devices, fetch(): lax.all_to_all(outgoing, 'tile', split_axis=1, concat_axis=1, tiled=True)  26.2 us
    all_to_all x1, waiting for transfers between devices, adjoint(): lax.all_to_all(terms, 'tile', split_axis=1, concat_axis=1, tiled=True)  25.1 us
    dot_general x3, matrix products, forward(): jnp.einsum('cnk,nrk->ncr', tiles, sensitivity, preferred_element_type=jnp...  18.1 us
    unnamed x19, local copies, waits for them, and re-layouts  15.1 us
  transfers between devices with their start and end apart: 3, of which 2 were waited for; matrix products, arithmetic and copies ran while one was open for 3% of the time, Pallas kernels for 3%

profile of v12, /device:TPU:1, one launch (start us, length us, event | category | flops | bytes accessed | tf_op | source)
XLA Modules:
  0.0 504.2 jit_solution(8448793234893038839)
XLA Ops:
  0.6 1.3 copy.61
  2.0 6.0 %all-to-all-start = ((s32[1,8,4]{2,0,1:T(1,128)}), s32[1,8,4]{2,0,1:T(1,128)S(1)}, u32[]{:S(2)}, u32[]{:S(2)}) async-start(s32[1,8,4]{2,0,1:T(1,128)} %copy.61), calls=%async_computation | async-start | bytes 8192 | tf_op jit(solution)/shard_map/all_to_all | solution.py:335
  7.9 0.8 copy.62
  8.8 1.2 multiply_reduce_fusion.2
  10.6 16.2 %shard_map.59 = f32[8,128]{1,0:T(8,128)} custom-call(f32[8,128]{1,0:T(8,128)} %scatter.10.x_ref), custom_call_target="tpu_custom_call" | custom-call | tf_op jit(solution)/shard_map/pallas_call | solution.py:80
  26.8 0.7 fusion.41
  27.5 1.1 fusion.19
  29.3 6.3 %convert_bitcast_fusion.1 = bf16[64,32,512]{2,0,1:T(8,128)(2,1)} fusion(bf16[32,256,512]{2,1,0:T(8,128)(2,1)} %param.15, bf16[32,64,256]{2,1,0:T(8,128)(2,1)S(1)} %gather_fusion, pred[32]{0:T(512)(128)(4,1)S(1)} %compare_and_fusion.1), kind=kOutput, calls=%fused_computation.25 | convolution fusion | flops 538443776 | bytes 11534368 | tf_op jit(solution)/shard_map/cnr,nrk->cnk/dot_general | solution.py:363
  35.6 4.9 all-to-all-start.1
  41.0 0.7 reduce.19
  41.8 25.1 %all-to-all-done.1 = bf16[64,32,512]{2,0,1:T(8,128)(2,1)S(1)} async-done(((bf16[64,32,512]{2,0,1:T(8,128)(2,1)}), bf16[64,32,512]{2,0,1:T(8,128)(2,1)S(1)}, u32[]{:S(2)}, u32[]{:S(2)}) %all-to-all-start.1) | async-done | bytes 2097184 | tf_op jit(solution)/shard_map/all_to_all | solution.py:366
  66.8 1.7 fusion.8
  68.6 6.3 %copy.86 = f32[8,8,48,512]{3,1,2,0:T(8,128)} copy(f32[8,8,48,512]{3,2,1,0:T(8,128)S(1)} %bitcast.85) | data formatting | bytes 12582912
  74.8 97.3 %shard_map.60 = (f32[64,24576]{1,0:T(8,128)}, f32[64,128]{1,0:T(8,128)}) custom-call(f32[64,24576]{1,0:T(8,128)} %bitcast.83), custom_call_target="tpu_custom_call" | custom-call | tf_op jit(solution)/shard_map/pallas_call | solution.py:307
  172.1 0.9 fusion.25
  173.0 6.3 %fusion.46 = (bf16[64,24576]{1,0:T(8,128)(2,1)S(1)}, f32[64,24576]{1,0:T(8,128)}) fusion(f32[64,24576]{1,0:T(8,128)} %get-tuple-element.45, f32[64]{0:T(128)S(1)} %fusion.25), kind=kLoop, calls=%fused_computation.82 | loop fusion | flops 3145728 | bytes 15728896 | tf_op jit(solution)/shard_map/convert_element_type | solution.py:391
  179.8 2.0 gather_fusion.1
  181.9 1.8 select_bitcast_fusion.2
  183.7 30.4 %all_to_all.30 = bf16[64,32,512]{2,0,1:T(8,128)(2,1)S(1)} all-to-all(bf16[64,32,512]{2,0,1:T(8,128)(2,1)S(1)} %select_bitcast_fusion.2), channel_id=1, replica_groups=mesh['ray'=16,'tile'=8] {'tile'}, dimensions={1} | all-to-all | bytes 4194304 | tf_op jit(solution)/shard_map/all_to_all | solution.py:348
  214.1 6.0 %fusion.47 = f32[32,64,256]{2,1,0:T(8,128)S(1)} fusion(bf16[64,32,512]{2,0,1:T(8,128)(2,1)S(1)} %all_to_all.30, bf16[32,256,512]{2,1,0:T(8,128)(2,1)} %param.15), kind=kOutput, calls=%fused_computation.83 | convolution fusion | flops 536870912 | bytes 12582912 | tf_op jit(solution)/shard_map/cnk,nrk->ncr/dot_general | solution.py:353
  220.1 2.0 fusion.6
  222.5 0.6 scatter.11.x_ref
  223.2 12.4 %shard_map.61 = f32[8,128]{1,0:T(8,128)} custom-call(f32[8,128]{1,0:T(8,128)} %scatter.11.x_ref), custom_call_target="tpu_custom_call" | custom-call | tf_op jit(solution)/shard_map/pallas_call | solution.py:80
  235.6 0.7 fusion.43
  236.4 0.6 gather_fusion.2
  237.0 5.0 convert_bitcast_fusion
  242.0 31.4 %all_to_all.31 = bf16[64,32,512]{2,0,1:T(8,128)(2,1)S(1)} all-to-all(bf16[64,32,512]{2,0,1:T(8,128)(2,1)S(1)} %convert_bitcast_fusion), channel_id=1, replica_groups=mesh['ray'=16,'tile'=8] {'tile'}, dimensions={1} | all-to-all | bytes 4194304 | tf_op jit(solution)/shard_map/all_to_all | solution.py:366
  273.4 1.7 fusion.4
  275.2 6.2 %copy.88 = f32[8,8,48,512]{3,1,2,0:T(8,128)} copy(f32[8,8,48,512]{3,2,1,0:T(8,128)S(1)} %bitcast.84) | data formatting | bytes 12582912
  281.4 0.7 broadcast_in_dim.20.refs_2_
  282.0 106.0 %shard_map.62 = (f32[64,24576]{1,0:T(8,128)}, f32[64,128]{1,0:T(8,128)}) custom-call(f32[64,24576]{1,0:T(8,128)} %bitcast.82, f32[64,24576]{1,0:T(8,128)} %get-tuple-element.56.refs_1_, f32[64,128]{1,0:T(8,128)} %broadcast_in_dim.20.refs_2_), custom_call_target="tpu_custom_call" | custom-call | tf_op jit(solution)/shard_map/pallas_call | solution.py:307
  388.1 0.9 fusion.26
  388.9 3.2 fusion.10
  392.6 2.0 gather_fusion.3
  394.7 3.2 select_bitcast_fusion.1
  397.8 4.8 all-to-all-start.4
  402.9 26.2 %all-to-all-done.4 = bf16[64,32,512]{2,0,1:T(8,128)(2,1)S(1)} async-done(((bf16[64,32,512]{2,0,1:T(8,128)(2,1)}), bf16[64,32,512]{2,0,1:T(8,128)(2,1)S(1)}, u32[]{:S(2)}, u32[]{:S(2)}) %all-to-all-start.4) | async-done | bytes 2097184 | tf_op jit(solution)/shard_map/all_to_all | solution.py:348
  429.0 6.0 %fusion.48 = f32[32,64,256]{2,1,0:T(8,128)S(1)} fusion(bf16[64,32,512]{2,0,1:T(8,128)(2,1)S(1)} %all-to-all-done.4, bf16[32,256,512]{2,1,0:T(8,128)(2,1)} %param.15), kind=kOutput, calls=%fused_computation.84 | convolution fusion | flops 536870912 | bytes 12582912 | tf_op jit(solution)/shard_map/cnk,nrk->ncr/dot_general | solution.py:353
  435.1 2.0 fusion.2
  438.1 13.4 %shard_map.63 = f32[8,128]{1,0:T(8,128)} custom-call(f32[8,128]{1,0:T(8,128)} %scatter.14.x_ref), custom_call_target="tpu_custom_call" | custom-call | tf_op jit(solution)/shard_map/pallas_call | solution.py:80
  451.5 0.7 multiply_bitcast_fusion
  452.5 7.1 %fusion.45 = (bf16[64,24576]{1,0:T(8,128)(2,1)S(1)}, f32[64,24576]{1,0:T(8,128)}) fusion(f32[64,24576]{1,0:T(8,128)} %get-tuple-element.56.refs_1_, f32[64]{0:T(128)S(1)} %get-tuple-element.50, f32[64,24576]{1,0:T(8,128)} %get-tuple-element.47, f32[64]{0:T(128)S(1)} %fusion.26, f32[64]{0:T(128)S(1)} %get-tuple-element.49, f32[64]{0:T(128)S(1)} %get-tuple-element.48), kind=kLoop, calls=%fused_computation.81 | loop fusion | flops 11010048 | bytes 22021120 | tf_op jit(solution)/shard_map/convert_element_type | solution.py:407
  460.0 2.0 gather_fusion.4
  462.0 1.8 select_bitcast_fusion
  463.8 31.2 %all_to_all.32 = bf16[64,32,512]{2,0,1:T(8,128)(2,1)S(1)} all-to-all(bf16[64,32,512]{2,0,1:T(8,128)(2,1)S(1)} %select_bitcast_fusion), channel_id=1, replica_groups=mesh['ray'=16,'tile'=8] {'tile'}, dimensions={1} | all-to-all | bytes 4194304 | tf_op jit(solution)/shard_map/all_to_all | solution.py:348
  495.1 6.0 %fusion.49 = f32[32,64,256]{2,1,0:T(8,128)S(1)} fusion(bf16[64,32,512]{2,0,1:T(8,128)(2,1)S(1)} %all_to_all.32, bf16[32,256,512]{2,1,0:T(8,128)(2,1)} %param.15), kind=kOutput, calls=%fused_computation.85 | convolution fusion | flops 536870912 | bytes 12582912 | tf_op jit(solution)/shard_map/cnk,nrk->ncr/dot_general | solution.py:353
  501.1 2.0 fusion
  503.3 0.9 sub.15
  (40 shorter events, 5.4 us)
Async XLA Ops:
  2.0 33.6 %all-to-all-start = ((s32[1,8,4]{2,0,1:T(1,128)}), s32[1,8,4]{2,0,1:T(1,128)S(1)}, u32[]{:S(2)}, u32[]{:S(2)}) async-start(s32[1,8,4]{2,0,1:T(1,128)} %copy.61), calls=%async_computation | async-start | bytes 8192 | tf_op jit(solution)/shard_map/all_to_all | solution.py:335
  35.6 31.2 %all-to-all-start.1 = ((bf16[64,32,512]{2,0,1:T(8,128)(2,1)}), bf16[64,32,512]{2,0,1:T(8,128)(2,1)S(1)}, u32[]{:S(2)}, u32[]{:S(2)}) async-start(bf16[64,32,512]{2,0,1:T(8,128)(2,1)} %convert_bitcast_fusion.1), calls=%async_computation.1 | async-start | bytes 4194304 | tf_op jit(solution)/shard_map/all_to_all | solution.py:366
  220.1 2.1 copy-start
  222.5 13.9 %copy-start.2 = (f32[64,2048]{1,0:T(8,128)}, f32[64,2048]{1,0:T(8,128)S(1)}, u32[]{:S(2)}) copy-start(f32[64,2048]{1,0:T(8,128)S(1)} %get-tuple-element.54) | copy-start | bytes 1572868
  397.8 31.2 %all-to-all-start.4 = ((bf16[64,32,512]{2,0,1:T(8,128)(2,1)}), bf16[64,32,512]{2,0,1:T(8,128)(2,1)S(1)}, u32[]{:S(2)}, u32[]{:S(2)}) async-start(bf16[64,32,512]{2,0,1:T(8,128)(2,1)} %select_bitcast_fusion.1), calls=%async_computation.4 | async-start | bytes 4194304 | tf_op jit(solution)/shard_map/all_to_all | solution.py:348
  435.0 2.2 copy-start.3
  435.1 17.2 %copy-start.4 = (f32[64,128]{1,0:T(8,128)S(1)}, f32[64,128]{1,0:T(8,128)}, u32[]{:S(2)}) copy-start(f32[64,128]{1,0:T(8,128)} %get-tuple-element.44) | copy-start | bytes 98308
  435.1 17.2 %copy-start.5 = (f32[64,128]{1,0:T(8,128)S(1)}, f32[64,128]{1,0:T(8,128)}, u32[]{:S(2)}) copy-start(f32[64,128]{1,0:T(8,128)} %get-tuple-element.46) | copy-start | bytes 98308
  501.1 2.1 copy-start.1

commit v13 on v6

--- a/solution.py
+++ b/solution.py
@@ -98,11 +98,11 @@
     return ((inner, 1), (rays // inner, inner))
 
 
-def allreduce_kernel(axes, x_ref, o_ref, part, rbuf1, acc1, rbuf2, send_sems, recv_sems):
+def allreduce_kernel(axes, x_hbm, o_ref, x_ref, part, rbuf1, acc1, rbuf2, load_sem, send_sems, recv_sems):
     me = lax.axis_index("ray")
     tile = lax.axis_index("tile")
-    rows = x_ref.shape[0]
-    half = x_ref.shape[1] // 2
+    rows = x_hbm.shape[0]
+    half = x_hbm.shape[1] // 2
     w1 = half // axes[0][0]
     w2 = w1 // axes[1][0]
 
@@ -125,6 +125,8 @@
             return carry
         lax.fori_loop(0, rows // 8, body, 0)
 
+    load = pltpu.make_async_copy(x_hbm, x_ref, load_sem)
+    load.start()
     barrier = pltpu.get_barrier_semaphore()
     greeted = 0
     for axis in axes:
@@ -146,7 +148,7 @@
         sends.append(copy)
         return pltpu.make_async_remote_copy(src_ref=src, dst_ref=landing, **sems)
 
-    def reduce_scatter(stage, segs, rbuf, acc):
+    def reduce_scatter(stage, segs, rbuf, acc, first):
         steps = segs[0][0][0] - 1
         for s in range(steps):
             waits = []
@@ -154,10 +156,12 @@
                 size, p = axis[0], pos(axis)
                 for d in range(2):
                     sign = 1 if d == 0 else -1
-                    src = own((p - sign * (s + 1) + 2 * size) % size, d) if s == 0 else acc.at[h, d, s - 1]
+                    src = first[h]((p - sign * (s + 1) + 2 * size) % size, d) if s == 0 else acc.at[h, d, s - 1]
                     waits.append((h, d, send(stage, h, d, s, axis, src, rbuf.at[h, d, s], rbuf.at[h, d, s])))
             for h, d, copy in waits:
                 copy.wait_recv()
+            if s == 0:
+                load.wait()
             for h, (axis, own, final) in enumerate(segs):
                 size, p = axis[0], pos(axis)
                 for d in range(2):
@@ -241,7 +245,8 @@
                      o_ref.at[:, cols(base + p2 * w2, w2)]))
         seg3.append((a2, lambda j, base=base: o_ref.at[:, cols(base + j * w2, w2)]))
         seg4.append((a1, lambda j, d, h=h: o_ref.at[:, cols(h * half + j * w1 + d * q1, q1)]))
-    reduce_scatter(0, seg1, rbuf1, acc1)
+    firsts = [lambda j, d, h=h: x_hbm.at[:, cols(h * half + j * w1 + d * q1, q1)] for h in range(2)]
+    reduce_scatter(0, seg1, rbuf1, acc1, firsts)
     direct_reduce_scatter(1, seg2, rbuf2, w2)
     direct_all_gather(2, seg3)
     all_gather(3, seg4)
@@ -259,13 +264,15 @@
     return pl.pallas_call(
         functools.partial(allreduce_kernel, axes),
         out_shape=jax.ShapeDtypeStruct((rows, width), jnp.float32),
-        in_specs=[pl.BlockSpec(memory_space=pltpu.VMEM)],
+        in_specs=[pl.BlockSpec(memory_space=pl.ANY)],
         out_specs=pl.BlockSpec(memory_space=pltpu.VMEM),
         scratch_shapes=[
+            pltpu.VMEM((rows, width), jnp.float32),
             pltpu.VMEM((2, rows, w1), jnp.float32),
             pltpu.VMEM((2, 2, steps, rows, w1 // 2), jnp.float32),
             pltpu.VMEM((2, 2, steps, rows, w1 // 2), jnp.float32),
             pltpu.VMEM((2, steps, rows, w2), jnp.float32),
+            pltpu.SemaphoreType.DMA(()),
             pltpu.SemaphoreType.DMA((4, 2, 2, steps)),
             pltpu.SemaphoreType.DMA((4, 2, 2, steps)),
         ],

time: 495 us -> 490 us (0.990)
  Pallas kernels: 226 us -> 221 us
    pallas_call x2, Pallas kernels: 167 us -> 162 us  [ray_allreduce(): pl.pallas_call(functools.partial(allreduce_kernel, axes), out_shape=jax.S...]
where the time goes in v13:
time: 490 us; the launch traced here: 489 us
  Pallas kernels  221 us (45%)
  blocking collectives  93.2 us (19%)
  waiting for transfers between devices  50.7 us (10%)
  other arithmetic  41.2 us (8%)
  matrix products  38.7 us (8%)
  local copies, waits for them, and re-layouts  27.4 us (6%)
  starting transfers between devices  15.8 us (3%)
    pallas_call x2, Pallas kernels, ray_allreduce(): pl.pallas_call(functools.partial(allreduce_kernel, axes), out_shape=jax.S...  162 us
    all_to_all x2, blocking collectives, fetch(): lax.all_to_all(outgoing, 'tile', split_axis=1, concat_axis=1, tiled=True)  61.7 us
    pallas_call x5, Pallas kernels, group_sum(): pl.pallas_call(functools.partial(reduce_kernel, plan), out_shape=jax.Shap...  58.8 us
    all_to_all x1, blocking collectives, adjoint(): lax.all_to_all(terms, 'tile', split_axis=1, concat_axis=1, tiled=True)  31.5 us
    all_to_all x1, waiting for transfers between devices, fetch(): lax.all_to_all(outgoing, 'tile', split_axis=1, concat_axis=1, tiled=True)  25.6 us
    all_to_all x1, waiting for transfers between devices, adjoint(): lax.all_to_all(terms, 'tile', split_axis=1, concat_axis=1, tiled=True)  25.1 us
    dot_general x3, matrix products, forward(): jnp.einsum('cnk,nrk->ncr', tiles, sensitivity, preferred_element_type=jnp...  18.1 us
    unnamed x15, local copies, waits for them, and re-layouts  15.1 us
  transfers between devices with their start and end apart: 3, of which 2 were waited for; matrix products, arithmetic and copies ran while one was open for 3% of the time, Pallas kernels for 3%

profile of v13, /device:TPU:1, one launch (start us, length us, event | category | flops | bytes accessed | tf_op | source)
XLA Modules:
  0.0 488.7 jit_solution(10347549311727585687)
XLA Ops:
  0.6 1.3 copy.25
  2.0 6.0 %all-to-all-start = ((s32[1,8,4]{2,0,1:T(1,128)}), s32[1,8,4]{2,0,1:T(1,128)S(1)}, u32[]{:S(2)}, u32[]{:S(2)}) async-start(s32[1,8,4]{2,0,1:T(1,128)} %copy.25), calls=%async_computation | async-start | bytes 8192 | tf_op jit(solution)/shard_map/all_to_all | solution.py:290
  7.9 0.8 copy.26
  8.8 1.2 multiply_reduce_fusion.4
  10.6 16.2 %shard_map.59 = f32[8,128]{1,0:T(8,128)} custom-call(f32[8,128]{1,0:T(8,128)} %scatter.16.x_ref), custom_call_target="tpu_custom_call" | custom-call | tf_op jit(solution)/shard_map/pallas_call | solution.py:80
  27.5 1.1 fusion.19
  29.3 6.3 %convert_bitcast_fusion.1 = bf16[64,32,512]{2,0,1:T(8,128)(2,1)} fusion(bf16[32,256,512]{2,1,0:T(8,128)(2,1)} %param.19, bf16[32,64,256]{2,1,0:T(8,128)(2,1)S(1)} %gather_fusion, pred[32]{0:T(512)(128)(4,1)S(1)} %compare_and_fusion.1), kind=kOutput, calls=%fused_computation.28 | convolution fusion | flops 538443776 | bytes 11534368 | tf_op jit(solution)/shard_map/cnr,nrk->cnk/dot_general | solution.py:318
  35.6 4.9 %all-to-all-start.1 = ((bf16[64,32,512]{2,0,1:T(8,128)(2,1)}), bf16[64,32,512]{2,0,1:T(8,128)(2,1)S(1)}, u32[]{:S(2)}, u32[]{:S(2)}) async-start(bf16[64,32,512]{2,0,1:T(8,128)(2,1)} %convert_bitcast_fusion.1), calls=%async_computation.1 | async-start | bytes 4194304 | tf_op jit(solution)/shard_map/all_to_all | solution.py:321
  41.8 25.1 %all-to-all-done.1 = bf16[64,32,512]{2,0,1:T(8,128)(2,1)S(1)} async-done(((bf16[64,32,512]{2,0,1:T(8,128)(2,1)}), bf16[64,32,512]{2,0,1:T(8,128)(2,1)S(1)}, u32[]{:S(2)}, u32[]{:S(2)}) %all-to-all-start.1) | async-done | bytes 2097184 | tf_op jit(solution)/shard_map/all_to_all | solution.py:321
  66.8 1.7 fusion.8
  68.6 6.3 %copy.42 = f32[8,8,48,512]{3,1,2,0:T(8,128)} copy(f32[8,8,48,512]{3,2,1,0:T(8,128)S(1)} %bitcast.109) | data formatting | bytes 12582912
  74.8 82.5 %shard_map.60 = f32[64,24576]{1,0:T(8,128)} custom-call(f32[64,24576]{1,0:T(8,128)} %bitcast.110), custom_call_target="tpu_custom_call" | custom-call | tf_op jit(solution)/shard_map/pallas_call | solution.py:264
  157.4 3.3 multiply_reduce_fusion.1
  161.3 8.0 %shard_map.61 = f32[8,128]{1,0:T(8,128)} custom-call(f32[8,128]{1,0:T(8,128)} %scatter.19.x_ref), custom_call_target="tpu_custom_call" | custom-call | tf_op jit(solution)/shard_map/pallas_call | solution.py:80
  170.0 3.2 fusion.38
  173.7 2.0 gather_fusion.1
  175.7 1.8 select_bitcast_fusion.2
  177.5 30.2 %all_to_all.30 = bf16[64,32,512]{2,0,1:T(8,128)(2,1)S(1)} all-to-all(bf16[64,32,512]{2,0,1:T(8,128)(2,1)S(1)} %select_bitcast_fusion.2), channel_id=1, replica_groups=mesh['ray'=16,'tile'=8] {'tile'}, dimensions={1} | all-to-all | bytes 4194304 | tf_op jit(solution)/shard_map/all_to_all | solution.py:303
  207.7 6.0 %fusion.42 = f32[32,64,256]{2,1,0:T(8,128)S(1)} fusion(bf16[64,32,512]{2,0,1:T(8,128)(2,1)S(1)} %all_to_all.30, bf16[32,256,512]{2,1,0:T(8,128)(2,1)} %param.19), kind=kOutput, calls=%fused_computation.79 | convolution fusion | flops 536870912 | bytes 12582912 | tf_op jit(solution)/shard_map/cnk,nrk->ncr/dot_general | solution.py:308
  213.8 2.0 fusion.6
  216.8 12.1 %shard_map.62 = f32[8,128]{1,0:T(8,128)} custom-call(f32[8,128]{1,0:T(8,128)} %scatter.20.x_ref), custom_call_target="tpu_custom_call" | custom-call | tf_op jit(solution)/shard_map/pallas_call | solution.py:80
  228.9 0.7 sqrt_bitcast_fusion.1
  230.4 5.0 %convert_bitcast_fusion = bf16[64,32,512]{2,0,1:T(8,128)(2,1)S(1)} fusion(bf16[32,256,512]{2,1,0:T(8,128)(2,1)} %param.19, bf16[32,64,256]{2,1,0:T(8,128)(2,1)S(1)} %gather_fusion.2, pred[32]{0:T(512)(128)(4,1)S(1)} %compare_and_fusion.1), kind=kOutput, calls=%fused_computation.27 | convolution fusion | flops 538443776 | bytes 11534368 | tf_op jit(solution)/shard_map/cnr,nrk->cnk/dot_general | solution.py:318
  235.4 31.5 %all_to_all.31 = bf16[64,32,512]{2,0,1:T(8,128)(2,1)S(1)} all-to-all(bf16[64,32,512]{2,0,1:T(8,128)(2,1)S(1)} %convert_bitcast_fusion), channel_id=1, replica_groups=mesh['ray'=16,'tile'=8] {'tile'}, dimensions={1} | all-to-all | bytes 4194304 | tf_op jit(solution)/shard_map/all_to_all | solution.py:321
  266.9 1.7 fusion.4
  268.6 6.3 %copy.44 = f32[8,8,48,512]{3,1,2,0:T(8,128)} copy(f32[8,8,48,512]{3,2,1,0:T(8,128)S(1)} %bitcast.108) | data formatting | bytes 12582912
  274.9 79.4 %shard_map.63 = f32[64,24576]{1,0:T(8,128)} custom-call(f32[64,24576]{1,0:T(8,128)} %bitcast.111), custom_call_target="tpu_custom_call" | custom-call | tf_op jit(solution)/shard_map/pallas_call | solution.py:264
  354.2 5.8 %multiply_reduce_fusion = f32[64]{0:T(128)S(1)} fusion(f32[64,24576]{1,0:T(8,128)} %shard_map.63, f32[64]{0:T(128)S(1)} %sqrt_bitcast_fusion.1, f32[64,24576]{1,0:T(8,128)} %shard_map.60, f32[64]{0:T(128)S(1)} %sqrt_bitcast_fusion.2), kind=kLoop, calls=%fused_computation.6 | loop fusion | flops 7864256 | bytes 12583680 | tf_op jit(solution)/shard_map/reduce_sum | solution.py:329
  360.7 10.4 %shard_map.64 = f32[8,128]{1,0:T(8,128)} custom-call(f32[8,128]{1,0:T(8,128)} %scatter.21.x_ref), custom_call_target="tpu_custom_call" | custom-call | tf_op jit(solution)/shard_map/pallas_call | solution.py:80
  371.0 0.7 sqrt_bitcast_fusion
  371.7 5.2 %fusion.10 = bf16[64,24576]{1,0:T(8,128)(2,1)S(1)} fusion(f32[64]{0:T(128)S(1)} %sqrt_bitcast_fusion, f32[64,24576]{1,0:T(8,128)} %shard_map.63, f32[64]{0:T(128)S(1)} %sqrt_bitcast_fusion.1, f32[64,24576]{1,0:T(8,128)} %shard_map.60, f32[64]{0:T(128)S(1)} %sqrt_bitcast_fusion.2), kind=kLoop, calls=%fused_computation.29 | loop fusion | flops 7864320 | bytes 15729408 | tf_op jit(solution)/shard_map/convert_element_type | solution.py:347
  377.4 2.0 gather_fusion.3
  379.4 3.2 select_bitcast_fusion.1
  382.6 5.0 %all-to-all-start.4 = ((bf16[64,32,512]{2,0,1:T(8,128)(2,1)}), bf16[64,32,512]{2,0,1:T(8,128)(2,1)S(1)}, u32[]{:S(2)}, u32[]{:S(2)}) async-start(bf16[64,32,512]{2,0,1:T(8,128)(2,1)} %select_bitcast_fusion.1), calls=%async_computation.4 | async-start | bytes 4194304 | tf_op jit(solution)/shard_map/all_to_all | solution.py:303
  387.5 0.7 multiply_divide_fusion.2
  388.3 25.6 %all-to-all-done.4 = bf16[64,32,512]{2,0,1:T(8,128)(2,1)S(1)} async-done(((bf16[64,32,512]{2,0,1:T(8,128)(2,1)}), bf16[64,32,512]{2,0,1:T(8,128)(2,1)S(1)}, u32[]{:S(2)}, u32[]{:S(2)}) %all-to-all-start.4) | async-done | bytes 2097184 | tf_op jit(solution)/shard_map/all_to_all | solution.py:303
  413.9 6.0 %fusion.43 = f32[32,64,256]{2,1,0:T(8,128)S(1)} fusion(bf16[64,32,512]{2,0,1:T(8,128)(2,1)S(1)} %all-to-all-done.4, bf16[32,256,512]{2,1,0:T(8,128)(2,1)} %param.19), kind=kOutput, calls=%fused_computation.80 | convolution fusion | flops 536870912 | bytes 12582912 | tf_op jit(solution)/shard_map/cnk,nrk->ncr/dot_general | solution.py:308
  419.9 2.0 fusion.2
  422.9 12.1 %shard_map.65 = f32[8,128]{1,0:T(8,128)} custom-call(f32[8,128]{1,0:T(8,128)} %scatter.24.x_ref), custom_call_target="tpu_custom_call" | custom-call | tf_op jit(solution)/shard_map/pallas_call | solution.py:80
  435.0 0.7 multiply_divide_fusion.1
  435.8 0.7 multiply_divide_fusion
  436.5 7.4 %fusion.39 = (bf16[64,24576]{1,0:T(8,128)(2,1)S(1)}, f32[64,24576]{1,0:T(8,128)}) fusion(f32[64]{0:T(128)S(1)} %multiply_divide_fusion, f32[64]{0:T(128)S(1)} %sqrt_bitcast_fusion, f32[64,24576]{1,0:T(8,128)} %shard_map.63, f32[64]{0:T(128)S(1)} %sqrt_bitcast_fusion.1, f32[64]{0:T(128)S(1)} %get-tuple-element.69, f32[64,24576]{1,0:T(8,128)} %shard_map.60, ...), kind=kLoop, calls=%fused_computation.78 | loop fusion | flops 15728640 | bytes 22021632 | tf_op jit(solution)/shard_map/convert_element_type | solution.py:364
  444.2 2.0 gather_fusion.4
  446.3 1.8 select_bitcast_fusion
  448.1 31.5 %all_to_all.32 = bf16[64,32,512]{2,0,1:T(8,128)(2,1)S(1)} all-to-all(bf16[64,32,512]{2,0,1:T(8,128)(2,1)S(1)} %select_bitcast_fusion), channel_id=1, replica_groups=mesh['ray'=16,'tile'=8] {'tile'}, dimensions={1} | all-to-all | bytes 4194304 | tf_op jit(solution)/shard_map/all_to_all | solution.py:303
  479.6 6.0 %fusion.44 = f32[32,64,256]{2,1,0:T(8,128)S(1)} fusion(bf16[64,32,512]{2,0,1:T(8,128)(2,1)S(1)} %all_to_all.32, bf16[32,256,512]{2,1,0:T(8,128)(2,1)} %param.19), kind=kOutput, calls=%fused_computation.81 | convolution fusion | flops 536870912 | bytes 12582912 | tf_op jit(solution)/shard_map/cnk,nrk->ncr/dot_general | solution.py:308
  485.6 2.0 fusion
  487.8 0.9 sub.19
  (39 shorter events, 9.4 us)
Async XLA Ops:
  2.0 33.6 %all-to-all-start = ((s32[1,8,4]{2,0,1:T(1,128)}), s32[1,8,4]{2,0,1:T(1,128)S(1)}, u32[]{:S(2)}, u32[]{:S(2)}) async-start(s32[1,8,4]{2,0,1:T(1,128)} %copy.25), calls=%async_computation | async-start | bytes 8192 | tf_op jit(solution)/shard_map/all_to_all | solution.py:290
  35.6 31.2 %all-to-all-start.1 = ((bf16[64,32,512]{2,0,1:T(8,128)(2,1)}), bf16[64,32,512]{2,0,1:T(8,128)(2,1)S(1)}, u32[]{:S(2)}, u32[]{:S(2)}) async-start(bf16[64,32,512]{2,0,1:T(8,128)(2,1)} %convert_bitcast_fusion.1), calls=%async_computation.1 | async-start | bytes 4194304 | tf_op jit(solution)/shard_map/all_to_all | solution.py:321
  213.7 2.1 copy-start
  216.2 13.6 %copy-start.2 = (f32[64,2048]{1,0:T(8,128)}, f32[64,2048]{1,0:T(8,128)S(1)}, u32[]{:S(2)}) copy-start(f32[64,2048]{1,0:T(8,128)S(1)} %get-tuple-element.72) | copy-start | bytes 1572868
  382.6 31.3 %all-to-all-start.4 = ((bf16[64,32,512]{2,0,1:T(8,128)(2,1)}), bf16[64,32,512]{2,0,1:T(8,128)(2,1)S(1)}, u32[]{:S(2)}, u32[]{:S(2)}) async-start(bf16[64,32,512]{2,0,1:T(8,128)(2,1)} %select_bitcast_fusion.1), calls=%async_computation.4 | async-start | bytes 4194304 | tf_op jit(solution)/shard_map/all_to_all | solution.py:303
  419.9 2.1 copy-start.3
  485.6 2.1 copy-start.1

commit v14 on v13

--- a/solution.py
+++ b/solution.py
@@ -98,7 +98,7 @@
     return ((inner, 1), (rays // inner, inner))
 
 
-def allreduce_kernel(axes, x_hbm, o_ref, x_ref, part, rbuf1, acc1, rbuf2, load_sem, send_sems, recv_sems):
+def allreduce_kernel(axes, x_hbm, o_hbm, x_ref, o_ref, part, rbuf1, acc1, rbuf2, load_sem, store_sems, send_sems, recv_sems):
     me = lax.axis_index("ray")
     tile = lax.axis_index("tile")
     rows = x_hbm.shape[0]
@@ -183,6 +183,11 @@
                     waits.append(send(stage, h, d, s, axis, src, src, landing))
             for copy in waits:
                 copy.wait_recv()
+            for h, (axis, region) in enumerate(segs):
+                size, p = axis[0], pos(axis)
+                for d in range(2):
+                    sign = 1 if d == 0 else -1
+                    store(h, (p - sign * (s + 1) + 2 * size) % size, d)
 
     def direct_reduce_scatter(stage, segs, rbuf, width):
         waits = []
@@ -233,6 +238,13 @@
             copy.wait_recv()
 
     q1, q2 = w1 // 2, w2 // 2
+    stores = []
+
+    def store(h, j, d):
+        region = cols(h * half + j * w1 + d * q1, q1)
+        copy = pltpu.make_async_copy(o_ref.at[:, region], o_hbm.at[:, region], store_sems.at[h, j, d])
+        copy.start()
+        stores.append(copy)
     seg1, seg2, seg3, seg4 = [], [], [], []
     for h, (a1, a2) in enumerate(plans):
         p1, p2 = pos(a1), pos(a2)
@@ -249,9 +261,14 @@
     reduce_scatter(0, seg1, rbuf1, acc1, firsts)
     direct_reduce_scatter(1, seg2, rbuf2, w2)
     direct_all_gather(2, seg3)
+    for h, (a1, a2) in enumerate(plans):
+        for d in range(2):
+            store(h, pos(a1), d)
     all_gather(3, seg4)
     for copy in sends:
         copy.wait_send()
+    for copy in stores:
+        copy.wait()
 
 
 def ray_allreduce(mesh, owned):
@@ -265,14 +282,16 @@
         functools.partial(allreduce_kernel, axes),
         out_shape=jax.ShapeDtypeStruct((rows, width), jnp.float32),
         in_specs=[pl.BlockSpec(memory_space=pl.ANY)],
-        out_specs=pl.BlockSpec(memory_space=pltpu.VMEM),
+        out_specs=pl.BlockSpec(memory_space=pl.ANY),
         scratch_shapes=[
+            pltpu.VMEM((rows, width), jnp.float32),
             pltpu.VMEM((rows, width), jnp.float32),
             pltpu.VMEM((2, rows, w1), jnp.float32),
             pltpu.VMEM((2, 2, steps, rows, w1 // 2), jnp.float32),
             pltpu.VMEM((2, 2, steps, rows, w1 // 2), jnp.float32),
             pltpu.VMEM((2, steps, rows, w2), jnp.float32),
             pltpu.SemaphoreType.DMA(()),
+            pltpu.SemaphoreType.DMA((2, axes[0][0], 2)),
             pltpu.SemaphoreType.DMA((4, 2, 2, steps)),
             pltpu.SemaphoreType.DMA((4, 2, 2, steps)),
         ],

time: 490 us -> 487 us (level)
  no operation moved by 1% of the time
where the time goes in v14:
time: 487 us; the launch traced here: 486 us
  Pallas kernels  218 us (45%)
  blocking collectives  93.2 us (19%)
  waiting for transfers between devices  50.7 us (10%)
  other arithmetic  41.2 us (8%)
  matrix products  38.7 us (8%)
  local copies, waits for them, and re-layouts  27.4 us (6%)
  starting transfers between devices  15.8 us (3%)
    pallas_call x2, Pallas kernels, ray_allreduce(): pl.pallas_call(functools.partial(allreduce_kernel, axes), out_shape=jax.S...  158 us
    all_to_all x2, blocking collectives, fetch(): lax.all_to_all(outgoing, 'tile', split_axis=1, concat_axis=1, tiled=True)  61.7 us
    pallas_call x5, Pallas kernels, group_sum(): pl.pallas_call(functools.partial(reduce_kernel, plan), out_shape=jax.Shap...  59.4 us
    all_to_all x1, blocking collectives, adjoint(): lax.all_to_all(terms, 'tile', split_axis=1, concat_axis=1, tiled=True)  31.6 us
    all_to_all x1, waiting for transfers between devices, fetch(): lax.all_to_all(outgoing, 'tile', split_axis=1, concat_axis=1, tiled=True)  25.6 us
    all_to_all x1, waiting for transfers between devices, adjoint(): lax.all_to_all(terms, 'tile', split_axis=1, concat_axis=1, tiled=True)  25.1 us
    dot_general x3, matrix products, forward(): jnp.einsum('cnk,nrk->ncr', tiles, sensitivity, preferred_element_type=jnp...  18.1 us
    unnamed x15, local copies, waits for them, and re-layouts  15.1 us
  transfers between devices with their start and end apart: 3, of which 2 were waited for; matrix products, arithmetic and copies ran while one was open for 3% of the time, Pallas kernels for 3%

profile of v14, /device:TPU:1, one launch (start us, length us, event | category | flops | bytes accessed | tf_op | source)
XLA Modules:
  0.0 485.9 jit_solution(3761064501721552282)
XLA Ops:
  0.6 1.3 copy.25
  2.0 6.0 %all-to-all-start = ((s32[1,8,4]{2,0,1:T(1,128)}), s32[1,8,4]{2,0,1:T(1,128)S(1)}, u32[]{:S(2)}, u32[]{:S(2)}) async-start(s32[1,8,4]{2,0,1:T(1,128)} %copy.25), calls=%async_computation | async-start | bytes 8192 | tf_op jit(solution)/shard_map/all_to_all | solution.py:309
  7.9 0.8 copy.26
  8.8 1.2 multiply_reduce_fusion.4
  10.6 16.2 %shard_map.59 = f32[8,128]{1,0:T(8,128)} custom-call(f32[8,128]{1,0:T(8,128)} %scatter.16.x_ref), custom_call_target="tpu_custom_call" | custom-call | tf_op jit(solution)/shard_map/pallas_call | solution.py:80
  27.5 1.1 fusion.19
  29.3 6.3 %convert_bitcast_fusion.1 = bf16[64,32,512]{2,0,1:T(8,128)(2,1)} fusion(bf16[32,256,512]{2,1,0:T(8,128)(2,1)} %param.19, bf16[32,64,256]{2,1,0:T(8,128)(2,1)S(1)} %gather_fusion, pred[32]{0:T(512)(128)(4,1)S(1)} %compare_and_fusion.1), kind=kOutput, calls=%fused_computation.28 | convolution fusion | flops 538443776 | bytes 11534368 | tf_op jit(solution)/shard_map/cnr,nrk->cnk/dot_general | solution.py:337
  35.6 4.9 %all-to-all-start.1 = ((bf16[64,32,512]{2,0,1:T(8,128)(2,1)}), bf16[64,32,512]{2,0,1:T(8,128)(2,1)S(1)}, u32[]{:S(2)}, u32[]{:S(2)}) async-start(bf16[64,32,512]{2,0,1:T(8,128)(2,1)} %convert_bitcast_fusion.1), calls=%async_computation.1 | async-start | bytes 4194304 | tf_op jit(solution)/shard_map/all_to_all | solution.py:340
  41.8 25.1 %all-to-all-done.1 = bf16[64,32,512]{2,0,1:T(8,128)(2,1)S(1)} async-done(((bf16[64,32,512]{2,0,1:T(8,128)(2,1)}), bf16[64,32,512]{2,0,1:T(8,128)(2,1)S(1)}, u32[]{:S(2)}, u32[]{:S(2)}) %all-to-all-start.1) | async-done | bytes 2097184 | tf_op jit(solution)/shard_map/all_to_all | solution.py:340
  66.8 1.7 fusion.8
  68.6 6.3 %copy.42 = f32[8,8,48,512]{3,1,2,0:T(8,128)} copy(f32[8,8,48,512]{3,2,1,0:T(8,128)S(1)} %bitcast.109) | data formatting | bytes 12582912
  74.8 81.3 %shard_map.60 = f32[64,24576]{1,0:T(8,128)} custom-call(f32[64,24576]{1,0:T(8,128)} %bitcast.110), custom_call_target="tpu_custom_call" | custom-call | tf_op jit(solution)/shard_map/pallas_call | solution.py:281
  156.1 3.3 multiply_reduce_fusion.1
  160.0 8.0 %shard_map.61 = f32[8,128]{1,0:T(8,128)} custom-call(f32[8,128]{1,0:T(8,128)} %scatter.19.x_ref), custom_call_target="tpu_custom_call" | custom-call | tf_op jit(solution)/shard_map/pallas_call | solution.py:80
  168.7 3.2 fusion.38
  172.3 2.0 gather_fusion.1
  174.3 1.8 select_bitcast_fusion.2
  176.2 30.2 %all_to_all.30 = bf16[64,32,512]{2,0,1:T(8,128)(2,1)S(1)} all-to-all(bf16[64,32,512]{2,0,1:T(8,128)(2,1)S(1)} %select_bitcast_fusion.2), channel_id=1, replica_groups=mesh['ray'=16,'tile'=8] {'tile'}, dimensions={1} | all-to-all | bytes 4194304 | tf_op jit(solution)/shard_map/all_to_all | solution.py:322
  206.4 6.0 %fusion.42 = f32[32,64,256]{2,1,0:T(8,128)S(1)} fusion(bf16[64,32,512]{2,0,1:T(8,128)(2,1)S(1)} %all_to_all.30, bf16[32,256,512]{2,1,0:T(8,128)(2,1)} %param.19), kind=kOutput, calls=%fused_computation.79 | convolution fusion | flops 536870912 | bytes 12582912 | tf_op jit(solution)/shard_map/cnk,nrk->ncr/dot_general | solution.py:327
  212.5 2.0 fusion.6
  215.5 12.0 %shard_map.62 = f32[8,128]{1,0:T(8,128)} custom-call(f32[8,128]{1,0:T(8,128)} %scatter.20.x_ref), custom_call_target="tpu_custom_call" | custom-call | tf_op jit(solution)/shard_map/pallas_call | solution.py:80
  227.5 0.7 sqrt_bitcast_fusion.1
  229.0 5.0 %convert_bitcast_fusion = bf16[64,32,512]{2,0,1:T(8,128)(2,1)S(1)} fusion(bf16[32,256,512]{2,1,0:T(8,128)(2,1)} %param.19, bf16[32,64,256]{2,1,0:T(8,128)(2,1)S(1)} %gather_fusion.2, pred[32]{0:T(512)(128)(4,1)S(1)} %compare_and_fusion.1), kind=kOutput, calls=%fused_computation.27 | convolution fusion | flops 538443776 | bytes 11534368 | tf_op jit(solution)/shard_map/cnr,nrk->cnk/dot_general | solution.py:337
  234.0 31.6 %all_to_all.31 = bf16[64,32,512]{2,0,1:T(8,128)(2,1)S(1)} all-to-all(bf16[64,32,512]{2,0,1:T(8,128)(2,1)S(1)} %convert_bitcast_fusion), channel_id=1, replica_groups=mesh['ray'=16,'tile'=8] {'tile'}, dimensions={1} | all-to-all | bytes 4194304 | tf_op jit(solution)/shard_map/all_to_all | solution.py:340
  265.5 1.7 fusion.4
  267.3 6.3 %copy.44 = f32[8,8,48,512]{3,1,2,0:T(8,128)} copy(f32[8,8,48,512]{3,2,1,0:T(8,128)S(1)} %bitcast.108) | data formatting | bytes 12582912
  273.5 77.2 %shard_map.63 = f32[64,24576]{1,0:T(8,128)} custom-call(f32[64,24576]{1,0:T(8,128)} %bitcast.111), custom_call_target="tpu_custom_call" | custom-call | tf_op jit(solution)/shard_map/pallas_call | solution.py:281
  350.8 5.8 %multiply_reduce_fusion = f32[64]{0:T(128)S(1)} fusion(f32[64,24576]{1,0:T(8,128)} %shard_map.63, f32[64]{0:T(128)S(1)} %sqrt_bitcast_fusion.1, f32[64,24576]{1,0:T(8,128)} %shard_map.60, f32[64]{0:T(128)S(1)} %sqrt_bitcast_fusion.2), kind=kLoop, calls=%fused_computation.6 | loop fusion | flops 7864256 | bytes 12583680 | tf_op jit(solution)/shard_map/reduce_sum | solution.py:348
  357.2 11.1 %shard_map.64 = f32[8,128]{1,0:T(8,128)} custom-call(f32[8,128]{1,0:T(8,128)} %scatter.21.x_ref), custom_call_target="tpu_custom_call" | custom-call | tf_op jit(solution)/shard_map/pallas_call | solution.py:80
  368.3 0.7 sqrt_bitcast_fusion
  369.0 5.2 %fusion.10 = bf16[64,24576]{1,0:T(8,128)(2,1)S(1)} fusion(f32[64]{0:T(128)S(1)} %sqrt_bitcast_fusion, f32[64,24576]{1,0:T(8,128)} %shard_map.63, f32[64]{0:T(128)S(1)} %sqrt_bitcast_fusion.1, f32[64,24576]{1,0:T(8,128)} %shard_map.60, f32[64]{0:T(128)S(1)} %sqrt_bitcast_fusion.2), kind=kLoop, calls=%fused_computation.29 | loop fusion | flops 7864320 | bytes 15729408 | tf_op jit(solution)/shard_map/convert_element_type | solution.py:366
  374.6 2.0 gather_fusion.3
  376.6 3.2 select_bitcast_fusion.1
  379.8 5.0 %all-to-all-start.4 = ((bf16[64,32,512]{2,0,1:T(8,128)(2,1)}), bf16[64,32,512]{2,0,1:T(8,128)(2,1)S(1)}, u32[]{:S(2)}, u32[]{:S(2)}) async-start(bf16[64,32,512]{2,0,1:T(8,128)(2,1)} %select_bitcast_fusion.1), calls=%async_computation.4 | async-start | bytes 4194304 | tf_op jit(solution)/shard_map/all_to_all | solution.py:322
  384.8 0.7 multiply_divide_fusion.2
  385.5 25.6 %all-to-all-done.4 = bf16[64,32,512]{2,0,1:T(8,128)(2,1)S(1)} async-done(((bf16[64,32,512]{2,0,1:T(8,128)(2,1)}), bf16[64,32,512]{2,0,1:T(8,128)(2,1)S(1)}, u32[]{:S(2)}, u32[]{:S(2)}) %all-to-all-start.4) | async-done | bytes 2097184 | tf_op jit(solution)/shard_map/all_to_all | solution.py:322
  411.1 6.0 %fusion.43 = f32[32,64,256]{2,1,0:T(8,128)S(1)} fusion(bf16[64,32,512]{2,0,1:T(8,128)(2,1)S(1)} %all-to-all-done.4, bf16[32,256,512]{2,1,0:T(8,128)(2,1)} %param.19), kind=kOutput, calls=%fused_computation.80 | convolution fusion | flops 536870912 | bytes 12582912 | tf_op jit(solution)/shard_map/cnk,nrk->ncr/dot_general | solution.py:327
  417.1 2.0 fusion.2
  420.1 12.1 %shard_map.65 = f32[8,128]{1,0:T(8,128)} custom-call(f32[8,128]{1,0:T(8,128)} %scatter.24.x_ref), custom_call_target="tpu_custom_call" | custom-call | tf_op jit(solution)/shard_map/pallas_call | solution.py:80
  432.3 0.7 multiply_divide_fusion.1
  433.0 0.7 multiply_divide_fusion
  433.7 7.4 %fusion.39 = (bf16[64,24576]{1,0:T(8,128)(2,1)S(1)}, f32[64,24576]{1,0:T(8,128)}) fusion(f32[64]{0:T(128)S(1)} %multiply_divide_fusion, f32[64]{0:T(128)S(1)} %sqrt_bitcast_fusion, f32[64,24576]{1,0:T(8,128)} %shard_map.63, f32[64]{0:T(128)S(1)} %sqrt_bitcast_fusion.1, f32[64]{0:T(128)S(1)} %get-tuple-element.69, f32[64,24576]{1,0:T(8,128)} %shard_map.60, ...), kind=kLoop, calls=%fused_computation.78 | loop fusion | flops 15728640 | bytes 22021632 | tf_op jit(solution)/shard_map/convert_element_type | solution.py:383
  441.5 2.0 gather_fusion.4
  443.5 1.8 select_bitcast_fusion
  445.3 31.5 %all_to_all.32 = bf16[64,32,512]{2,0,1:T(8,128)(2,1)S(1)} all-to-all(bf16[64,32,512]{2,0,1:T(8,128)(2,1)S(1)} %select_bitcast_fusion), channel_id=1, replica_groups=mesh['ray'=16,'tile'=8] {'tile'}, dimensions={1} | all-to-all | bytes 4194304 | tf_op jit(solution)/shard_map/all_to_all | solution.py:322
  476.8 6.0 %fusion.44 = f32[32,64,256]{2,1,0:T(8,128)S(1)} fusion(bf16[64,32,512]{2,0,1:T(8,128)(2,1)S(1)} %all_to_all.32, bf16[32,256,512]{2,1,0:T(8,128)(2,1)} %param.19), kind=kOutput, calls=%fused_computation.81 | convolution fusion | flops 536870912 | bytes 12582912 | tf_op jit(solution)/shard_map/cnk,nrk->ncr/dot_general | solution.py:327
  482.9 2.0 fusion
  485.0 0.9 sub.19
  (39 shorter events, 9.4 us)
Async XLA Ops:
  2.0 33.6 %all-to-all-start = ((s32[1,8,4]{2,0,1:T(1,128)}), s32[1,8,4]{2,0,1:T(1,128)S(1)}, u32[]{:S(2)}, u32[]{:S(2)}) async-start(s32[1,8,4]{2,0,1:T(1,128)} %copy.25), calls=%async_computation | async-start | bytes 8192 | tf_op jit(solution)/shard_map/all_to_all | solution.py:309
  35.6 31.2 %all-to-all-start.1 = ((bf16[64,32,512]{2,0,1:T(8,128)(2,1)}), bf16[64,32,512]{2,0,1:T(8,128)(2,1)S(1)}, u32[]{:S(2)}, u32[]{:S(2)}) async-start(bf16[64,32,512]{2,0,1:T(8,128)(2,1)} %convert_bitcast_fusion.1), calls=%async_computation.1 | async-start | bytes 4194304 | tf_op jit(solution)/shard_map/all_to_all | solution.py:340
  212.4 2.1 copy-start
  214.9 13.5 %copy-start.2 = (f32[64,2048]{1,0:T(8,128)}, f32[64,2048]{1,0:T(8,128)S(1)}, u32[]{:S(2)}) copy-start(f32[64,2048]{1,0:T(8,128)S(1)} %get-tuple-element.72) | copy-start | bytes 1572868
  379.8 31.3 %all-to-all-start.4 = ((bf16[64,32,512]{2,0,1:T(8,128)(2,1)}), bf16[64,32,512]{2,0,1:T(8,128)(2,1)S(1)}, u32[]{:S(2)}, u32[]{:S(2)}) async-start(bf16[64,32,512]{2,0,1:T(8,128)(2,1)} %select_bitcast_fusion.1), calls=%async_computation.4 | async-start | bytes 4194304 | tf_op jit(solution)/shard_map/all_to_all | solution.py:322
  417.1 2.1 copy-start.3
  482.8 2.1 copy-start.1

commit v15 on v14

--- a/solution.py
+++ b/solution.py
@@ -318,7 +318,7 @@
 
     def fetch(field_bf):
         owned = field_bf.reshape(columns, TILE_DEV, CB)
-        outgoing = jnp.take(owned, requests, axis=1)
+        outgoing = jnp.take(owned, requests, axis=1, mode="clip")
         tiles = lax.all_to_all(outgoing, "tile", split_axis=1, concat_axis=1, tiled=True)
         return tiles
 
@@ -333,7 +333,7 @@
         return summed.reshape(columns, BUND_DEV * RB)
 
     def adjoint(rays_bf):
-        picked = jnp.take(rays_bf.reshape(columns, BUND_DEV, RB), bundles, axis=1)
+        picked = jnp.take(rays_bf.reshape(columns, BUND_DEV, RB), bundles, axis=1, mode="clip")
         terms = jnp.einsum(
             "cnr,nrk->cnk", picked, sensitivity, preferred_element_type=jnp.float32
         ).astype(jnp.bfloat16)

time: 487 us -> 481 us (0.988)
  other arithmetic: 41.2 us -> 34.3 us
    select_n x5 -> x0, other arithmetic: 6.85 us -> none  [the longest x4 6.85 us: fetch(): outgoing = jnp.take(owned, requests, axis=1)]
where the time goes in v15:
time: 481 us; the launch traced here: 480 us
  Pallas kernels  218 us (45%)
  blocking collectives  93.6 us (19%)
  waiting for transfers between devices  50.7 us (11%)
  matrix products  38.7 us (8%)
  other arithmetic  34.3 us (7%)
  local copies, waits for them, and re-layouts  27.4 us (6%)
  starting transfers between devices  15.8 us (3%)
    pallas_call x2, Pallas kernels, ray_allreduce(): pl.pallas_call(functools.partial(allreduce_kernel, axes), out_shape=jax.S...  158 us
    all_to_all x2, blocking collectives, fetch(): lax.all_to_all(outgoing, 'tile', split_axis=1, concat_axis=1, tiled=True)  62.3 us
    pallas_call x5, Pallas kernels, group_sum(): pl.pallas_call(functools.partial(reduce_kernel, plan), out_shape=jax.Shap...  60.4 us
    all_to_all x1, blocking collectives, adjoint(): lax.all_to_all(terms, 'tile', split_axis=1, concat_axis=1, tiled=True)  31.3 us
    all_to_all x1, waiting for transfers between devices, fetch(): lax.all_to_all(outgoing, 'tile', split_axis=1, concat_axis=1, tiled=True)  25.6 us
    all_to_all x1, waiting for transfers between devices, adjoint(): lax.all_to_all(terms, 'tile', split_axis=1, concat_axis=1, tiled=True)  25.1 us
    dot_general x3, matrix products, forward(): jnp.einsum('cnk,nrk->ncr', tiles, sensitivity, preferred_element_type=jnp...  18.1 us
    unnamed x15, local copies, waits for them, and re-layouts  15.1 us
  transfers between devices with their start and end apart: 3, of which 2 were waited for; matrix products, arithmetic and copies ran while one was open for 3% of the time, Pallas kernels for 3%

profile of v15, /device:TPU:1, one launch (start us, length us, event | category | flops | bytes accessed | tf_op | source)
XLA Modules:
  0.0 479.7 jit_solution(5378982420714912095)
XLA Ops:
  0.6 1.3 copy.25
  2.0 6.0 %all-to-all-start = ((s32[1,8,4]{2,0,1:T(1,128)}), s32[1,8,4]{2,0,1:T(1,128)S(1)}, u32[]{:S(2)}, u32[]{:S(2)}) async-start(s32[1,8,4]{2,0,1:T(1,128)} %copy.25), calls=%async_computation | async-start | bytes 8192 | tf_op jit(solution)/shard_map/all_to_all | solution.py:309
  7.9 1.2 multiply_reduce_fusion.4
  9.7 16.2 %shard_map.59 = f32[8,128]{1,0:T(8,128)} custom-call(f32[8,128]{1,0:T(8,128)} %scatter.16.x_ref), custom_call_target="tpu_custom_call" | custom-call | tf_op jit(solution)/shard_map/pallas_call | solution.py:80
  25.9 0.7 sqrt_bitcast_fusion.3
  26.6 0.8 copy.26
  27.5 1.1 fusion.13
  29.3 6.3 %convert_bitcast_fusion.1 = bf16[64,32,512]{2,0,1:T(8,128)(2,1)} fusion(bf16[32,256,512]{2,1,0:T(8,128)(2,1)} %param.15, bf16[32,64,256]{2,1,0:T(8,128)(2,1)S(1)} %gather_fusion), kind=kOutput, calls=%fused_computation.25 | convolution fusion | flops 537919488 | bytes 11534336 | tf_op jit(solution)/shard_map/cnr,nrk->cnk/dot_general | solution.py:337
  35.5 4.9 %all-to-all-start.1 = ((bf16[64,32,512]{2,0,1:T(8,128)(2,1)}), bf16[64,32,512]{2,0,1:T(8,128)(2,1)S(1)}, u32[]{:S(2)}, u32[]{:S(2)}) async-start(bf16[64,32,512]{2,0,1:T(8,128)(2,1)} %convert_bitcast_fusion.1), calls=%async_computation.1 | async-start | bytes 4194304 | tf_op jit(solution)/shard_map/all_to_all | solution.py:340
  40.9 0.7 reduce.13
  41.7 25.1 %all-to-all-done.1 = bf16[64,32,512]{2,0,1:T(8,128)(2,1)S(1)} async-done(((bf16[64,32,512]{2,0,1:T(8,128)(2,1)}), bf16[64,32,512]{2,0,1:T(8,128)(2,1)S(1)}, u32[]{:S(2)}, u32[]{:S(2)}) %all-to-all-start.1) | async-done | bytes 2097184 | tf_op jit(solution)/shard_map/all_to_all | solution.py:340
  66.8 1.7 fusion.8
  68.5 6.3 %copy.42 = f32[8,8,48,512]{3,1,2,0:T(8,128)} copy(f32[8,8,48,512]{3,2,1,0:T(8,128)S(1)} %bitcast.106) | data formatting | bytes 12582912
  74.8 81.3 %shard_map.60 = f32[64,24576]{1,0:T(8,128)} custom-call(f32[64,24576]{1,0:T(8,128)} %bitcast.107), custom_call_target="tpu_custom_call" | custom-call | tf_op jit(solution)/shard_map/pallas_call | solution.py:281
  156.1 3.3 multiply_reduce_fusion.1
  160.0 8.0 %shard_map.61 = f32[8,128]{1,0:T(8,128)} custom-call(f32[8,128]{1,0:T(8,128)} %scatter.19.x_ref), custom_call_target="tpu_custom_call" | custom-call | tf_op jit(solution)/shard_map/pallas_call | solution.py:80
  167.9 0.7 sqrt_bitcast_fusion.2
  168.6 3.2 fusion.30
  172.3 2.0 gather_fusion.1
  174.3 30.7 %all_to_all.30 = bf16[64,32,512]{2,0,1:T(8,128)(2,1)S(1)} all-to-all(bf16[64,32,512]{2,0,1:T(8,128)(2,1)} %bitcast.117), channel_id=1, replica_groups=mesh['ray'=16,'tile'=8] {'tile'}, dimensions={1} | all-to-all | bytes 4194304 | tf_op jit(solution)/shard_map/all_to_all | solution.py:322
  205.0 6.0 %fusion.34 = f32[32,64,256]{2,1,0:T(8,128)S(1)} fusion(bf16[64,32,512]{2,0,1:T(8,128)(2,1)S(1)} %all_to_all.30, bf16[32,256,512]{2,1,0:T(8,128)(2,1)} %param.15), kind=kOutput, calls=%fused_computation.64 | convolution fusion | flops 536870912 | bytes 12582912 | tf_op jit(solution)/shard_map/cnk,nrk->ncr/dot_general | solution.py:327
  211.0 2.0 fusion.6
  214.1 12.9 %shard_map.62 = f32[8,128]{1,0:T(8,128)} custom-call(f32[8,128]{1,0:T(8,128)} %scatter.20.x_ref), custom_call_target="tpu_custom_call" | custom-call | tf_op jit(solution)/shard_map/pallas_call | solution.py:80
  227.0 0.7 sqrt_bitcast_fusion.1
  228.4 5.0 %convert_bitcast_fusion = bf16[64,32,512]{2,0,1:T(8,128)(2,1)S(1)} fusion(bf16[32,256,512]{2,1,0:T(8,128)(2,1)} %param.15, bf16[32,64,256]{2,1,0:T(8,128)(2,1)S(1)} %gather_fusion.2), kind=kOutput, calls=%fused_computation.24 | convolution fusion | flops 537919488 | bytes 11534336 | tf_op jit(solution)/shard_map/cnr,nrk->cnk/dot_general | solution.py:337
  233.4 31.3 %all_to_all.31 = bf16[64,32,512]{2,0,1:T(8,128)(2,1)S(1)} all-to-all(bf16[64,32,512]{2,0,1:T(8,128)(2,1)S(1)} %convert_bitcast_fusion), channel_id=1, replica_groups=mesh['ray'=16,'tile'=8] {'tile'}, dimensions={1} | all-to-all | bytes 4194304 | tf_op jit(solution)/shard_map/all_to_all | solution.py:340
  264.6 1.7 fusion.4
  266.4 6.3 %copy.44 = f32[8,8,48,512]{3,1,2,0:T(8,128)} copy(f32[8,8,48,512]{3,2,1,0:T(8,128)S(1)} %bitcast.105) | data formatting | bytes 12582912
  272.7 76.6 %shard_map.63 = f32[64,24576]{1,0:T(8,128)} custom-call(f32[64,24576]{1,0:T(8,128)} %bitcast.108), custom_call_target="tpu_custom_call" | custom-call | tf_op jit(solution)/shard_map/pallas_call | solution.py:281
  349.3 5.8 %multiply_reduce_fusion = f32[64]{0:T(128)S(1)} fusion(f32[64,24576]{1,0:T(8,128)} %shard_map.63, f32[64]{0:T(128)S(1)} %sqrt_bitcast_fusion.1, f32[64,24576]{1,0:T(8,128)} %shard_map.60, f32[64]{0:T(128)S(1)} %sqrt_bitcast_fusion.2), kind=kLoop, calls=%fused_computation.6 | loop fusion | flops 7864256 | bytes 12583680 | tf_op jit(solution)/shard_map/reduce_sum | solution.py:348
  355.7 11.4 %shard_map.64 = f32[8,128]{1,0:T(8,128)} custom-call(f32[8,128]{1,0:T(8,128)} %scatter.21.x_ref), custom_call_target="tpu_custom_call" | custom-call | tf_op jit(solution)/shard_map/pallas_call | solution.py:80
  367.1 0.7 sqrt_bitcast_fusion
  367.7 5.2 %fusion.10 = bf16[64,24576]{1,0:T(8,128)(2,1)S(1)} fusion(f32[64]{0:T(128)S(1)} %sqrt_bitcast_fusion, f32[64,24576]{1,0:T(8,128)} %shard_map.63, f32[64]{0:T(128)S(1)} %sqrt_bitcast_fusion.1, f32[64,24576]{1,0:T(8,128)} %shard_map.60, f32[64]{0:T(128)S(1)} %sqrt_bitcast_fusion.2), kind=kLoop, calls=%fused_computation.26 | loop fusion | flops 7864320 | bytes 15729408 | tf_op jit(solution)/shard_map/convert_element_type | solution.py:366
  373.4 2.0 gather_fusion.3
  375.4 5.0 %all-to-all-start.4 = ((bf16[64,32,512]{2,0,1:T(8,128)(2,1)}), bf16[64,32,512]{2,0,1:T(8,128)(2,1)S(1)}, u32[]{:S(2)}, u32[]{:S(2)}) async-start(bf16[64,32,512]{2,0,1:T(8,128)(2,1)} %bitcast.115), calls=%async_computation.4 | async-start | bytes 4194304 | tf_op jit(solution)/shard_map/all_to_all | solution.py:322
  380.4 0.7 multiply_divide_fusion.2
  381.1 25.6 %all-to-all-done.4 = bf16[64,32,512]{2,0,1:T(8,128)(2,1)S(1)} async-done(((bf16[64,32,512]{2,0,1:T(8,128)(2,1)}), bf16[64,32,512]{2,0,1:T(8,128)(2,1)S(1)}, u32[]{:S(2)}, u32[]{:S(2)}) %all-to-all-start.4) | async-done | bytes 2097184 | tf_op jit(solution)/shard_map/all_to_all | solution.py:322
  406.7 6.0 %fusion.35 = f32[32,64,256]{2,1,0:T(8,128)S(1)} fusion(bf16[64,32,512]{2,0,1:T(8,128)(2,1)S(1)} %all-to-all-done.4, bf16[32,256,512]{2,1,0:T(8,128)(2,1)} %param.15), kind=kOutput, calls=%fused_computation.65 | convolution fusion | flops 536870912 | bytes 12582912 | tf_op jit(solution)/shard_map/cnk,nrk->ncr/dot_general | solution.py:327
  412.7 2.0 fusion.2
  415.7 12.0 %shard_map.65 = f32[8,128]{1,0:T(8,128)} custom-call(f32[8,128]{1,0:T(8,128)} %scatter.24.x_ref), custom_call_target="tpu_custom_call" | custom-call | tf_op jit(solution)/shard_map/pallas_call | solution.py:80
  427.7 0.7 multiply_divide_fusion.1
  428.5 0.7 multiply_divide_fusion
  429.2 7.4 %fusion.31 = (bf16[64,24576]{1,0:T(8,128)(2,1)S(1)}, f32[64,24576]{1,0:T(8,128)}) fusion(f32[64]{0:T(128)S(1)} %multiply_divide_fusion, f32[64]{0:T(128)S(1)} %sqrt_bitcast_fusion, f32[64,24576]{1,0:T(8,128)} %shard_map.63, f32[64]{0:T(128)S(1)} %sqrt_bitcast_fusion.1, f32[64]{0:T(128)S(1)} %get-tuple-element.67, f32[64,24576]{1,0:T(8,128)} %shard_map.60, ...), kind=kLoop, calls=%fused_computation.63 | loop fusion | flops 15728640 | bytes 22021632 | tf_op jit(solution)/shard_map/convert_element_type | solution.py:383
  436.9 2.0 gather_fusion.4
  439.0 31.7 %all_to_all.32 = bf16[64,32,512]{2,0,1:T(8,128)(2,1)S(1)} all-to-all(bf16[64,32,512]{2,0,1:T(8,128)(2,1)} %bitcast.116), channel_id=1, replica_groups=mesh['ray'=16,'tile'=8] {'tile'}, dimensions={1} | all-to-all | bytes 4194304 | tf_op jit(solution)/shard_map/all_to_all | solution.py:322
  470.6 6.0 %fusion.36 = f32[32,64,256]{2,1,0:T(8,128)S(1)} fusion(bf16[64,32,512]{2,0,1:T(8,128)(2,1)S(1)} %all_to_all.32, bf16[32,256,512]{2,1,0:T(8,128)(2,1)} %param.15), kind=kOutput, calls=%fused_computation.66 | convolution fusion | flops 536870912 | bytes 12582912 | tf_op jit(solution)/shard_map/cnk,nrk->ncr/dot_general | solution.py:327
  476.7 2.0 fusion
  478.8 0.9 sub.19
  (32 shorter events, 7.4 us)
Async XLA Ops:
  2.0 33.6 %all-to-all-start = ((s32[1,8,4]{2,0,1:T(1,128)}), s32[1,8,4]{2,0,1:T(1,128)S(1)}, u32[]{:S(2)}, u32[]{:S(2)}) async-start(s32[1,8,4]{2,0,1:T(1,128)} %copy.25), calls=%async_computation | async-start | bytes 8192 | tf_op jit(solution)/shard_map/all_to_all | solution.py:309
  35.5 31.2 %all-to-all-start.1 = ((bf16[64,32,512]{2,0,1:T(8,128)(2,1)}), bf16[64,32,512]{2,0,1:T(8,128)(2,1)S(1)}, u32[]{:S(2)}, u32[]{:S(2)}) async-start(bf16[64,32,512]{2,0,1:T(8,128)(2,1)} %convert_bitcast_fusion.1), calls=%async_computation.1 | async-start | bytes 4194304 | tf_op jit(solution)/shard_map/all_to_all | solution.py:340
  211.0 2.1 copy-start
  213.4 14.4 %copy-start.2 = (f32[64,2048]{1,0:T(8,128)}, f32[64,2048]{1,0:T(8,128)S(1)}, u32[]{:S(2)}) copy-start(f32[64,2048]{1,0:T(8,128)S(1)} %get-tuple-element.70) | copy-start | bytes 1572868
  375.4 31.3 %all-to-all-start.4 = ((bf16[64,32,512]{2,0,1:T(8,128)(2,1)}), bf16[64,32,512]{2,0,1:T(8,128)(2,1)S(1)}, u32[]{:S(2)}, u32[]{:S(2)}) async-start(bf16[64,32,512]{2,0,1:T(8,128)(2,1)} %bitcast.115), calls=%async_computation.4 | async-start | bytes 4194304 | tf_op jit(solution)/shard_map/all_to_all | solution.py:322
  412.7 2.1 copy-start.3
  476.7 2.1 copy-start.1

commit v16 on v9

--- a/solution.py
+++ b/solution.py
@@ -106,11 +106,11 @@
     return ((inner, 1), (rays // inner, inner))
 
 
-def allreduce_kernel(axes, x_ref, o_ref, part, rbuf1, acc1, rbuf2, send_sems, recv_sems):
+def allreduce_kernel(axes, x_hbm, o_hbm, x_ref, o_ref, part, rbuf1, acc1, rbuf2, load_sem, store_sems, send_sems, recv_sems):
     me = lax.axis_index("ray")
     tile = lax.axis_index("tile")
-    rows = x_ref.shape[0]
-    half = x_ref.shape[1] // 2
+    rows = x_hbm.shape[0]
+    half = x_hbm.shape[1] // 2
     w1 = half // axes[0][0]
     w2 = w1 // axes[1][0]
 
@@ -133,6 +133,8 @@
             return carry
         lax.fori_loop(0, rows // 8, body, 0)
 
+    load = pltpu.make_async_copy(x_hbm, x_ref, load_sem)
+    load.start()
     barrier = pltpu.get_barrier_semaphore()
     greeted = 0
     for axis in axes:
@@ -154,7 +156,7 @@
         sends.append(copy)
         return pltpu.make_async_remote_copy(src_ref=src, dst_ref=landing, **sems)
 
-    def reduce_scatter(stage, segs, rbuf, acc):
+    def reduce_scatter(stage, segs, rbuf, acc, first):
         steps = segs[0][0][0] - 1
         for s in range(steps):
             waits = []
@@ -162,10 +164,12 @@
                 size, p = axis[0], pos(axis)
                 for d in range(2):
                     sign = 1 if d == 0 else -1
-                    src = own((p - sign * (s + 1) + 2 * size) % size, d) if s == 0 else acc.at[h, d, s - 1]
+                    src = first[h]((p - sign * (s + 1) + 2 * size) % size, d) if s == 0 else acc.at[h, d, s - 1]
                     waits.append((h, d, send(stage, h, d, s, axis, src, rbuf.at[h, d, s], rbuf.at[h, d, s])))
             for h, d, copy in waits:
                 copy.wait_recv()
+            if s == 0:
+                load.wait()
             for h, (axis, own, final) in enumerate(segs):
                 size, p = axis[0], pos(axis)
                 for d in range(2):
@@ -187,6 +191,11 @@
                     waits.append(send(stage, h, d, s, axis, src, src, landing))
             for copy in waits:
                 copy.wait_recv()
+            for h, (axis, region) in enumerate(segs):
+                size, p = axis[0], pos(axis)
+                for d in range(2):
+                    sign = 1 if d == 0 else -1
+                    store(h, (p - sign * (s + 1) + 2 * size) % size, d)
 
     def direct_reduce_scatter(stage, segs, rbuf, width):
         waits = []
@@ -237,6 +246,13 @@
             copy.wait_recv()
 
     q1, q2 = w1 // 2, w2 // 2
+    stores = []
+
+    def store(h, j, d):
+        region = cols(h * half + j * w1 + d * q1, q1)
+        copy = pltpu.make_async_copy(o_ref.at[:, region], o_hbm.at[:, region], store_sems.at[h, j, d])
+        copy.start()
+        stores.append(copy)
     seg1, seg2, seg3, seg4 = [], [], [], []
     for h, (a1, a2) in enumerate(plans):
         p1, p2 = pos(a1), pos(a2)
@@ -249,12 +265,18 @@
                      o_ref.at[:, cols(base + p2 * w2, w2)]))
         seg3.append((a2, lambda j, base=base: o_ref.at[:, cols(base + j * w2, w2)]))
         seg4.append((a1, lambda j, d, h=h: o_ref.at[:, cols(h * half + j * w1 + d * q1, q1)]))
-    reduce_scatter(0, seg1, rbuf1, acc1)
+    firsts = [lambda j, d, h=h: x_hbm.at[:, cols(h * half + j * w1 + d * q1, q1)] for h in range(2)]
+    reduce_scatter(0, seg1, rbuf1, acc1, firsts)
     direct_reduce_scatter(1, seg2, rbuf2, w2)
     direct_all_gather(2, seg3)
+    for h, (a1, a2) in enumerate(plans):
+        for d in range(2):
+            store(h, pos(a1), d)
     all_gather(3, seg4)
     for copy in sends:
         copy.wait_send()
+    for copy in stores:
+        copy.wait()
 
 
 def ray_allreduce(mesh, owned):
@@ -267,13 +289,17 @@
     return pl.pallas_call(
         functools.partial(allreduce_kernel, axes),
         out_shape=jax.ShapeDtypeStruct((rows, width), jnp.float32),
-        in_specs=[pl.BlockSpec(memory_space=pltpu.VMEM)],
-        out_specs=pl.BlockSpec(memory_space=pltpu.VMEM),
+        in_specs=[pl.BlockSpec(memory_space=pl.ANY)],
+        out_specs=pl.BlockSpec(memory_space=pl.ANY),
         scratch_shapes=[
+            pltpu.VMEM((rows, width), jnp.float32),
+            pltpu.VMEM((rows, width), jnp.float32),
             pltpu.VMEM((2, rows, w1), jnp.float32),
             pltpu.VMEM((2, 2, steps, rows, w1 // 2), jnp.float32),
             pltpu.VMEM((2, 2, steps, rows, w1 // 2), jnp.float32),
             pltpu.VMEM((2, steps, rows, w2), jnp.float32),
+            pltpu.SemaphoreType.DMA(()),
+            pltpu.SemaphoreType.DMA((2, axes[0][0], 2)),
             pltpu.SemaphoreType.DMA((4, 2, 2, steps)),
             pltpu.SemaphoreType.DMA((4, 2, 2, steps)),
         ],
@@ -300,7 +326,7 @@
 
     def fetch(field_bf):
         owned = field_bf.reshape(columns, TILE_DEV, CB)
-        outgoing = jnp.take(owned, requests, axis=1)
+        outgoing = jnp.take(owned, requests, axis=1, mode="clip")
         tiles = lax.all_to_all(outgoing, "tile", split_axis=1, concat_axis=1, tiled=True)
         return tiles
 
@@ -315,7 +341,7 @@
         return summed.reshape(columns, BUND_DEV * RB)
 
     def adjoint(rays_bf):
-        picked = jnp.take(rays_bf.reshape(columns, BUND_DEV, RB), bundles, axis=1)
+        picked = jnp.take(rays_bf.reshape(columns, BUND_DEV, RB), bundles, axis=1, mode="clip")
         terms = jnp.einsum(
             "cnr,nrk->cnk", picked, sensitivity, preferred_element_type=jnp.float32
         ).astype(jnp.bfloat16)

time: 496 us -> 481 us (0.970)
  Pallas kernels: 226 us -> 219 us
  other arithmetic: 41.2 us -> 34.3 us
    pallas_call x2, Pallas kernels: 166 us -> 158 us  [ray_allreduce(): pl.pallas_call(functools.partial(allreduce_kernel, axes), out_shape=jax.S...]
    select_n x5 -> x0, other arithmetic: 6.85 us -> none  [the longest x4 6.85 us: fetch(): outgoing = jnp.take(owned, requests, axis=1)]
where the time goes in v16:
time: 481 us; the launch traced here: 480 us
  Pallas kernels  219 us (46%)
  blocking collectives  93.5 us (19%)
  waiting for transfers between devices  50.7 us (11%)
  matrix products  38.7 us (8%)
  other arithmetic  34.3 us (7%)
  local copies, waits for them, and re-layouts  27.4 us (6%)
  starting transfers between devices  15.8 us (3%)
    pallas_call x2, Pallas kernels, ray_allreduce(): pl.pallas_call(functools.partial(allreduce_kernel, axes), out_shape=jax.S...  158 us
    all_to_all x2, blocking collectives, fetch(): lax.all_to_all(outgoing, 'tile', split_axis=1, concat_axis=1, tiled=True)  62.2 us
    pallas_call x5, Pallas kernels, group_sum(): pl.pallas_call(functools.partial(reduce_kernel, plan), out_shape=jax.Shap...  60.9 us
    all_to_all x1, blocking collectives, adjoint(): lax.all_to_all(terms, 'tile', split_axis=1, concat_axis=1, tiled=True)  31.3 us
    all_to_all x1, waiting for transfers between devices, fetch(): lax.all_to_all(outgoing, 'tile', split_axis=1, concat_axis=1, tiled=True)  25.6 us
    all_to_all x1, waiting for transfers between devices, adjoint(): lax.all_to_all(terms, 'tile', split_axis=1, concat_axis=1, tiled=True)  25.1 us
    dot_general x3, matrix products, forward(): jnp.einsum('cnk,nrk->ncr', tiles, sensitivity, preferred_element_type=jnp...  18.1 us
    unnamed x15, local copies, waits for them, and re-layouts  15.1 us
  transfers between devices with their start and end apart: 3, of which 2 were waited for; matrix products, arithmetic and copies ran while one was open for 3% of the time, Pallas kernels for 3%

profile of v16, /device:TPU:1, one launch (start us, length us, event | category | flops | bytes accessed | tf_op | source)
XLA Modules:
  0.0 480.2 jit_solution(18422821171770620730)
XLA Ops:
  0.6 1.3 copy.25
  2.0 6.0 %all-to-all-start = ((s32[1,8,4]{2,0,1:T(1,128)}), s32[1,8,4]{2,0,1:T(1,128)S(1)}, u32[]{:S(2)}, u32[]{:S(2)}) async-start(s32[1,8,4]{2,0,1:T(1,128)} %copy.25), calls=%async_computation | async-start | bytes 8192 | tf_op jit(solution)/shard_map/all_to_all | solution.py:317
  7.9 1.2 multiply_reduce_fusion.4
  9.7 16.4 %shard_map.59 = f32[8,128]{1,0:T(8,128)} custom-call(f32[8,128]{1,0:T(8,128)} %scatter.16.x_ref), custom_call_target="tpu_custom_call" | custom-call | tf_op jit(solution)/shard_map/pallas_call | solution.py:88
  26.2 0.7 sqrt_bitcast_fusion.3
  26.9 0.8 copy.26
  27.7 1.1 fusion.13
  29.5 6.3 %convert_bitcast_fusion.1 = bf16[64,32,512]{2,0,1:T(8,128)(2,1)} fusion(bf16[32,256,512]{2,1,0:T(8,128)(2,1)} %param.15, bf16[32,64,256]{2,1,0:T(8,128)(2,1)S(1)} %gather_fusion), kind=kOutput, calls=%fused_computation.25 | convolution fusion | flops 537919488 | bytes 11534336 | tf_op jit(solution)/shard_map/cnr,nrk->cnk/dot_general | solution.py:345
  35.8 4.9 %all-to-all-start.1 = ((bf16[64,32,512]{2,0,1:T(8,128)(2,1)}), bf16[64,32,512]{2,0,1:T(8,128)(2,1)S(1)}, u32[]{:S(2)}, u32[]{:S(2)}) async-start(bf16[64,32,512]{2,0,1:T(8,128)(2,1)} %convert_bitcast_fusion.1), calls=%async_computation.1 | async-start | bytes 4194304 | tf_op jit(solution)/shard_map/all_to_all | solution.py:348
  41.2 0.7 reduce.13
  42.0 25.1 %all-to-all-done.1 = bf16[64,32,512]{2,0,1:T(8,128)(2,1)S(1)} async-done(((bf16[64,32,512]{2,0,1:T(8,128)(2,1)}), bf16[64,32,512]{2,0,1:T(8,128)(2,1)S(1)}, u32[]{:S(2)}, u32[]{:S(2)}) %all-to-all-start.1) | async-done | bytes 2097184 | tf_op jit(solution)/shard_map/all_to_all | solution.py:348
  67.1 1.7 fusion.8
  68.8 6.3 %copy.42 = f32[8,8,48,512]{3,1,2,0:T(8,128)} copy(f32[8,8,48,512]{3,2,1,0:T(8,128)S(1)} %bitcast.106) | data formatting | bytes 12582912
  75.1 80.7 %shard_map.60 = f32[64,24576]{1,0:T(8,128)} custom-call(f32[64,24576]{1,0:T(8,128)} %bitcast.107), custom_call_target="tpu_custom_call" | custom-call | tf_op jit(solution)/shard_map/pallas_call | solution.py:289
  155.7 3.3 multiply_reduce_fusion.1
  159.6 8.2 %shard_map.61 = f32[8,128]{1,0:T(8,128)} custom-call(f32[8,128]{1,0:T(8,128)} %scatter.19.x_ref), custom_call_target="tpu_custom_call" | custom-call | tf_op jit(solution)/shard_map/pallas_call | solution.py:88
  167.9 0.7 sqrt_bitcast_fusion.2
  168.6 3.2 fusion.30
  172.2 2.0 gather_fusion.1
  174.2 30.7 %all_to_all.30 = bf16[64,32,512]{2,0,1:T(8,128)(2,1)S(1)} all-to-all(bf16[64,32,512]{2,0,1:T(8,128)(2,1)} %bitcast.117), channel_id=1, replica_groups=mesh['ray'=16,'tile'=8] {'tile'}, dimensions={1} | all-to-all | bytes 4194304 | tf_op jit(solution)/shard_map/all_to_all | solution.py:330
  204.9 6.0 %fusion.34 = f32[32,64,256]{2,1,0:T(8,128)S(1)} fusion(bf16[64,32,512]{2,0,1:T(8,128)(2,1)S(1)} %all_to_all.30, bf16[32,256,512]{2,1,0:T(8,128)(2,1)} %param.15), kind=kOutput, calls=%fused_computation.64 | convolution fusion | flops 536870912 | bytes 12582912 | tf_op jit(solution)/shard_map/cnk,nrk->ncr/dot_general | solution.py:335
  211.0 2.0 fusion.6
  214.0 12.9 %shard_map.62 = f32[8,128]{1,0:T(8,128)} custom-call(f32[8,128]{1,0:T(8,128)} %scatter.20.x_ref), custom_call_target="tpu_custom_call" | custom-call | tf_op jit(solution)/shard_map/pallas_call | solution.py:88
  226.9 0.7 sqrt_bitcast_fusion.1
  228.4 5.0 %convert_bitcast_fusion = bf16[64,32,512]{2,0,1:T(8,128)(2,1)S(1)} fusion(bf16[32,256,512]{2,1,0:T(8,128)(2,1)} %param.15, bf16[32,64,256]{2,1,0:T(8,128)(2,1)S(1)} %gather_fusion.2), kind=kOutput, calls=%fused_computation.24 | convolution fusion | flops 537919488 | bytes 11534336 | tf_op jit(solution)/shard_map/cnr,nrk->cnk/dot_general | solution.py:345
  233.4 31.3 %all_to_all.31 = bf16[64,32,512]{2,0,1:T(8,128)(2,1)S(1)} all-to-all(bf16[64,32,512]{2,0,1:T(8,128)(2,1)S(1)} %convert_bitcast_fusion), channel_id=1, replica_groups=mesh['ray'=16,'tile'=8] {'tile'}, dimensions={1} | all-to-all | bytes 4194304 | tf_op jit(solution)/shard_map/all_to_all | solution.py:348
  264.6 1.7 fusion.4
  266.4 6.3 %copy.44 = f32[8,8,48,512]{3,1,2,0:T(8,128)} copy(f32[8,8,48,512]{3,2,1,0:T(8,128)S(1)} %bitcast.105) | data formatting | bytes 12582912
  272.6 77.4 %shard_map.63 = f32[64,24576]{1,0:T(8,128)} custom-call(f32[64,24576]{1,0:T(8,128)} %bitcast.108), custom_call_target="tpu_custom_call" | custom-call | tf_op jit(solution)/shard_map/pallas_call | solution.py:289
  350.0 5.8 %multiply_reduce_fusion = f32[64]{0:T(128)S(1)} fusion(f32[64,24576]{1,0:T(8,128)} %shard_map.63, f32[64]{0:T(128)S(1)} %sqrt_bitcast_fusion.1, f32[64,24576]{1,0:T(8,128)} %shard_map.60, f32[64]{0:T(128)S(1)} %sqrt_bitcast_fusion.2), kind=kLoop, calls=%fused_computation.6 | loop fusion | flops 7864256 | bytes 12583680 | tf_op jit(solution)/shard_map/reduce_sum | solution.py:356
  356.4 10.7 %shard_map.64 = f32[8,128]{1,0:T(8,128)} custom-call(f32[8,128]{1,0:T(8,128)} %scatter.21.x_ref), custom_call_target="tpu_custom_call" | custom-call | tf_op jit(solution)/shard_map/pallas_call | solution.py:88
  367.1 0.7 sqrt_bitcast_fusion
  367.8 5.2 %fusion.10 = bf16[64,24576]{1,0:T(8,128)(2,1)S(1)} fusion(f32[64]{0:T(128)S(1)} %sqrt_bitcast_fusion, f32[64,24576]{1,0:T(8,128)} %shard_map.63, f32[64]{0:T(128)S(1)} %sqrt_bitcast_fusion.1, f32[64,24576]{1,0:T(8,128)} %shard_map.60, f32[64]{0:T(128)S(1)} %sqrt_bitcast_fusion.2), kind=kLoop, calls=%fused_computation.26 | loop fusion | flops 7864320 | bytes 15729408 | tf_op jit(solution)/shard_map/convert_element_type | solution.py:374
  373.4 2.0 gather_fusion.3
  375.4 5.0 %all-to-all-start.4 = ((bf16[64,32,512]{2,0,1:T(8,128)(2,1)}), bf16[64,32,512]{2,0,1:T(8,128)(2,1)S(1)}, u32[]{:S(2)}, u32[]{:S(2)}) async-start(bf16[64,32,512]{2,0,1:T(8,128)(2,1)} %bitcast.115), calls=%async_computation.4 | async-start | bytes 4194304 | tf_op jit(solution)/shard_map/all_to_all | solution.py:330
  380.4 0.7 multiply_divide_fusion.2
  381.1 25.6 %all-to-all-done.4 = bf16[64,32,512]{2,0,1:T(8,128)(2,1)S(1)} async-done(((bf16[64,32,512]{2,0,1:T(8,128)(2,1)}), bf16[64,32,512]{2,0,1:T(8,128)(2,1)S(1)}, u32[]{:S(2)}, u32[]{:S(2)}) %all-to-all-start.4) | async-done | bytes 2097184 | tf_op jit(solution)/shard_map/all_to_all | solution.py:330
  406.7 6.0 %fusion.35 = f32[32,64,256]{2,1,0:T(8,128)S(1)} fusion(bf16[64,32,512]{2,0,1:T(8,128)(2,1)S(1)} %all-to-all-done.4, bf16[32,256,512]{2,1,0:T(8,128)(2,1)} %param.15), kind=kOutput, calls=%fused_computation.65 | convolution fusion | flops 536870912 | bytes 12582912 | tf_op jit(solution)/shard_map/cnk,nrk->ncr/dot_general | solution.py:335
  412.7 2.0 fusion.2
  415.8 12.6 %shard_map.65 = f32[8,128]{1,0:T(8,128)} custom-call(f32[8,128]{1,0:T(8,128)} %scatter.24.x_ref), custom_call_target="tpu_custom_call" | custom-call | tf_op jit(solution)/shard_map/pallas_call | solution.py:88
  428.4 0.7 multiply_divide_fusion.1
  429.1 0.7 multiply_divide_fusion
  429.8 7.4 %fusion.31 = (bf16[64,24576]{1,0:T(8,128)(2,1)S(1)}, f32[64,24576]{1,0:T(8,128)}) fusion(f32[64]{0:T(128)S(1)} %multiply_divide_fusion, f32[64]{0:T(128)S(1)} %sqrt_bitcast_fusion, f32[64,24576]{1,0:T(8,128)} %shard_map.63, f32[64]{0:T(128)S(1)} %sqrt_bitcast_fusion.1, f32[64]{0:T(128)S(1)} %get-tuple-element.67, f32[64,24576]{1,0:T(8,128)} %shard_map.60, ...), kind=kLoop, calls=%fused_computation.63 | loop fusion | flops 15728640 | bytes 22021632 | tf_op jit(solution)/shard_map/convert_element_type | solution.py:391
  437.6 2.0 gather_fusion.4
  439.6 31.5 %all_to_all.32 = bf16[64,32,512]{2,0,1:T(8,128)(2,1)S(1)} all-to-all(bf16[64,32,512]{2,0,1:T(8,128)(2,1)} %bitcast.116), channel_id=1, replica_groups=mesh['ray'=16,'tile'=8] {'tile'}, dimensions={1} | all-to-all | bytes 4194304 | tf_op jit(solution)/shard_map/all_to_all | solution.py:330
  471.1 6.0 %fusion.36 = f32[32,64,256]{2,1,0:T(8,128)S(1)} fusion(bf16[64,32,512]{2,0,1:T(8,128)(2,1)S(1)} %all_to_all.32, bf16[32,256,512]{2,1,0:T(8,128)(2,1)} %param.15), kind=kOutput, calls=%fused_computation.66 | convolution fusion | flops 536870912 | bytes 12582912 | tf_op jit(solution)/shard_map/cnk,nrk->ncr/dot_general | solution.py:335
  477.2 2.0 fusion
  479.3 0.9 sub.19
  (32 shorter events, 7.4 us)
Async XLA Ops:
  2.0 33.8 %all-to-all-start = ((s32[1,8,4]{2,0,1:T(1,128)}), s32[1,8,4]{2,0,1:T(1,128)S(1)}, u32[]{:S(2)}, u32[]{:S(2)}) async-start(s32[1,8,4]{2,0,1:T(1,128)} %copy.25), calls=%async_computation | async-start | bytes 8192 | tf_op jit(solution)/shard_map/all_to_all | solution.py:317
  35.8 31.3 %all-to-all-start.1 = ((bf16[64,32,512]{2,0,1:T(8,128)(2,1)}), bf16[64,32,512]{2,0,1:T(8,128)(2,1)S(1)}, u32[]{:S(2)}, u32[]{:S(2)}) async-start(bf16[64,32,512]{2,0,1:T(8,128)(2,1)} %convert_bitcast_fusion.1), calls=%async_computation.1 | async-start | bytes 4194304 | tf_op jit(solution)/shard_map/all_to_all | solution.py:348
  211.0 2.1 copy-start
  213.4 14.4 %copy-start.2 = (f32[64,2048]{1,0:T(8,128)}, f32[64,2048]{1,0:T(8,128)S(1)}, u32[]{:S(2)}) copy-start(f32[64,2048]{1,0:T(8,128)S(1)} %get-tuple-element.70) | copy-start | bytes 1572868
  375.4 31.3 %all-to-all-start.4 = ((bf16[64,32,512]{2,0,1:T(8,128)(2,1)}), bf16[64,32,512]{2,0,1:T(8,128)(2,1)S(1)}, u32[]{:S(2)}, u32[]{:S(2)}) async-start(bf16[64,32,512]{2,0,1:T(8,128)(2,1)} %bitcast.115), calls=%async_computation.4 | async-start | bytes 4194304 | tf_op jit(solution)/shard_map/all_to_all | solution.py:330
  412.7 2.1 copy-start.3
  477.2 2.1 copy-start.1

commit v17 on v16

--- a/solution.py
+++ b/solution.py
@@ -335,8 +335,15 @@
         partial_value = jnp.einsum(
             "cnk,nrk->ncr", tiles, sensitivity, preferred_element_type=jnp.float32
         )
-        summed = jnp.einsum(
-            "ncr,nb->cbr", partial_value, bundle_onehot, precision=lax.Precision.HIGHEST
+        hi_f = lax.reduce_precision(partial_value, exponent_bits=8, mantissa_bits=7)
+        rest = partial_value - hi_f
+        mid_f = lax.reduce_precision(rest, exponent_bits=8, mantissa_bits=7)
+        hi, mid = hi_f.astype(jnp.bfloat16), mid_f.astype(jnp.bfloat16)
+        lo = (rest - mid_f).astype(jnp.bfloat16)
+        onehot_bf = bundle_onehot.astype(jnp.bfloat16)
+        summed = sum(
+            jnp.einsum("ncr,nb->cbr", part, onehot_bf, preferred_element_type=jnp.float32)
+            for part in (hi, mid, lo)
         )
         return summed.reshape(columns, BUND_DEV * RB)
 

time: 481 us -> 482 us (level)
  no operation moved by 1% of the time
where the time goes in v17:
time: 482 us; the launch traced here: 481 us
  Pallas kernels  219 us (45%)
  blocking collectives  93.5 us (19%)
  waiting for transfers between devices  50.7 us (11%)
  matrix products  39 us (8%)
  other arithmetic  34.3 us (7%)
  local copies, waits for them, and re-layouts  27.4 us (6%)
  starting transfers between devices  15.8 us (3%)
    pallas_call x2, Pallas kernels, ray_allreduce(): pl.pallas_call(functools.partial(allreduce_kernel, axes), out_shape=jax.S...  158 us
    all_to_all x2, blocking collectives, fetch(): lax.all_to_all(outgoing, 'tile', split_axis=1, concat_axis=1, tiled=True)  62.2 us
    pallas_call x5, Pallas kernels, group_sum(): pl.pallas_call(functools.partial(reduce_kernel, plan), out_shape=jax.Shap...  60.9 us
    all_to_all x1, blocking collectives, adjoint(): lax.all_to_all(terms, 'tile', split_axis=1, concat_axis=1, tiled=True)  31.3 us
    all_to_all x1, waiting for transfers between devices, fetch(): lax.all_to_all(outgoing, 'tile', split_axis=1, concat_axis=1, tiled=True)  25.6 us
    all_to_all x1, waiting for transfers between devices, adjoint(): lax.all_to_all(terms, 'tile', split_axis=1, concat_axis=1, tiled=True)  25.1 us
    dot_general x3, matrix products, forward(): jnp.einsum('cnk,nrk->ncr', tiles, sensitivity, preferred_element_type=jnp...  18.2 us
    unnamed x15, local copies, waits for them, and re-layouts  15.1 us
  transfers between devices with their start and end apart: 3, of which 2 were waited for; matrix products, arithmetic and copies ran while one was open for 3% of the time, Pallas kernels for 3%

profile of v17, /device:TPU:1, one launch (start us, length us, event | category | flops | bytes accessed | tf_op | source)
XLA Modules:
  0.0 480.5 jit_solution(7489819663845737280)
XLA Ops:
  0.6 1.3 copy.49
  2.0 6.0 %all-to-all-start = ((s32[1,8,4]{2,0,1:T(1,128)}), s32[1,8,4]{2,0,1:T(1,128)S(1)}, u32[]{:S(2)}, u32[]{:S(2)}) async-start(s32[1,8,4]{2,0,1:T(1,128)} %copy.49), calls=%async_computation | async-start | bytes 8192 | tf_op jit(solution)/shard_map/all_to_all | solution.py:317
  7.9 1.2 multiply_reduce_fusion.4
  9.7 16.4 %shard_map.59 = f32[8,128]{1,0:T(8,128)} custom-call(f32[8,128]{1,0:T(8,128)} %scatter.16.x_ref), custom_call_target="tpu_custom_call" | custom-call | tf_op jit(solution)/shard_map/pallas_call | solution.py:88
  26.2 0.7 sqrt_bitcast_fusion.3
  26.9 0.8 copy.50
  27.7 1.1 fusion.22
  29.5 6.3 %convert_bitcast_fusion.1 = bf16[64,32,512]{2,0,1:T(8,128)(2,1)} fusion(bf16[32,256,512]{2,1,0:T(8,128)(2,1)} %param.15, bf16[32,64,256]{2,1,0:T(8,128)(2,1)S(1)} %gather_fusion), kind=kOutput, calls=%fused_computation.34 | convolution fusion | flops 537919488 | bytes 11534336 | tf_op jit(solution)/shard_map/cnr,nrk->cnk/dot_general | solution.py:352
  35.8 4.9 %all-to-all-start.1 = ((bf16[64,32,512]{2,0,1:T(8,128)(2,1)}), bf16[64,32,512]{2,0,1:T(8,128)(2,1)S(1)}, u32[]{:S(2)}, u32[]{:S(2)}) async-start(bf16[64,32,512]{2,0,1:T(8,128)(2,1)} %convert_bitcast_fusion.1), calls=%async_computation.1 | async-start | bytes 4194304 | tf_op jit(solution)/shard_map/all_to_all | solution.py:355
  42.0 25.1 %all-to-all-done.1 = bf16[64,32,512]{2,0,1:T(8,128)(2,1)S(1)} async-done(((bf16[64,32,512]{2,0,1:T(8,128)(2,1)}), bf16[64,32,512]{2,0,1:T(8,128)(2,1)S(1)}, u32[]{:S(2)}, u32[]{:S(2)}) %all-to-all-start.1) | async-done | bytes 2097184 | tf_op jit(solution)/shard_map/all_to_all | solution.py:355
  67.1 1.7 fusion.5
  68.8 6.3 %copy.72 = f32[8,8,48,512]{3,1,2,0:T(8,128)} copy(f32[8,8,48,512]{3,2,1,0:T(8,128)S(1)} %bitcast.112) | data formatting | bytes 12582912
  75.1 80.7 %shard_map.60 = f32[64,24576]{1,0:T(8,128)} custom-call(f32[64,24576]{1,0:T(8,128)} %bitcast.113), custom_call_target="tpu_custom_call" | custom-call | tf_op jit(solution)/shard_map/pallas_call | solution.py:289
  155.7 3.3 multiply_reduce_fusion.1
  159.6 8.2 %shard_map.61 = f32[8,128]{1,0:T(8,128)} custom-call(f32[8,128]{1,0:T(8,128)} %scatter.19.x_ref), custom_call_target="tpu_custom_call" | custom-call | tf_op jit(solution)/shard_map/pallas_call | solution.py:88
  167.9 0.7 sqrt_bitcast_fusion.2
  168.6 3.2 fusion.51
  172.2 2.0 gather_fusion.1
  174.2 30.7 %all_to_all.30 = bf16[64,32,512]{2,0,1:T(8,128)(2,1)S(1)} all-to-all(bf16[64,32,512]{2,0,1:T(8,128)(2,1)} %bitcast.123), channel_id=1, replica_groups=mesh['ray'=16,'tile'=8] {'tile'}, dimensions={1} | all-to-all | bytes 4194304 | tf_op jit(solution)/shard_map/all_to_all | solution.py:330
  204.9 6.1 %fusion = (bf16[32,64,256]{2,1,0:T(8,128)(2,1)S(1)}, bf16[32,64,256]{2,1,0:T(8,128)(2,1)S(1)}, bf16[32,64,256]{2,1,0:T(8,128)(2,1)S(1)}) fusion(bf16[64,32,512]{2,0,1:T(8,128)(2,1)S(1)} %all_to_all.30, bf16[32,256,512]{2,1,0:T(8,128)(2,1)} %param.15), kind=kOutput, calls=%fused_computation.26 | convolution fusion | flops 540540928 | bytes 13631488 | tf_op jit(solution)/shard_map/cnk,nrk->ncr/dot_general | solution.py:335
  211.7 0.7 convolution_add_fusion.5
  212.4 0.7 convolution_add_fusion.4
  214.1 12.9 %shard_map.62 = f32[8,128]{1,0:T(8,128)} custom-call(f32[8,128]{1,0:T(8,128)} %scatter.20.x_ref), custom_call_target="tpu_custom_call" | custom-call | tf_op jit(solution)/shard_map/pallas_call | solution.py:88
  227.0 0.7 sqrt_bitcast_fusion.1
  228.5 5.0 %convert_bitcast_fusion = bf16[64,32,512]{2,0,1:T(8,128)(2,1)S(1)} fusion(bf16[32,256,512]{2,1,0:T(8,128)(2,1)} %param.15, bf16[32,64,256]{2,1,0:T(8,128)(2,1)S(1)} %gather_fusion.2), kind=kOutput, calls=%fused_computation.33 | convolution fusion | flops 537919488 | bytes 11534336 | tf_op jit(solution)/shard_map/cnr,nrk->cnk/dot_general | solution.py:352
  233.5 31.3 %all_to_all.31 = bf16[64,32,512]{2,0,1:T(8,128)(2,1)S(1)} all-to-all(bf16[64,32,512]{2,0,1:T(8,128)(2,1)S(1)} %convert_bitcast_fusion), channel_id=1, replica_groups=mesh['ray'=16,'tile'=8] {'tile'}, dimensions={1} | all-to-all | bytes 4194304 | tf_op jit(solution)/shard_map/all_to_all | solution.py:355
  264.7 1.7 fusion.3
  266.5 6.3 %copy.74 = f32[8,8,48,512]{3,1,2,0:T(8,128)} copy(f32[8,8,48,512]{3,2,1,0:T(8,128)S(1)} %bitcast.111) | data formatting | bytes 12582912
  272.7 77.3 %shard_map.63 = f32[64,24576]{1,0:T(8,128)} custom-call(f32[64,24576]{1,0:T(8,128)} %bitcast.114), custom_call_target="tpu_custom_call" | custom-call | tf_op jit(solution)/shard_map/pallas_call | solution.py:289
  350.0 5.8 %multiply_reduce_fusion = f32[64]{0:T(128)S(1)} fusion(f32[64,24576]{1,0:T(8,128)} %shard_map.63, f32[64]{0:T(128)S(1)} %sqrt_bitcast_fusion.1, f32[64,24576]{1,0:T(8,128)} %shard_map.60, f32[64]{0:T(128)S(1)} %sqrt_bitcast_fusion.2), kind=kLoop, calls=%fused_computation.6 | loop fusion | flops 7864256 | bytes 12583680 | tf_op jit(solution)/shard_map/reduce_sum | solution.py:363
  356.5 10.7 %shard_map.64 = f32[8,128]{1,0:T(8,128)} custom-call(f32[8,128]{1,0:T(8,128)} %scatter.21.x_ref), custom_call_target="tpu_custom_call" | custom-call | tf_op jit(solution)/shard_map/pallas_call | solution.py:88
  367.2 0.7 sqrt_bitcast_fusion
  367.8 5.2 %fusion.7 = bf16[64,24576]{1,0:T(8,128)(2,1)S(1)} fusion(f32[64]{0:T(128)S(1)} %sqrt_bitcast_fusion, f32[64,24576]{1,0:T(8,128)} %shard_map.63, f32[64]{0:T(128)S(1)} %sqrt_bitcast_fusion.1, f32[64,24576]{1,0:T(8,128)} %shard_map.60, f32[64]{0:T(128)S(1)} %sqrt_bitcast_fusion.2), kind=kLoop, calls=%fused_computation.41 | loop fusion | flops 7864320 | bytes 15729408 | tf_op jit(solution)/shard_map/convert_element_type | solution.py:381
  373.5 2.0 gather_fusion.3
  375.5 5.0 %all-to-all-start.4 = ((bf16[64,32,512]{2,0,1:T(8,128)(2,1)}), bf16[64,32,512]{2,0,1:T(8,128)(2,1)S(1)}, u32[]{:S(2)}, u32[]{:S(2)}) async-start(bf16[64,32,512]{2,0,1:T(8,128)(2,1)} %bitcast.121), calls=%async_computation.4 | async-start | bytes 4194304 | tf_op jit(solution)/shard_map/all_to_all | solution.py:330
  380.5 0.7 multiply_divide_fusion.2
  381.2 25.6 %all-to-all-done.4 = bf16[64,32,512]{2,0,1:T(8,128)(2,1)S(1)} async-done(((bf16[64,32,512]{2,0,1:T(8,128)(2,1)}), bf16[64,32,512]{2,0,1:T(8,128)(2,1)S(1)}, u32[]{:S(2)}, u32[]{:S(2)}) %all-to-all-start.4) | async-done | bytes 2097184 | tf_op jit(solution)/shard_map/all_to_all | solution.py:330
  406.8 6.1 %fusion.1 = (bf16[32,64,256]{2,1,0:T(8,128)(2,1)S(1)}, bf16[32,64,256]{2,1,0:T(8,128)(2,1)S(1)}, bf16[32,64,256]{2,1,0:T(8,128)(2,1)S(1)}) fusion(bf16[64,32,512]{2,0,1:T(8,128)(2,1)S(1)} %all-to-all-done.4, bf16[32,256,512]{2,1,0:T(8,128)(2,1)} %param.15), kind=kOutput, calls=%fused_computation.27 | convolution fusion | flops 540540928 | bytes 13631488 | tf_op jit(solution)/shard_map/cnk,nrk->ncr/dot_general | solution.py:335
  414.3 0.7 convolution_add_fusion.2
  416.0 12.6 %shard_map.65 = f32[8,128]{1,0:T(8,128)} custom-call(f32[8,128]{1,0:T(8,128)} %scatter.24.x_ref), custom_call_target="tpu_custom_call" | custom-call | tf_op jit(solution)/shard_map/pallas_call | solution.py:88
  428.6 0.7 multiply_divide_fusion.1
  429.4 0.7 multiply_divide_fusion
  430.1 7.4 %fusion.52 = (bf16[64,24576]{1,0:T(8,128)(2,1)S(1)}, f32[64,24576]{1,0:T(8,128)}) fusion(f32[64]{0:T(128)S(1)} %multiply_divide_fusion, f32[64]{0:T(128)S(1)} %sqrt_bitcast_fusion, f32[64,24576]{1,0:T(8,128)} %shard_map.63, f32[64]{0:T(128)S(1)} %sqrt_bitcast_fusion.1, f32[64]{0:T(128)S(1)} %get-tuple-element.67, f32[64,24576]{1,0:T(8,128)} %shard_map.60, ...), kind=kLoop, calls=%fused_computation.97 | loop fusion | flops 15728640 | bytes 22021632 | tf_op jit(solution)/shard_map/convert_element_type | solution.py:398
  437.8 2.0 gather_fusion.4
  439.9 31.5 %all_to_all.32 = bf16[64,32,512]{2,0,1:T(8,128)(2,1)S(1)} all-to-all(bf16[64,32,512]{2,0,1:T(8,128)(2,1)} %bitcast.122), channel_id=1, replica_groups=mesh['ray'=16,'tile'=8] {'tile'}, dimensions={1} | all-to-all | bytes 4194304 | tf_op jit(solution)/shard_map/all_to_all | solution.py:330
  471.4 6.1 %fusion.2 = (bf16[32,64,256]{2,1,0:T(8,128)(2,1)S(1)}, bf16[32,64,256]{2,1,0:T(8,128)(2,1)S(1)}, bf16[32,64,256]{2,1,0:T(8,128)(2,1)S(1)}) fusion(bf16[64,32,512]{2,0,1:T(8,128)(2,1)S(1)} %all_to_all.32, bf16[32,256,512]{2,1,0:T(8,128)(2,1)} %param.15), kind=kOutput, calls=%fused_computation.28 | convolution fusion | flops 540540928 | bytes 13631488 | tf_op jit(solution)/shard_map/cnk,nrk->ncr/dot_general | solution.py:335
  478.1 0.7 convolution_add_fusion.1
  479.6 0.9 sub.43
  (38 shorter events, 11.4 us)
Async XLA Ops:
  2.0 33.8 %all-to-all-start = ((s32[1,8,4]{2,0,1:T(1,128)}), s32[1,8,4]{2,0,1:T(1,128)S(1)}, u32[]{:S(2)}, u32[]{:S(2)}) async-start(s32[1,8,4]{2,0,1:T(1,128)} %copy.49), calls=%async_computation | async-start | bytes 8192 | tf_op jit(solution)/shard_map/all_to_all | solution.py:317
  35.8 31.3 %all-to-all-start.1 = ((bf16[64,32,512]{2,0,1:T(8,128)(2,1)}), bf16[64,32,512]{2,0,1:T(8,128)(2,1)S(1)}, u32[]{:S(2)}, u32[]{:S(2)}) async-start(bf16[64,32,512]{2,0,1:T(8,128)(2,1)} %convert_bitcast_fusion.1), calls=%async_computation.1 | async-start | bytes 4194304 | tf_op jit(solution)/shard_map/all_to_all | solution.py:355
  211.0 2.2 copy-start
  213.5 14.4 %copy-start.2 = (f32[64,2048]{1,0:T(8,128)}, f32[64,2048]{1,0:T(8,128)S(1)}, u32[]{:S(2)}) copy-start(f32[64,2048]{1,0:T(8,128)S(1)} %get-tuple-element.70) | copy-start | bytes 1572868
  375.5 31.3 %all-to-all-start.4 = ((bf16[64,32,512]{2,0,1:T(8,128)(2,1)}), bf16[64,32,512]{2,0,1:T(8,128)(2,1)S(1)}, u32[]{:S(2)}, u32[]{:S(2)}) async-start(bf16[64,32,512]{2,0,1:T(8,128)(2,1)} %bitcast.121), calls=%async_computation.4 | async-start | bytes 4194304 | tf_op jit(solution)/shard_map/all_to_all | solution.py:330
  412.9 2.2 copy-start.3
  477.4 2.2 copy-start.1

commit v18 on v16

--- a/solution.py
+++ b/solution.py
@@ -304,7 +304,7 @@
             pltpu.SemaphoreType.DMA((4, 2, 2, steps)),
         ],
         compiler_params=pltpu.CompilerParams(
-            collective_id=2, has_side_effects=True, vmem_limit_bytes=60 * 1024 * 1024),
+            collective_id=2, has_side_effects=True, vmem_limit_bytes=32 * 1024 * 1024),
     )(owned)
 
 

time: 481 us -> 473 us (0.983)
  other arithmetic: 34.3 us -> 27 us
    reduce_sum x2, other arithmetic: 9.08 us -> 1.82 us  [cell_norm(): local = jnp.sum(field * field, axis=1)]
    unnamed x15 -> x23, local copies, waits for them, and re-layouts: 15.1 us -> 13.4 us
where the time goes in v18:
time: 473 us; the launch traced here: 472 us
  Pallas kernels  219 us (46%)
  blocking collectives  93.5 us (20%)
  waiting for transfers between devices  50.7 us (11%)
  matrix products  38.7 us (8%)
  other arithmetic  27 us (6%)
  local copies, waits for them, and re-layouts  25.6 us (5%)
  starting transfers between devices  15.8 us (3%)
    pallas_call x2, Pallas kernels, ray_allreduce(): pl.pallas_call(functools.partial(allreduce_kernel, axes), out_shape=jax.S...  157 us
    all_to_all x2, blocking collectives, fetch(): lax.all_to_all(outgoing, 'tile', split_axis=1, concat_axis=1, tiled=True)  62.2 us
    pallas_call x5, Pallas kernels, group_sum(): pl.pallas_call(functools.partial(reduce_kernel, plan), out_shape=jax.Shap...  61.7 us
    all_to_all x1, blocking collectives, adjoint(): lax.all_to_all(terms, 'tile', split_axis=1, concat_axis=1, tiled=True)  31.3 us
    all_to_all x1, waiting for transfers between devices, fetch(): lax.all_to_all(outgoing, 'tile', split_axis=1, concat_axis=1, tiled=True)  25.6 us
    all_to_all x1, waiting for transfers between devices, adjoint(): lax.all_to_all(terms, 'tile', split_axis=1, concat_axis=1, tiled=True)  25.1 us
    dot_general x3, matrix products, forward(): jnp.einsum('cnk,nrk->ncr', tiles, sensitivity, preferred_element_type=jnp...  18.1 us
    unnamed x23, local copies, waits for them, and re-layouts  13.4 us
  transfers between devices with their start and end apart: 3, of which 2 were waited for; matrix products, arithmetic and copies ran while one was open for 3% of the time, Pallas kernels for 3%

profile of v18, /device:TPU:1, one launch (start us, length us, event | category | flops | bytes accessed | tf_op | source)
XLA Modules:
  0.0 471.5 jit_solution(1172456581602300610)
XLA Ops:
  0.6 1.3 copy.25
  2.0 6.0 %all-to-all-start = ((s32[1,8,4]{2,0,1:T(1,128)}), s32[1,8,4]{2,0,1:T(1,128)S(1)}, u32[]{:S(2)}, u32[]{:S(2)}) async-start(s32[1,8,4]{2,0,1:T(1,128)} %copy.25), calls=%async_computation | async-start | bytes 8192 | tf_op jit(solution)/shard_map/all_to_all | solution.py:317
  7.9 1.2 multiply_reduce_fusion.4
  9.7 16.5 %shard_map.59 = f32[8,128]{1,0:T(8,128)} custom-call(f32[8,128]{1,0:T(8,128)} %scatter.16.x_ref), custom_call_target="tpu_custom_call" | custom-call | tf_op jit(solution)/shard_map/pallas_call | solution.py:88
  26.2 0.7 sqrt_bitcast_fusion.3
  26.9 0.8 copy.26
  27.7 1.1 fusion.13
  29.5 6.3 %convert_bitcast_fusion.1 = bf16[64,32,512]{2,0,1:T(8,128)(2,1)} fusion(bf16[32,256,512]{2,1,0:T(8,128)(2,1)} %param.15, bf16[32,64,256]{2,1,0:T(8,128)(2,1)S(1)} %gather_fusion), kind=kOutput, calls=%fused_computation.25 | convolution fusion | flops 537919488 | bytes 11534336 | tf_op jit(solution)/shard_map/cnr,nrk->cnk/dot_general | solution.py:345
  35.8 4.9 %all-to-all-start.1 = ((bf16[64,32,512]{2,0,1:T(8,128)(2,1)}), bf16[64,32,512]{2,0,1:T(8,128)(2,1)S(1)}, u32[]{:S(2)}, u32[]{:S(2)}) async-start(bf16[64,32,512]{2,0,1:T(8,128)(2,1)} %convert_bitcast_fusion.1), calls=%async_computation.1 | async-start | bytes 4194304 | tf_op jit(solution)/shard_map/all_to_all | solution.py:348
  42.0 25.1 %all-to-all-done.1 = bf16[64,32,512]{2,0,1:T(8,128)(2,1)S(1)} async-done(((bf16[64,32,512]{2,0,1:T(8,128)(2,1)}), bf16[64,32,512]{2,0,1:T(8,128)(2,1)S(1)}, u32[]{:S(2)}, u32[]{:S(2)}) %all-to-all-start.1) | async-done | bytes 2097184 | tf_op jit(solution)/shard_map/all_to_all | solution.py:348
  67.1 1.7 fusion.8
  68.8 3.7 copy.42
  72.5 80.6 %shard_map.60 = f32[64,24576]{1,0:T(8,128)S(1)} custom-call(f32[64,24576]{1,0:T(8,128)S(1)} %bitcast.107), custom_call_target="tpu_custom_call" | custom-call | tf_op jit(solution)/shard_map/pallas_call | solution.py:289
  153.6 2.2 copy-done
  156.4 8.1 %shard_map.61 = f32[8,128]{1,0:T(8,128)} custom-call(f32[8,128]{1,0:T(8,128)} %scatter.19.x_ref), custom_call_target="tpu_custom_call" | custom-call | tf_op jit(solution)/shard_map/pallas_call | solution.py:88
  164.5 0.7 sqrt_bitcast_fusion.2
  165.2 3.2 fusion.30
  168.8 2.0 gather_fusion.1
  170.9 30.6 %all_to_all.30 = bf16[64,32,512]{2,0,1:T(8,128)(2,1)S(1)} all-to-all(bf16[64,32,512]{2,0,1:T(8,128)(2,1)} %bitcast.119), channel_id=1, replica_groups=mesh['ray'=16,'tile'=8] {'tile'}, dimensions={1} | all-to-all | bytes 4194304 | tf_op jit(solution)/shard_map/all_to_all | solution.py:330
  201.5 6.0 %fusion.34 = f32[32,64,256]{2,1,0:T(8,128)S(1)} fusion(bf16[64,32,512]{2,0,1:T(8,128)(2,1)S(1)} %all_to_all.30, bf16[32,256,512]{2,1,0:T(8,128)(2,1)} %param.15), kind=kOutput, calls=%fused_computation.64 | convolution fusion | flops 536870912 | bytes 12582912 | tf_op jit(solution)/shard_map/cnk,nrk->ncr/dot_general | solution.py:335
  207.6 2.0 fusion.6
  210.6 13.4 %shard_map.62 = f32[8,128]{1,0:T(8,128)} custom-call(f32[8,128]{1,0:T(8,128)} %scatter.20.x_ref), custom_call_target="tpu_custom_call" | custom-call | tf_op jit(solution)/shard_map/pallas_call | solution.py:88
  224.0 0.7 sqrt_bitcast_fusion.1
  225.5 5.0 %convert_bitcast_fusion = bf16[64,32,512]{2,0,1:T(8,128)(2,1)S(1)} fusion(bf16[32,256,512]{2,1,0:T(8,128)(2,1)} %param.15, bf16[32,64,256]{2,1,0:T(8,128)(2,1)S(1)} %gather_fusion.2), kind=kOutput, calls=%fused_computation.24 | convolution fusion | flops 537919488 | bytes 11534336 | tf_op jit(solution)/shard_map/cnr,nrk->cnk/dot_general | solution.py:345
  230.4 31.3 %all_to_all.31 = bf16[64,32,512]{2,0,1:T(8,128)(2,1)S(1)} all-to-all(bf16[64,32,512]{2,0,1:T(8,128)(2,1)S(1)} %convert_bitcast_fusion), channel_id=1, replica_groups=mesh['ray'=16,'tile'=8] {'tile'}, dimensions={1} | all-to-all | bytes 4194304 | tf_op jit(solution)/shard_map/all_to_all | solution.py:348
  261.7 1.7 fusion.4
  263.4 3.6 copy.44
  267.0 76.8 %shard_map.63 = f32[64,24576]{1,0:T(8,128)S(1)} custom-call(f32[64,24576]{1,0:T(8,128)S(1)} %bitcast.108), custom_call_target="tpu_custom_call" | custom-call | tf_op jit(solution)/shard_map/pallas_call | solution.py:289
  343.9 1.3 multiply_reduce_fusion
  345.2 1.3 copy-done.1
  347.1 11.0 %shard_map.64 = f32[8,128]{1,0:T(8,128)} custom-call(f32[8,128]{1,0:T(8,128)} %scatter.21.x_ref), custom_call_target="tpu_custom_call" | custom-call | tf_op jit(solution)/shard_map/pallas_call | solution.py:88
  358.1 0.7 sqrt_bitcast_fusion
  358.8 5.2 %fusion.10 = bf16[64,24576]{1,0:T(8,128)(2,1)S(1)} fusion(f32[64]{0:T(128)S(1)} %sqrt_bitcast_fusion, f32[64,24576]{1,0:T(8,128)} %copy-done.1, f32[64]{0:T(128)S(1)} %sqrt_bitcast_fusion.1, f32[64,24576]{1,0:T(8,128)} %copy-done, f32[64]{0:T(128)S(1)} %sqrt_bitcast_fusion.2), kind=kLoop, calls=%fused_computation.26 | loop fusion | flops 7864320 | bytes 15729408 | tf_op jit(solution)/shard_map/convert_element_type | solution.py:374
  364.4 2.0 gather_fusion.3
  366.5 5.0 %all-to-all-start.4 = ((bf16[64,32,512]{2,0,1:T(8,128)(2,1)}), bf16[64,32,512]{2,0,1:T(8,128)(2,1)S(1)}, u32[]{:S(2)}, u32[]{:S(2)}) async-start(bf16[64,32,512]{2,0,1:T(8,128)(2,1)} %bitcast.117), calls=%async_computation.4 | async-start | bytes 4194304 | tf_op jit(solution)/shard_map/all_to_all | solution.py:330
  371.4 0.7 multiply_divide_fusion.2
  372.2 25.6 %all-to-all-done.4 = bf16[64,32,512]{2,0,1:T(8,128)(2,1)S(1)} async-done(((bf16[64,32,512]{2,0,1:T(8,128)(2,1)}), bf16[64,32,512]{2,0,1:T(8,128)(2,1)S(1)}, u32[]{:S(2)}, u32[]{:S(2)}) %all-to-all-start.4) | async-done | bytes 2097184 | tf_op jit(solution)/shard_map/all_to_all | solution.py:330
  397.8 6.0 %fusion.35 = f32[32,64,256]{2,1,0:T(8,128)S(1)} fusion(bf16[64,32,512]{2,0,1:T(8,128)(2,1)S(1)} %all-to-all-done.4, bf16[32,256,512]{2,1,0:T(8,128)(2,1)} %param.15), kind=kOutput, calls=%fused_computation.65 | convolution fusion | flops 536870912 | bytes 12582912 | tf_op jit(solution)/shard_map/cnk,nrk->ncr/dot_general | solution.py:335
  403.8 2.0 fusion.2
  406.8 12.8 %shard_map.65 = f32[8,128]{1,0:T(8,128)} custom-call(f32[8,128]{1,0:T(8,128)} %scatter.24.x_ref), custom_call_target="tpu_custom_call" | custom-call | tf_op jit(solution)/shard_map/pallas_call | solution.py:88
  419.6 0.7 multiply_divide_fusion.1
  420.4 0.7 multiply_divide_fusion
  421.1 7.4 %fusion.31 = (bf16[64,24576]{1,0:T(8,128)(2,1)S(1)}, f32[64,24576]{1,0:T(8,128)}) fusion(f32[64]{0:T(128)S(1)} %multiply_divide_fusion, f32[64]{0:T(128)S(1)} %sqrt_bitcast_fusion, f32[64,24576]{1,0:T(8,128)} %copy-done.1, f32[64]{0:T(128)S(1)} %sqrt_bitcast_fusion.1, f32[64]{0:T(128)S(1)} %get-tuple-element.67, f32[64,24576]{1,0:T(8,128)} %copy-done, ...), kind=kLoop, calls=%fused_computation.63 | loop fusion | flops 15728640 | bytes 22021632 | tf_op jit(solution)/shard_map/convert_element_type | solution.py:391
  428.8 2.0 gather_fusion.4
  430.9 31.6 %all_to_all.32 = bf16[64,32,512]{2,0,1:T(8,128)(2,1)S(1)} all-to-all(bf16[64,32,512]{2,0,1:T(8,128)(2,1)} %bitcast.118), channel_id=1, replica_groups=mesh['ray'=16,'tile'=8] {'tile'}, dimensions={1} | all-to-all | bytes 4194304 | tf_op jit(solution)/shard_map/all_to_all | solution.py:330
  462.4 6.0 %fusion.36 = f32[32,64,256]{2,1,0:T(8,128)S(1)} fusion(bf16[64,32,512]{2,0,1:T(8,128)(2,1)S(1)} %all_to_all.32, bf16[32,256,512]{2,1,0:T(8,128)(2,1)} %param.15), kind=kOutput, calls=%fused_computation.66 | convolution fusion | flops 536870912 | bytes 12582912 | tf_op jit(solution)/shard_map/cnk,nrk->ncr/dot_general | solution.py:335
  468.5 2.0 fusion
  470.6 0.9 sub.19
  (41 shorter events, 8.5 us)
Async XLA Ops:
  2.0 33.8 %all-to-all-start = ((s32[1,8,4]{2,0,1:T(1,128)}), s32[1,8,4]{2,0,1:T(1,128)S(1)}, u32[]{:S(2)}, u32[]{:S(2)}) async-start(s32[1,8,4]{2,0,1:T(1,128)} %copy.25), calls=%async_computation | async-start | bytes 8192 | tf_op jit(solution)/shard_map/all_to_all | solution.py:317
  35.8 31.3 %all-to-all-start.1 = ((bf16[64,32,512]{2,0,1:T(8,128)(2,1)}), bf16[64,32,512]{2,0,1:T(8,128)(2,1)S(1)}, u32[]{:S(2)}, u32[]{:S(2)}) async-start(bf16[64,32,512]{2,0,1:T(8,128)(2,1)} %convert_bitcast_fusion.1), calls=%async_computation.1 | async-start | bytes 4194304 | tf_op jit(solution)/shard_map/all_to_all | solution.py:348
  153.1 2.7 copy-start
  207.6 2.1 copy-start.2
  210.0 14.9 %copy-start.4 = (f32[64,2048]{1,0:T(8,128)}, f32[64,2048]{1,0:T(8,128)S(1)}, u32[]{:S(2)}) copy-start(f32[64,2048]{1,0:T(8,128)S(1)} %get-tuple-element.70) | copy-start | bytes 1572868
  263.4 80.4 %slice-start = ((s8[6291456]{0:T(1024)(128)(4,1)}), s8[4194304]{0:T(1024)(128)(4,1)S(1)}, s32[]{:S(2)}) async-start(s8[6291456]{0:T(1024)(128)(4,1)} %bitcast.105), calls=%async_computation.6 | async-start | bytes 8388608
  267.0 76.8 %slice-start.1 = ((s8[6291456]{0:T(1024)(128)(4,1)}), s8[2097152]{0:T(1024)(128)(4,1)S(1)}, s32[]{:S(2)}) async-start(s8[6291456]{0:T(1024)(128)(4,1)} %bitcast.105), calls=%async_computation.7 | async-start | bytes 4194304
  343.9 2.6 copy-start.1
  366.5 31.3 %all-to-all-start.4 = ((bf16[64,32,512]{2,0,1:T(8,128)(2,1)}), bf16[64,32,512]{2,0,1:T(8,128)(2,1)S(1)}, u32[]{:S(2)}, u32[]{:S(2)}) async-start(bf16[64,32,512]{2,0,1:T(8,128)(2,1)} %bitcast.117), calls=%async_computation.4 | async-start | bytes 4194304 | tf_op jit(solution)/shard_map/all_to_all | solution.py:330
  403.8 2.1 copy-start.5
  468.5 2.1 copy-start.3

commit v19 on v18

--- a/solution.py
+++ b/solution.py
@@ -95,7 +95,7 @@
             pltpu.SemaphoreType.DMA((len(plan), depth)),
             pltpu.SemaphoreType.DMA((len(plan), depth)),
         ],
-        compiler_params=pltpu.CompilerParams(collective_id=collective_id, has_side_effects=True),
+        compiler_params=pltpu.CompilerParams(collective_id=collective_id, has_side_effects=True, vmem_limit_bytes=1024 * 1024),
     )(block)
     return out[0, :width]
 

time: 473 us -> 450 us (0.951)
  other arithmetic: 27 us -> 15.4 us
  local copies, waits for them, and re-layouts: 25.6 us -> 19.1 us
  Pallas kernels: 219 us -> 214 us
    convert_element_type x2, other arithmetic: 8.44 us -> 1.55 us  [per_device(): rounded = model_dir.astype(jnp.bfloat16)]
    pallas_call x5, Pallas kernels: 61.7 us -> 57 us  [group_sum(): pl.pallas_call(functools.partial(reduce_kernel, plan), out_shape=jax.Shap...]
where the time goes in v19:
time: 450 us; the launch traced here: 449 us
  Pallas kernels  214 us (48%)
  blocking collectives  93.5 us (21%)
  waiting for transfers between devices  51.4 us (11%)
  matrix products  38.7 us (9%)
  local copies, waits for them, and re-layouts  19.1 us (4%)
  starting transfers between devices  15.8 us (4%)
  other arithmetic  15.4 us (3%)
    pallas_call x2, Pallas kernels, ray_allreduce(): pl.pallas_call(functools.partial(allreduce_kernel, axes), out_shape=jax.S...  157 us
    all_to_all x2, blocking collectives, fetch(): lax.all_to_all(outgoing, 'tile', split_axis=1, concat_axis=1, tiled=True)  62.2 us
    pallas_call x5, Pallas kernels, group_sum(): pl.pallas_call(functools.partial(reduce_kernel, plan), out_shape=jax.Shap...  57 us
    all_to_all x1, blocking collectives, adjoint(): lax.all_to_all(terms, 'tile', split_axis=1, concat_axis=1, tiled=True)  31.3 us
    all_to_all x1, waiting for transfers between devices, fetch(): lax.all_to_all(outgoing, 'tile', split_axis=1, concat_axis=1, tiled=True)  26.3 us
    all_to_all x1, waiting for transfers between devices, adjoint(): lax.all_to_all(terms, 'tile', split_axis=1, concat_axis=1, tiled=True)  25.1 us
    dot_general x3, matrix products, forward(): jnp.einsum('cnk,nrk->ncr', tiles, sensitivity, preferred_element_type=jnp...  18.1 us
    dot_general x2, matrix products, adjoint(): jnp.einsum('cnr,nrk->cnk', picked, sensitivity, preferred_element_type=jn...  11.2 us
  transfers between devices with their start and end apart: 3, of which 2 were waited for; matrix products, arithmetic and copies ran while one was open for 3% of the time, Pallas kernels for 3%

profile of v19, /device:TPU:1, one launch (start us, length us, event | category | flops | bytes accessed | tf_op | source)
XLA Modules:
  0.0 449.2 jit_solution(1708826795219645248)
XLA Ops:
  0.6 1.3 copy.25
  2.0 6.0 %all-to-all-start = ((s32[1,8,4]{2,0,1:T(1,128)}), s32[1,8,4]{2,0,1:T(1,128)S(1)}, u32[]{:S(2)}, u32[]{:S(2)}) async-start(s32[1,8,4]{2,0,1:T(1,128)} %copy.25), calls=%async_computation | async-start | bytes 8192 | tf_op jit(solution)/shard_map/all_to_all | solution.py:317
  7.9 1.2 multiply_reduce_fusion.4
  9.1 15.6 %shard_map.59 = f32[8,128]{1,0:T(8,128)S(1)} custom-call(f32[8,128]{1,0:T(8,128)S(1)} %scatter.16.x_ref), custom_call_target="tpu_custom_call" | custom-call | tf_op jit(solution)/shard_map/pallas_call | solution.py:88
  24.8 0.8 copy.26
  25.7 1.1 fusion.13
  26.8 0.6 gather_fusion
  27.5 6.3 %convert_bitcast_fusion.1 = bf16[64,32,512]{2,0,1:T(8,128)(2,1)} fusion(bf16[32,256,512]{2,1,0:T(8,128)(2,1)} %param.15, bf16[32,64,256]{2,1,0:T(8,128)(2,1)S(1)} %gather_fusion), kind=kOutput, calls=%fused_computation.25 | convolution fusion | flops 537919488 | bytes 11534336 | tf_op jit(solution)/shard_map/cnr,nrk->cnk/dot_general | solution.py:345
  33.7 4.8 %all-to-all-start.1 = ((bf16[64,32,512]{2,0,1:T(8,128)(2,1)}), bf16[64,32,512]{2,0,1:T(8,128)(2,1)S(1)}, u32[]{:S(2)}, u32[]{:S(2)}) async-start(bf16[64,32,512]{2,0,1:T(8,128)(2,1)} %convert_bitcast_fusion.1), calls=%async_computation.1 | async-start | bytes 4194304 | tf_op jit(solution)/shard_map/all_to_all | solution.py:348
  38.6 0.5 broadcast.186
  39.1 0.7 reduce.13
  39.8 25.1 %all-to-all-done.1 = bf16[64,32,512]{2,0,1:T(8,128)(2,1)S(1)} async-done(((bf16[64,32,512]{2,0,1:T(8,128)(2,1)}), bf16[64,32,512]{2,0,1:T(8,128)(2,1)S(1)}, u32[]{:S(2)}, u32[]{:S(2)}) %all-to-all-start.1) | async-done | bytes 2097184 | tf_op jit(solution)/shard_map/all_to_all | solution.py:348
  64.9 1.7 fusion.8
  66.7 3.7 copy.42
  70.3 80.9 %shard_map.60 = f32[64,24576]{1,0:T(8,128)S(1)} custom-call(f32[64,24576]{1,0:T(8,128)S(1)} %bitcast.107), custom_call_target="tpu_custom_call" | custom-call | tf_op jit(solution)/shard_map/pallas_call | solution.py:289
  151.2 0.5 multiply_reduce_fusion.1
  151.7 6.8 %shard_map.61 = f32[8,128]{1,0:T(8,128)S(1)} custom-call(f32[8,128]{1,0:T(8,128)S(1)} %scatter.19.x_ref), custom_call_target="tpu_custom_call" | custom-call | tf_op jit(solution)/shard_map/pallas_call | solution.py:88
  158.5 0.4 fusion.30
  159.0 0.4 copy.64
  159.4 2.0 gather_fusion.1
  161.4 30.7 %all_to_all.30 = bf16[64,32,512]{2,0,1:T(8,128)(2,1)S(1)} all-to-all(bf16[64,32,512]{2,0,1:T(8,128)(2,1)} %bitcast.119), channel_id=1, replica_groups=mesh['ray'=16,'tile'=8] {'tile'}, dimensions={1} | all-to-all | bytes 4194304 | tf_op jit(solution)/shard_map/all_to_all | solution.py:330
  192.1 6.0 %fusion.34 = f32[32,64,256]{2,1,0:T(8,128)S(1)} fusion(bf16[64,32,512]{2,0,1:T(8,128)(2,1)S(1)} %all_to_all.30, bf16[32,256,512]{2,1,0:T(8,128)(2,1)} %param.15), kind=kOutput, calls=%fused_computation.64 | convolution fusion | flops 536870912 | bytes 12582912 | tf_op jit(solution)/shard_map/cnk,nrk->ncr/dot_general | solution.py:335
  198.1 2.0 fusion.6
  200.3 0.3 multiply_reduce_fusion.3
  200.6 12.5 %shard_map.62 = f32[8,128]{1,0:T(8,128)S(1)} custom-call(f32[8,128]{1,0:T(8,128)S(1)} %scatter.20.x_ref), custom_call_target="tpu_custom_call" | custom-call | tf_op jit(solution)/shard_map/pallas_call | solution.py:88
  213.3 0.6 gather_fusion.2
  213.9 5.0 %convert_bitcast_fusion = bf16[64,32,512]{2,0,1:T(8,128)(2,1)S(1)} fusion(bf16[32,256,512]{2,1,0:T(8,128)(2,1)} %param.15, bf16[32,64,256]{2,1,0:T(8,128)(2,1)S(1)} %gather_fusion.2), kind=kOutput, calls=%fused_computation.24 | convolution fusion | flops 537919488 | bytes 11534336 | tf_op jit(solution)/shard_map/cnr,nrk->cnk/dot_general | solution.py:345
  218.8 31.3 %all_to_all.31 = bf16[64,32,512]{2,0,1:T(8,128)(2,1)S(1)} all-to-all(bf16[64,32,512]{2,0,1:T(8,128)(2,1)S(1)} %convert_bitcast_fusion), channel_id=1, replica_groups=mesh['ray'=16,'tile'=8] {'tile'}, dimensions={1} | all-to-all | bytes 4194304 | tf_op jit(solution)/shard_map/all_to_all | solution.py:348
  250.1 1.7 fusion.4
  251.8 3.6 copy.44
  255.4 76.5 %shard_map.63 = f32[64,24576]{1,0:T(8,128)S(1)} custom-call(f32[64,24576]{1,0:T(8,128)S(1)} %bitcast.108), custom_call_target="tpu_custom_call" | custom-call | tf_op jit(solution)/shard_map/pallas_call | solution.py:289
  332.0 1.3 multiply_reduce_fusion
  333.3 10.1 %shard_map.64 = f32[8,128]{1,0:T(8,128)S(1)} custom-call(f32[8,128]{1,0:T(8,128)S(1)} %scatter.21.x_ref), custom_call_target="tpu_custom_call" | custom-call | tf_op jit(solution)/shard_map/pallas_call | solution.py:88
  343.4 1.1 fusion.10
  344.6 0.4 copy.63
  344.9 2.0 gather_fusion.3
  347.0 5.0 %all-to-all-start.4 = ((bf16[64,32,512]{2,0,1:T(8,128)(2,1)}), bf16[64,32,512]{2,0,1:T(8,128)(2,1)S(1)}, u32[]{:S(2)}, u32[]{:S(2)}) async-start(bf16[64,32,512]{2,0,1:T(8,128)(2,1)} %bitcast.117), calls=%async_computation.4 | async-start | bytes 4194304 | tf_op jit(solution)/shard_map/all_to_all | solution.py:330
  352.0 26.3 %all-to-all-done.4 = bf16[64,32,512]{2,0,1:T(8,128)(2,1)S(1)} async-done(((bf16[64,32,512]{2,0,1:T(8,128)(2,1)}), bf16[64,32,512]{2,0,1:T(8,128)(2,1)S(1)}, u32[]{:S(2)}, u32[]{:S(2)}) %all-to-all-start.4) | async-done | bytes 2097184 | tf_op jit(solution)/shard_map/all_to_all | solution.py:330
  378.3 6.0 %fusion.35 = f32[32,64,256]{2,1,0:T(8,128)S(1)} fusion(bf16[64,32,512]{2,0,1:T(8,128)(2,1)S(1)} %all-to-all-done.4, bf16[32,256,512]{2,1,0:T(8,128)(2,1)} %param.15), kind=kOutput, calls=%fused_computation.65 | convolution fusion | flops 536870912 | bytes 12582912 | tf_op jit(solution)/shard_map/cnk,nrk->ncr/dot_general | solution.py:335
  384.3 2.0 fusion.2
  386.7 12.0 %shard_map.65 = f32[8,128]{1,0:T(8,128)S(1)} custom-call(f32[8,128]{1,0:T(8,128)S(1)} %scatter.24.x_ref), custom_call_target="tpu_custom_call" | custom-call | tf_op jit(solution)/shard_map/pallas_call | solution.py:88
  398.8 7.4 %fusion.31 = (bf16[64,24576]{1,0:T(8,128)(2,1)S(1)}, f32[64,24576]{1,0:T(8,128)}) fusion(f32[64]{0:T(128)S(1)} %multiply_divide_fusion, f32[64]{0:T(128)S(1)} %sqrt_bitcast_fusion, f32[64,24576]{1,0:T(8,128)} %copy-done.1, f32[64]{0:T(128)S(1)} %sqrt_bitcast_fusion.1, f32[64]{0:T(128)S(1)} %get-tuple-element.67, f32[64,24576]{1,0:T(8,128)} %copy-done, ...), kind=kLoop, calls=%fused_computation.63 | loop fusion | flops 15728640 | bytes 22021632 | tf_op jit(solution)/shard_map/convert_element_type | solution.py:391
  406.2 0.4 copy.62
  406.6 2.0 gather_fusion.4
  408.6 31.6 %all_to_all.32 = bf16[64,32,512]{2,0,1:T(8,128)(2,1)S(1)} all-to-all(bf16[64,32,512]{2,0,1:T(8,128)(2,1)} %bitcast.118), channel_id=1, replica_groups=mesh['ray'=16,'tile'=8] {'tile'}, dimensions={1} | all-to-all | bytes 4194304 | tf_op jit(solution)/shard_map/all_to_all | solution.py:330
  440.2 6.0 %fusion.36 = f32[32,64,256]{2,1,0:T(8,128)S(1)} fusion(bf16[64,32,512]{2,0,1:T(8,128)(2,1)S(1)} %all_to_all.32, bf16[32,256,512]{2,1,0:T(8,128)(2,1)} %param.15), kind=kOutput, calls=%fused_computation.66 | convolution fusion | flops 536870912 | bytes 12582912 | tf_op jit(solution)/shard_map/cnk,nrk->ncr/dot_general | solution.py:335
  446.2 2.0 fusion
  448.4 0.9 sub.19
  (41 shorter events, 1.2 us)
Async XLA Ops:
  2.0 31.8 %all-to-all-start = ((s32[1,8,4]{2,0,1:T(1,128)}), s32[1,8,4]{2,0,1:T(1,128)S(1)}, u32[]{:S(2)}, u32[]{:S(2)}) async-start(s32[1,8,4]{2,0,1:T(1,128)} %copy.25), calls=%async_computation | async-start | bytes 8192 | tf_op jit(solution)/shard_map/all_to_all | solution.py:317
  33.7 31.2 %all-to-all-start.1 = ((bf16[64,32,512]{2,0,1:T(8,128)(2,1)}), bf16[64,32,512]{2,0,1:T(8,128)(2,1)S(1)}, u32[]{:S(2)}, u32[]{:S(2)}) async-start(bf16[64,32,512]{2,0,1:T(8,128)(2,1)} %convert_bitcast_fusion.1), calls=%async_computation.1 | async-start | bytes 4194304 | tf_op jit(solution)/shard_map/all_to_all | solution.py:348
  151.2 7.3 %copy-start = (f32[64,24576]{1,0:T(8,128)}, f32[64,24576]{1,0:T(8,128)S(1)}, u32[]{:S(2)}) copy-start(f32[64,24576]{1,0:T(8,128)S(1)} %shard_map.60) | copy-start | bytes 18874372
  198.1 2.1 copy-start.2
  200.6 12.7 %copy-start.4 = (f32[64,2048]{1,0:T(8,128)}, f32[64,2048]{1,0:T(8,128)S(1)}, u32[]{:S(2)}) copy-start(f32[64,2048]{1,0:T(8,128)S(1)} %get-tuple-element.70) | copy-start | bytes 1572868
  251.8 80.1 %slice-start = ((s8[6291456]{0:T(1024)(128)(4,1)}), s8[4194304]{0:T(1024)(128)(4,1)S(1)}, s32[]{:S(2)}) async-start(s8[6291456]{0:T(1024)(128)(4,1)} %bitcast.105), calls=%async_computation.6 | async-start | bytes 8388608
  255.4 76.6 %slice-start.1 = ((s8[6291456]{0:T(1024)(128)(4,1)}), s8[2097152]{0:T(1024)(128)(4,1)S(1)}, s32[]{:S(2)}) async-start(s8[6291456]{0:T(1024)(128)(4,1)} %bitcast.105), calls=%async_computation.7 | async-start | bytes 4194304
  332.0 11.4 %copy-start.1 = (f32[64,24576]{1,0:T(8,128)}, f32[64,24576]{1,0:T(8,128)S(1)}, u32[]{:S(2)}) copy-start(f32[64,24576]{1,0:T(8,128)S(1)} %shard_map.63) | copy-start | bytes 18874372
  347.0 31.4 %all-to-all-start.4 = ((bf16[64,32,512]{2,0,1:T(8,128)(2,1)}), bf16[64,32,512]{2,0,1:T(8,128)(2,1)S(1)}, u32[]{:S(2)}, u32[]{:S(2)}) async-start(bf16[64,32,512]{2,0,1:T(8,128)(2,1)} %bitcast.117), calls=%async_computation.4 | async-start | bytes 4194304 | tf_op jit(solution)/shard_map/all_to_all | solution.py:330
  384.3 2.1 copy-start.5
  446.2 2.1 copy-start.3
